TPU v7x, 32 devices: a whole 2x2x4 slice. The times are simulated.
32 devices in a mesh: row: 8 (over z, core), col: 4 (over y, x).
Axes of the slice: x: 2, y: 2, z: 4, core: 2. Of those that a mesh axis runs over, the one named last changes fastest.
Arguments:
- tiles: bfloat16 [4096, 128, 128], P(('row', 'col')), may hold values from -48 to 48
- tile_rows: int32 [4096], P(('row', 'col')), may hold values from 0 to 1023, as said below
- tile_cols: int32 [4096], P(('row', 'col')), may hold values from 0 to 1023, as said below
- tile_count: int32 [32], P(('row', 'col')), may hold values from 32 to 128, as said below
- degree: int32 [1024, 128], P(('row', 'col')), may hold values from 32 to 96
- labels: int32 [1024, 128], P(('row', 'col')), may hold values from 0 to 63
Outputs:
- scores: float32 [1024, 16, 128], P(('row', 'col'))
Inputs may be any that keep to these rules, and one draw needn't show every extreme that they name: tile_rows of the slots of device (r, c) lie in node-row blocks r * 128 to (r + 1) * 128 - 1. tile_cols of the slots of device (r, c) lie in node blocks (s * 4 + c) * 32 + o for some s below 8 and o below 32. `tile_count`: some device has all its slots live.
All inputs are finite; a program needn't handle non-finite values.
Results may differ from a plain program's by a relative error of at most 0.0039.
Values may be sent and summed in bfloat16 or wider, within the bound.
No kernel may reach another device: no remote copies, remote signals or barrier semaphores. Data moves between devices by JAX's collectives and lax.ppermute only.
A program may use at most 64 MiB of HBM per device.

v0:
```python
import jax
import jax.numpy as jnp
from jax import lax
from jax.sharding import PartitionSpec as P

QC = 16
ITERS = 2


def local(tiles, tile_rows, tile_cols, tile_count, degree, labels):
    ncol = lax.axis_size("col")
    row_pos = lax.axis_index("row")
    blk_dev = labels.shape[0]
    rblk = blk_dev * ncol
    scale = 1.0 / jnp.sqrt(degree.astype(jnp.float32))
    qidx = jnp.arange(QC, dtype=jnp.int32)
    prior = (labels[:, None, :] == qidx[None, :, None]).astype(jnp.float32)
    local_rows = tile_rows - row_pos * rblk
    owner = tile_cols // blk_dev
    local_cols = owner // ncol * blk_dev + tile_cols % blk_dev
    live = (jnp.arange(tiles.shape[0], dtype=jnp.int32) < tile_count[0]).astype(jnp.float32)
    field = prior
    for step in range(ITERS):
        if step == 0:
            own = (field * scale[:, None, :]).astype(jnp.bfloat16)
            gathered = lax.all_gather(own, "row", axis=0, tiled=True)
        else:
            own = (field * scale[:, None, :]).astype(jnp.bfloat16)
            gathered = lax.all_gather(own, "row", axis=0, tiled=True)
        picked = gathered[local_cols]
        terms = jnp.einsum("tqj,tij->tqi", picked, tiles, preferred_element_type=jnp.float32)
        terms = terms * live[:, None, None]
        partial_rows = jax.ops.segment_sum(terms, local_rows, num_segments=rblk)
        summed = lax.psum_scatter(partial_rows, "col", scatter_dimension=0, tiled=True)
        field = 0.8 * scale[:, None, :] * summed + 0.2 * prior
    return field


def solution(mesh):
    return jax.shard_map(
        local,
        mesh=mesh,
        in_specs=(
            P(("row", "col"), None, None),
            P(("row", "col")),
            P(("row", "col")),
            P(("row", "col")),
            P(("row", "col"), None),
            P(("row", "col"), None),
        ),
        out_specs=P(("row", "col"), None, None),
        check_vma=False,
    )
```

profile of v0, /device:TPU:0, one launch (start us, length us, event | category | flops | bytes accessed | tf_op | source)
XLA Modules:
  0.0 146.3 jit_solution(1190749417528610300)
XLA Ops:
  6.5 0.0 all-gather.3.cloned.1.call-start
  6.5 0.7 broadcast_multiply_fusion
  7.3 1.4 select_convert_fusion
  8.7 0.0 all-gather.3.cloned.1.call-update
  8.7 0.0 reduce-scatter.3.cloned.1.call-start
  9.4 0.7 compare_select_fusion
  10.1 0.7 broadcast_subtract_fusion
  10.8 23.0 %all-gather.3.cloned.1.call-done = bf16[256,16,128]{2,1,0:T(8,128)(2,1)} async-done(((bf16[32,16,128]{2,1,0:T(8,128)(2,1)}), bf16[256,16,128]{2,1,0:T(8,128)(2,1)}) %all-gather.3.cloned.1.call-update) | async-done | bytes 1048592 | tf_op jit(solution)/shard_map/all_gather | solution.py:26
  33.8 1.9 %gather_fusion = bf16[128,16,128]{2,1,0:T(8,128)(2,1)S(1)} fusion(bf16[256,16,128]{2,1,0:T(8,128)(2,1)} %all-gather.3.cloned.1.call-done, s32[1024]{0:T(1024)S(1)} %pad_clamp_fusion), kind=kCustom, calls=%fused_computation | custom fusion | bytes 1049088 | tf_op jit(solution)/shard_map/gather | solution.py:30
  35.7 0.0 copy-start.2
  35.7 4.5 %convolution_multiply_fusion.1 = f32[128,16,128]{2,1,0:T(8,128)S(1)} fusion(bf16[128,16,128]{2,1,0:T(8,128)(2,1)S(1)} %gather_fusion, bf16[128,128,128]{2,1,0:T(8,128)(2,1)} %param.6, f32[128]{0:T(128)S(1)} %compare_convert_fusion), kind=kOutput, calls=%fused_computation.5 | convolution fusion | flops 67371008 | bytes 5767680 | tf_op jit(solution)/shard_map/tqj,tij->tqi/dot_general | solution.py:31
  40.2 0.1 broadcast.42.clone
  40.3 5.2 %scatter_fusion = f32[128,16,128]{2,1,0:T(8,128)S(1)} fusion(f32[128,16,128]{2,1,0:T(8,128)S(1)} %broadcast.42.clone, s32[128]{0:T(128)S(1)} %broadcast_subtract_fusion, f32[128,16,128]{2,1,0:T(8,128)S(1)} %convolution_multiply_fusion.1), kind=kCustom, calls=%fused_computation.2 | custom fusion | flops 262144 | bytes 3146240 | tf_op jit(solution)/shard_map/scatter-add | solution.py:33
  45.5 0.0 copy-start.1
  45.5 1.0 copy-done.1
  46.4 0.0 reduce-scatter.3.cloned.1.call-update
  46.5 0.0 all-gather.5.cloned.1.call-start
  46.5 27.4 %reduce-scatter.3.cloned.1.call-done = f32[32,16,128]{2,1,0:T(8,128)} async-done(((f32[128,16,128]{2,1,0:T(8,128)}), f32[32,16,128]{2,1,0:T(8,128)}) %reduce-scatter.3.cloned.1.call-update) | async-done | bytes 262160 | tf_op jit(solution)/shard_map/reduce_scatter | solution.py:34
  74.0 0.0 copy-done.2
  74.0 1.7 %fusion.1 = bf16[32,16,128]{2,1,0:T(8,128)(2,1)} fusion(f32[32,16,128]{2,1,0:T(8,128)} %reduce-scatter.3.cloned.1.call-done, f32[32,128]{1,0:T(8,128)S(1)} %get-tuple-element.6, s32[32,128]{1,0:T(8,128)S(1)} %copy-done.2, f32[32,128]{1,0:T(8,128)S(1)} %get-tuple-element.5), kind=kLoop, calls=%fused_computation.9 | loop fusion | flops 393216 | bytes 442368 | tf_op jit(solution)/shard_map/convert_element_type | solution.py:28
  75.6 0.0 all-gather.5.cloned.1.call-update
  75.7 0.0 reduce-scatter.5.cloned.1.call-start
  75.7 22.2 %all-gather.5.cloned.1.call-done = bf16[256,16,128]{2,1,0:T(8,128)(2,1)} async-done(((bf16[32,16,128]{2,1,0:T(8,128)(2,1)}), bf16[256,16,128]{2,1,0:T(8,128)(2,1)}) %all-gather.5.cloned.1.call-update) | async-done | bytes 1048592 | tf_op jit(solution)/shard_map/all_gather | solution.py:29
  97.9 1.9 %gather_fusion.1 = bf16[128,16,128]{2,1,0:T(8,128)(2,1)S(1)} fusion(bf16[256,16,128]{2,1,0:T(8,128)(2,1)} %all-gather.5.cloned.1.call-done, s32[1024]{0:T(1024)S(1)} %pad_clamp_fusion), kind=kCustom, calls=%fused_computation.1 | custom fusion | bytes 1049088 | tf_op jit(solution)/shard_map/gather | solution.py:30
  99.9 4.5 %convolution_multiply_fusion = f32[128,16,128]{2,1,0:T(8,128)S(1)} fusion(bf16[128,16,128]{2,1,0:T(8,128)(2,1)S(1)} %gather_fusion.1, bf16[128,128,128]{2,1,0:T(8,128)(2,1)} %param.6, f32[128]{0:T(128)S(1)} %compare_convert_fusion), kind=kOutput, calls=%fused_computation.4 | convolution fusion | flops 67371008 | bytes 5767680 | tf_op jit(solution)/shard_map/tqj,tij->tqi/dot_general | solution.py:31
  104.3 0.1 broadcast.42
  104.4 5.2 %scatter_fusion.1 = f32[128,16,128]{2,1,0:T(8,128)S(1)} fusion(f32[128,16,128]{2,1,0:T(8,128)S(1)} %broadcast.42, s32[128]{0:T(128)S(1)} %broadcast_subtract_fusion, f32[128,16,128]{2,1,0:T(8,128)S(1)} %convolution_multiply_fusion), kind=kCustom, calls=%fused_computation.3 | custom fusion | flops 262144 | bytes 3146240 | tf_op jit(solution)/shard_map/scatter-add | solution.py:33
  109.6 0.0 copy-start
  109.6 1.0 copy-done
  110.6 0.0 reduce-scatter.5.cloned.1.call-update
  110.6 27.5 %reduce-scatter.5.cloned.1.call-done = f32[32,16,128]{2,1,0:T(8,128)} async-done(((f32[128,16,128]{2,1,0:T(8,128)}), f32[32,16,128]{2,1,0:T(8,128)}) %reduce-scatter.5.cloned.1.call-update) | async-done | bytes 262160 | tf_op jit(solution)/shard_map/reduce_scatter | solution.py:34
  138.1 1.7 %select_add_fusion = f32[32,16,128]{2,1,0:T(8,128)} fusion(f32[32,16,128]{2,1,0:T(8,128)} %reduce-scatter.5.cloned.1.call-done, s32[32,128]{1,0:T(8,128)S(1)} %copy-done.2, f32[32,128]{1,0:T(8,128)S(1)} %get-tuple-element.5), kind=kLoop, calls=%fused_computation.6 | loop fusion | flops 262144 | bytes 557056 | tf_op jit(solution)/shard_map/add | solution.py:35
  (2 shorter events, 0.0 us)
Async XLA Ops:
  6.5 27.3 %all-gather.3.cloned.1.call-start = ((), (), s32[]{:S(2)}) async-start(), calls=%async_computation.2 | async-start | bytes 1179648 | tf_op jit(solution)/shard_map/all_gather | solution.py:26
  8.7 65.3 %reduce-scatter.3.cloned.1.call-start = ((), (), s32[]{:S(2)}) async-start(), calls=%async_computation.3 | async-start | bytes 1310720 | tf_op jit(solution)/shard_map/reduce_scatter | solution.py:34
  35.7 38.2 %copy-start.2 = (s32[32,128]{1,0:T(8,128)S(1)}, s32[32,128]{1,0:T(8,128)}, u32[]{:S(2)}) copy-start(s32[32,128]{1,0:T(8,128)} %param.11) | copy-start | bytes 49156
  45.5 1.0 copy-start.1
  46.5 51.4 %all-gather.5.cloned.1.call-start = ((), (), s32[]{:S(2)}) async-start(), calls=%async_computation.4 | async-start | bytes 1179648 | tf_op jit(solution)/shard_map/all_gather | solution.py:29
  75.7 62.4 %reduce-scatter.5.cloned.1.call-start = ((), (), s32[]{:S(2)}) async-start(), calls=%async_computation.5 | async-start | bytes 1310720 | tf_op jit(solution)/shard_map/reduce_scatter | solution.py:34
  109.6 1.0 copy-start
Sparse Core Ops, SparseCore 0:
  9.0 24.7 all-gather.2
  46.6 27.3 reduce-scatter.2
  75.8 22.0 all-gather.4
  110.7 27.3 reduce-scatter.4
where the time goes:
time: 147 us; the launch traced here: 146 us
  waiting for transfers between devices  100 us (68%)
  other arithmetic  17.2 us (12%)
  between operations  13.9 us (9%)
  matrix products  8.93 us (6%)
  local copies, waits for them, and re-layouts  5.96 us (4%)
    reduce_scatter x2, waiting for transfers between devices, local(): lax.psum_scatter(partial_rows, 'col', scatter_dimension=0, tiled=True)  54.9 us
    all_gather x2, waiting for transfers between devices, local(): gathered = lax.all_gather(own, 'row', axis=0, tiled=True)  45.2 us
    scatter-add x2, other arithmetic, local(): partial_rows = jax.ops.segment_sum(terms, local_rows, num_segments=rblk)  10.4 us
    dot_general x2, matrix products, local(): jnp.einsum('tqj,tij->tqi', picked, tiles, preferred_element_type=jnp.floa...  8.93 us
    gather x2, local copies, waits for them, and re-layouts, local(): picked = gathered[local_cols]  3.86 us
    convert_element_type x2, other arithmetic, local(): own = (field * scale[:, None, :]).astype(jnp.bfloat16)  3.08 us
  transfers between devices with their start and end apart: 4, of which 4 were waited for; matrix products, arithmetic and copies ran while one was open for 1% of the time, Pallas kernels for 0%

commit v1 on v0

v1 whole, which is shorter than its diff:
```python
import functools

import jax
import jax.numpy as jnp
from jax import lax
from jax.experimental import pallas as pl
from jax.experimental.pallas import tpu as pltpu
from jax.sharding import PartitionSpec as P

QC = 16
ITERS = 2
CHUNK = 16

SMEM = pltpu.SMEM
VMEM = pltpu.VMEM


def div_mod(value, size):
    if size & (size - 1) == 0:
        return lax.shift_right_logical(value, size.bit_length() - 1), value & (size - 1)
    return lax.div(value, size), lax.rem(value, size)


def spread(seeded, nrow, ncol, blk, *refs):
    nz = nrow // 2
    rows_ref, cols_ref, count_ref, tiles_hbm = refs[:4]
    refs = refs[4:]
    if seeded:
        fields, refs = refs[:2], refs[2:]
    else:
        fields, refs = refs[: nrow], refs[nrow:]
    outs, refs = refs[:ncol], refs[ncol:]
    tiles, total, picks, tile_sem, pick_sem = refs
    nt = tiles.shape[0]
    row_pos, col_pos = lax.axis_index("row"), lax.axis_index("col")

    def tile_copy(i):
        part = pl.ds(i * CHUNK, CHUNK)
        return pltpu.make_async_copy(tiles_hbm.at[part], tiles.at[part], tile_sem.at[i])

    for i in range(nt // CHUNK):
        tile_copy(i).start()
    if not seeded:
        copies = [
            pltpu.make_async_copy(f, picks.at[pl.ds(i * blk, blk)], pick_sem.at[i])
            for i, f in enumerate(fields)
        ]
        for c in copies:
            c.start()
    total[...] = jnp.zeros_like(total)
    if seeded:
        for half, f in enumerate(fields):
            for i in range(nz):
                for kind in range(2):
                    picks[kind, pl.ds((half * nz + i) * blk, blk), :] = f[i, kind].astype(jnp.float32)
    else:
        for c in copies:
            c.wait()
    query = lax.broadcasted_iota(jnp.int32, (QC, 128), 0).astype(jnp.float32)
    count = count_ref[0]
    base = row_pos * blk * ncol

    def pick(t):
        owner, offset = div_mod(cols_ref[t], blk)
        source, _ = div_mod(owner, ncol)
        far = source ^ row_pos
        slot = (far & 1) * nz + lax.shift_right_logical(far, 1)
        place = slot * blk + offset
        if seeded:
            label = picks[0, pl.ds(place, 1), :]
            scale = picks[1, pl.ds(place, 1), :]
            return jnp.where(label == query, scale, 0.0).astype(jnp.bfloat16)
        return picks[place]

    def chunk(i, carry):
        tile_copy(i).wait()
        terms = []
        for u in range(CHUNK):
            t = i * CHUNK + u
            terms.append(
                lax.dot_general(
                    pick(t), tiles[t], (((1,), (1,)), ((), ())), preferred_element_type=jnp.float32
                )
            )
        for u in range(CHUNK):
            t = i * CHUNK + u
            row = jnp.where(t < count, rows_ref[t] - base, total.shape[0] - 1)
            total[row] += terms[u]
        return carry

    lax.fori_loop(0, nt // CHUNK, chunk, 0)
    for k in range(ncol):
        part = total[pl.ds((col_pos ^ k) * blk, blk)]
        outs[k][...] = part.astype(outs[k].dtype)


def spread_call(seeded, nrow, ncol, blk, rows, cols, count, tiles, fields):
    nt = tiles.shape[0]
    slots = nrow * blk
    shape = (blk, QC, 128)
    picks = pltpu.VMEM((2, slots, 128), jnp.float32) if seeded else pltpu.VMEM((slots, QC, 128), jnp.bfloat16)
    return pl.pallas_call(
        functools.partial(spread, seeded, nrow, ncol, blk),
        out_shape=[jax.ShapeDtypeStruct(shape, jnp.float32)]
        + [jax.ShapeDtypeStruct(shape, jnp.bfloat16)] * (ncol - 1),
        in_specs=[pl.BlockSpec(memory_space=SMEM)] * 3
        + [pl.BlockSpec(memory_space=pl.ANY)]
        + [pl.BlockSpec(memory_space=VMEM if seeded else pl.ANY)] * len(fields),
        out_specs=[pl.BlockSpec(memory_space=VMEM)] * ncol,
        scratch_shapes=[
            pltpu.VMEM(tiles.shape, tiles.dtype),
            pltpu.VMEM((blk * ncol + 1, QC, 128), jnp.float32),
            picks,
            pltpu.SemaphoreType.DMA((nt // CHUNK,)),
            pltpu.SemaphoreType.DMA((nrow,)),
        ],
        compiler_params=pltpu.CompilerParams(vmem_limit_bytes=24 << 20),
        cost_estimate=pl.CostEstimate(
            flops=2 * nt * QC * 128 * 128, bytes_accessed=tiles.size * 2 + slots * QC * 256, transcendentals=0
        ),
    )(rows, cols, count, tiles, *fields)


def local(nrow, ncol, tiles, tile_rows, tile_cols, tile_count, degree, labels):
    blk = labels.shape[0]
    nz = nrow // 2

    def from_row(x, d):
        return lax.ppermute(x, "row", [(i, i ^ d) for i in range(nrow)])

    def from_col(x, k):
        return lax.ppermute(x, "col", [(i, i ^ k) for i in range(ncol)])

    scale = 1.0 / jnp.sqrt(degree.astype(jnp.float32))
    qidx = jnp.arange(QC, dtype=jnp.int32)
    prior = (labels[:, None, :] == qidx[None, :, None]).astype(jnp.float32)
    for step in range(ITERS):
        if step == 0:
            own = jnp.stack([labels.astype(jnp.bfloat16), scale.astype(jnp.bfloat16)])
            near = jnp.stack([own] + [from_row(own, 2 * m) for m in range(1, nz)])
            fields = [near, from_row(near, 1)]
        else:
            own = (field * scale[:, None, :]).astype(jnp.bfloat16)
            near = [own] + [from_row(own, 2 * m) for m in range(1, nz)]
            fields = near + [from_row(x, 1) for x in near]
        outs = spread_call(step == 0, nrow, ncol, blk, tile_rows, tile_cols, tile_count, tiles, fields)
        summed = outs[0]
        for k in range(1, ncol):
            summed = summed + from_col(outs[k], k).astype(jnp.float32)
        field = 0.8 * scale[:, None, :] * summed + 0.2 * prior
    return field


def solution(mesh):
    nrow, ncol = mesh.shape["row"], mesh.shape["col"]
    return jax.shard_map(
        functools.partial(local, nrow, ncol),
        mesh=mesh,
        in_specs=(
            P(("row", "col"), None, None),
            P(("row", "col")),
            P(("row", "col")),
            P(("row", "col")),
            P(("row", "col"), None),
            P(("row", "col"), None),
        ),
        out_specs=P(("row", "col"), None, None),
        check_vma=False,
    )
```

time: 147 us -> 61.1 us (0.42)
  waiting for transfers between devices: 100 us -> 26.3 us
  starting transfers between devices: 0.13 us -> 17.8 us
  other arithmetic: 17.2 us -> 2.44 us
  between operations: 13.9 us -> 0.7 us
  Pallas kernels: 0 us -> 9.93 us
  matrix products: 8.93 us -> 0 us
  local copies, waits for them, and re-layouts: 5.96 us -> 3.5 us
    reduce_scatter x2 -> x0, waiting for transfers between devices: 54.9 us -> none  [local(): lax.psum_scatter(partial_rows, 'col', scatter_dimension=0, tiled=True)]
    all_gather x2 -> x0, waiting for transfers between devices: 45.2 us -> none  [local(): gathered = lax.all_gather(own, 'row', axis=0, tiled=True)]
    ppermute x0 -> x17, waiting for transfers between devices: none -> 26.3 us  [the longest x11 14.3 us: from_row(): return lax.ppermute(x, 'row', [(i, i ^ d) for i in range(nrow)])]
    ppermute x0 -> x17, starting transfers between devices: none -> 17.8 us  [the longest x11 10.7 us: from_row(): return lax.ppermute(x, 'row', [(i, i ^ d) for i in range(nrow)])]
    scatter-add x2 -> x0, other arithmetic: 10.4 us -> none  [local(): partial_rows = jax.ops.segment_sum(terms, local_rows, num_segments=rblk)]
    pallas_call x0 -> x2, Pallas kernels: none -> 9.93 us  [spread_call(): pl.pallas_call(functools.partial(spread, seeded, nrow, ncol, blk), out_sh...]
    dot_general x2 -> x0, matrix products: 8.93 us -> none  [local(): jnp.einsum('tqj,tij->tqi', picked, tiles, preferred_element_type=jnp.floa...]
    gather x2 -> x0, local copies, waits for them, and re-layouts: 3.86 us -> none  [local(): picked = gathered[local_cols]]
  transfers between devices with their start and end apart: 4 -> 17, of which waited for: 4 -> 13; matrix products, arithmetic and copies ran while one was open for 1% -> 0% of each run, Pallas kernels for 0% -> 0%
where the time goes in v1:
time: 61.1 us; the launch traced here: 60.7 us
  waiting for transfers between devices  26.3 us (43%)
  starting transfers between devices  17.8 us (29%)
  Pallas kernels  9.93 us (16%)
  local copies, waits for them, and re-layouts  3.5 us (6%)
  other arithmetic  2.44 us (4%)
  between operations  0.7 us (1%)
    ppermute x11, waiting for transfers between devices, from_row(): return lax.ppermute(x, 'row', [(i, i ^ d) for i in range(nrow)])  14.3 us
    ppermute x6, waiting for transfers between devices, from_col(): return lax.ppermute(x, 'col', [(i, i ^ k) for i in range(ncol)])  12.1 us
    ppermute x11, starting transfers between devices, from_row(): return lax.ppermute(x, 'row', [(i, i ^ d) for i in range(nrow)])  10.7 us
    pallas_call x2, Pallas kernels, spread_call(): pl.pallas_call(functools.partial(spread, seeded, nrow, ncol, blk), out_sh...  9.93 us
    ppermute x6, starting transfers between devices, from_col(): return lax.ppermute(x, 'col', [(i, i ^ k) for i in range(ncol)])  7.11 us
    unnamed x8, local copies, waits for them, and re-layouts  3.5 us
  transfers between devices with their start and end apart: 17, of which 13 were waited for; matrix products, arithmetic and copies ran while one was open for 0% of the time, Pallas kernels for 0%

profile of v1, /device:TPU:0, one launch (start us, length us, event | category | flops | bytes accessed | tf_op | source)
XLA Modules:
  0.0 60.7 jit_solution(6426320357251363574)
XLA Ops:
  0.0 0.0 copy-start.3
  0.0 0.8 %convert_bitcast_fusion.1 = bf16[1,32,128]{2,1,0:T(8,128)(2,1)S(1)} fusion(s32[32,128]{1,0:T(8,128)} %param.11), kind=kLoop, calls=%fused_computation.9 | loop fusion | flops 4096 | bytes 24576 | tf_op jit(solution)/shard_map/stack | solution.py:139
  0.8 0.7 %broadcast_multiply_fusion = (f32[32,128]{1,0:T(8,128)S(1)}, bf16[1,32,128]{2,1,0:T(8,128)(2,1)S(1)}, f32[32,128]{1,0:T(8,128)S(1)}) fusion(s32[32,128]{1,0:T(8,128)} %param.10), kind=kLoop, calls=%fused_computation.10 | loop fusion | flops 12288 | bytes 57344 | tf_op jit(solution)/shard_map/mul | solution.py:150
  1.5 4.1 %collective-permute-start.1 = (bf16[2,32,128]{2,1,0:T(8,128)(2,1)S(1)}, bf16[2,32,128]{2,1,0:T(8,128)(2,1)S(1)}, u32[]{:S(2)}, u32[]{:S(2)}) collective-permute-start(bf16[2,32,128]{2,1,0:T(8,128)(2,1)S(1)} %get-tuple-element.25), channel_id=1, source_target_pairs={{0,16},{4,20},{8,24},{12,28},{16,0},{20,4},{24,8},{28,12},{1,17},{... | collective-permute-start | bytes 49160 | tf_op jit(solution)/shard_map/ppermute | solution.py:129
  5.6 1.6 %collective-permute-start = (bf16[2,32,128]{2,1,0:T(8,128)(2,1)S(1)}, bf16[2,32,128]{2,1,0:T(8,128)(2,1)S(1)}, u32[]{:S(2)}, u32[]{:S(2)}) collective-permute-start(bf16[2,32,128]{2,1,0:T(8,128)(2,1)S(1)} %get-tuple-element.25), channel_id=1, source_target_pairs={{0,8},{4,12},{8,0},{12,4},{16,24},{20,28},{24,16},{28,20},{1,9},{5... | collective-permute-start | bytes 49160 | tf_op jit(solution)/shard_map/ppermute | solution.py:129
  7.2 0.0 collective-permute-start.2
  7.2 0.1 collective-permute-done.1
  7.3 2.0 %collective-permute-done = bf16[2,32,128]{2,1,0:T(8,128)(2,1)S(1)} collective-permute-done((bf16[2,32,128]{2,1,0:T(8,128)(2,1)S(1)}, bf16[2,32,128]{2,1,0:T(8,128)(2,1)S(1)}, u32[]{:S(2)}, u32[]{:S(2)}) %collective-permute-start) | collective-permute-done | bytes 16416 | tf_op jit(solution)/shard_map/ppermute | solution.py:129
  9.4 3.4 %collective-permute-done.2 = bf16[2,32,128]{2,1,0:T(8,128)(2,1)S(1)} collective-permute-done((bf16[2,32,128]{2,1,0:T(8,128)(2,1)S(1)}, bf16[2,32,128]{2,1,0:T(8,128)(2,1)S(1)}, u32[]{:S(2)}, u32[]{:S(2)}) %collective-permute-start.2) | collective-permute-done | bytes 16416 | tf_op jit(solution)/shard_map/ppermute | solution.py:129
  12.8 0.1 collective-permute-start.3
  13.5 0.6 collective-permute-done.3.refs_5_
  14.1 0.0 copy-start
  14.1 2.2 %copy-done = bf16[128,128,128]{2,1,0:T(8,128)(2,1)S(1)} copy-done((bf16[128,128,128]{2,1,0:T(8,128)(2,1)S(1)}, bf16[128,128,128]{2,1,0:T(8,128)(2,1)}, u32[]{:S(2)}) %copy-start) | copy-done | bytes 4194328
  16.3 0.0 copy-start.1
  16.3 0.7 %copy-done.1 = s32[128]{0:T(128)S(1)} copy-done((s32[128]{0:T(128)S(1)}, s32[128]{0:T(128)}, u32[]{:S(2)}) %copy-start.1) | copy-done | bytes 536
  16.9 0.0 copy-start.2
  16.9 0.7 %copy-done.2 = s32[128]{0:T(128)S(1)} copy-done((s32[128]{0:T(128)S(1)}, s32[128]{0:T(128)}, u32[]{:S(2)}) %copy-start.2) | copy-done | bytes 536
  17.6 4.3 %shard_map.64 = (f32[32,16,128]{2,1,0:T(8,128)S(1)}, bf16[32,16,128]{2,1,0:T(8,128)(2,1)S(1)}, bf16[32,16,128]{2,1,0:T(8,128)(2,1)S(1)}, bf16[32,16,128]{2,1,0:T(8,128)(2,1)S(1)}) custom-call(s32[128]{0:T(128)S(1)} %copy-done.1, s32[128]{0:T(128)S(1)} %copy-done.2, s32[1]{0:T(128)S(6)} %copy.7.refs_2_, bf16[128,128,128]{2,1,0:T(8,128)(2,1)S(1)} %copy-done, ...), custom_call_target="tpu_custom_call" | custom-call | flops 67108864 | bytes 5242880 | tf_op jit(solution)/shard_map/pallas_call | solution.py:102
  21.9 1.5 %collective-permute-start.4 = (bf16[32,16,128]{2,1,0:T(8,128)(2,1)S(1)}, bf16[32,16,128]{2,1,0:T(8,128)(2,1)S(1)}, u32[]{:S(2)}, u32[]{:S(2)}) collective-permute-start(bf16[32,16,128]{2,1,0:T(8,128)(2,1)S(1)} %get-tuple-element.14), channel_id=1, source_target_pairs={{0,1},{1,0},{2,3},{3,2},{4,5},{5,4},{6,7},{7,6},{8,9},{9,8},{10,11... | collective-permute-start | bytes 393224 | tf_op jit(solution)/shard_map/ppermute | solution.py:132
  23.4 1.6 %collective-permute-start.5 = (bf16[32,16,128]{2,1,0:T(8,128)(2,1)S(1)}, bf16[32,16,128]{2,1,0:T(8,128)(2,1)S(1)}, u32[]{:S(2)}, u32[]{:S(2)}) collective-permute-start(bf16[32,16,128]{2,1,0:T(8,128)(2,1)S(1)} %get-tuple-element.15), channel_id=1, source_target_pairs={{0,2},{1,3},{2,0},{3,1},{4,6},{5,7},{6,4},{7,5},{8,10},{9,11},{10,... | collective-permute-start | bytes 393224 | tf_op jit(solution)/shard_map/ppermute | solution.py:132
  25.0 0.5 collective-permute-start.6
  25.4 2.4 %collective-permute-done.4 = bf16[32,16,128]{2,1,0:T(8,128)(2,1)S(1)} collective-permute-done((bf16[32,16,128]{2,1,0:T(8,128)(2,1)S(1)}, bf16[32,16,128]{2,1,0:T(8,128)(2,1)S(1)}, u32[]{:S(2)}, u32[]{:S(2)}) %collective-permute-start.4) | collective-permute-done | bytes 131104 | tf_op jit(solution)/shard_map/ppermute | solution.py:132
  27.9 3.6 %collective-permute-done.5 = bf16[32,16,128]{2,1,0:T(8,128)(2,1)S(1)} collective-permute-done((bf16[32,16,128]{2,1,0:T(8,128)(2,1)S(1)}, bf16[32,16,128]{2,1,0:T(8,128)(2,1)S(1)}, u32[]{:S(2)}, u32[]{:S(2)}) %collective-permute-start.5) | collective-permute-done | bytes 131104 | tf_op jit(solution)/shard_map/ppermute | solution.py:132
  31.5 0.0 collective-permute-done.6
  31.5 0.0 copy-done.3
  31.5 0.1 fusion.1.refs_4_
  31.6 0.3 collective-permute-start.9
  31.9 0.0 collective-permute-start.8
  31.9 4.2 %collective-permute-start.7 = (bf16[32,16,128]{2,1,0:T(8,128)(2,1)S(1)}, bf16[32,16,128]{2,1,0:T(8,128)(2,1)S(1)}, u32[]{:S(2)}, u32[]{:S(2)}) collective-permute-start(bf16[32,16,128]{2,1,0:T(8,128)(2,1)S(1)} %fusion.1.refs_4_), channel_id=1, source_target_pairs={{0,8},{4,12},{8,0},{12,4},{16,24},{20,28},{24,16},{28,20},{1,9},{5... | collective-permute-start | bytes 393224 | tf_op jit(solution)/shard_map/ppermute | solution.py:129
  36.1 0.0 collective-permute-start.10
  36.1 3.9 %collective-permute-done.9.refs_7_ = bf16[32,16,128]{2,1,0:T(8,128)(2,1)S(1)} collective-permute-done((bf16[32,16,128]{2,1,0:T(8,128)(2,1)S(1)}, bf16[32,16,128]{2,1,0:T(8,128)(2,1)S(1)}, u32[]{:S(2)}, u32[]{:S(2)}) %collective-permute-start.9) | collective-permute-done | bytes 131104 | tf_op jit(solution)/shard_map/ppermute | solution.py:129
  40.0 0.0 collective-permute-start.13
  40.0 3.2 %collective-permute-done.8.refs_6_ = bf16[32,16,128]{2,1,0:T(8,128)(2,1)S(1)} collective-permute-done((bf16[32,16,128]{2,1,0:T(8,128)(2,1)S(1)}, bf16[32,16,128]{2,1,0:T(8,128)(2,1)S(1)}, u32[]{:S(2)}, u32[]{:S(2)}) %collective-permute-start.8) | collective-permute-done | bytes 131104 | tf_op jit(solution)/shard_map/ppermute | solution.py:129
  43.2 0.0 collective-permute-start.12
  43.2 0.0 collective-permute-done.7.refs_5_
  43.2 0.5 collective-permute-start.11
  43.7 0.0 collective-permute-done.10.refs_8_
  43.7 0.0 collective-permute-done.13.refs_11_
  43.7 0.8 %collective-permute-done.12.refs_10_ = bf16[32,16,128]{2,1,0:T(8,128)(2,1)S(1)} collective-permute-done((bf16[32,16,128]{2,1,0:T(8,128)(2,1)S(1)}, bf16[32,16,128]{2,1,0:T(8,128)(2,1)S(1)}, u32[]{:S(2)}, u32[]{:S(2)}) %collective-permute-start.12) | collective-permute-done | bytes 131104 | tf_op jit(solution)/shard_map/ppermute | solution.py:129
  44.5 0.2 collective-permute-done.11.refs_9_
  44.7 5.6 %shard_map.65 = (f32[32,16,128]{2,1,0:T(8,128)S(1)}, bf16[32,16,128]{2,1,0:T(8,128)(2,1)S(1)}, bf16[32,16,128]{2,1,0:T(8,128)(2,1)S(1)}, bf16[32,16,128]{2,1,0:T(8,128)(2,1)S(1)}) custom-call(s32[128]{0:T(128)S(1)} %copy-done.1, s32[128]{0:T(128)S(1)} %copy-done.2, s32[1]{0:T(128)S(6)} %copy.7.refs_2_, bf16[128,128,128]{2,1,0:T(8,128)(2,1)S(1)} %copy-done, ...), custom_call_target="tpu_custom_call" | custom-call | flops 67108864 | bytes 5242880 | tf_op jit(solution)/shard_map/pallas_call | solution.py:102
  50.4 1.3 %collective-permute-start.14 = (bf16[32,16,128]{2,1,0:T(8,128)(2,1)S(1)}, bf16[32,16,128]{2,1,0:T(8,128)(2,1)S(1)}, u32[]{:S(2)}, u32[]{:S(2)}) collective-permute-start(bf16[32,16,128]{2,1,0:T(8,128)(2,1)S(1)} %get-tuple-element.18), channel_id=1, source_target_pairs={{0,1},{1,0},{2,3},{3,2},{4,5},{5,4},{6,7},{7,6},{8,9},{9,8},{10,11... | collective-permute-start | bytes 393224 | tf_op jit(solution)/shard_map/ppermute | solution.py:132
  51.7 0.9 %collective-permute-start.15 = (bf16[32,16,128]{2,1,0:T(8,128)(2,1)S(1)}, bf16[32,16,128]{2,1,0:T(8,128)(2,1)S(1)}, u32[]{:S(2)}, u32[]{:S(2)}) collective-permute-start(bf16[32,16,128]{2,1,0:T(8,128)(2,1)S(1)} %get-tuple-element.19), channel_id=1, source_target_pairs={{0,2},{1,3},{2,0},{3,1},{4,6},{5,7},{6,4},{7,5},{8,10},{9,11},{10,... | collective-permute-start | bytes 393224 | tf_op jit(solution)/shard_map/ppermute | solution.py:132
  52.5 1.4 %collective-permute-start.16 = (bf16[32,16,128]{2,1,0:T(8,128)(2,1)S(1)}, bf16[32,16,128]{2,1,0:T(8,128)(2,1)S(1)}, u32[]{:S(2)}, u32[]{:S(2)}) collective-permute-start(bf16[32,16,128]{2,1,0:T(8,128)(2,1)S(1)} %get-tuple-element.20), channel_id=1, source_target_pairs={{0,3},{1,2},{2,1},{3,0},{4,7},{5,6},{6,5},{7,4},{8,11},{9,10},{10,... | collective-permute-start | bytes 393224 | tf_op jit(solution)/shard_map/ppermute | solution.py:132
  53.9 2.8 %collective-permute-done.14 = bf16[32,16,128]{2,1,0:T(8,128)(2,1)S(1)} collective-permute-done((bf16[32,16,128]{2,1,0:T(8,128)(2,1)S(1)}, bf16[32,16,128]{2,1,0:T(8,128)(2,1)S(1)}, u32[]{:S(2)}, u32[]{:S(2)}) %collective-permute-start.14) | collective-permute-done | bytes 131104 | tf_op jit(solution)/shard_map/ppermute | solution.py:132
  56.8 1.5 %collective-permute-done.15 = bf16[32,16,128]{2,1,0:T(8,128)(2,1)S(1)} collective-permute-done((bf16[32,16,128]{2,1,0:T(8,128)(2,1)S(1)}, bf16[32,16,128]{2,1,0:T(8,128)(2,1)S(1)}, u32[]{:S(2)}, u32[]{:S(2)}) %collective-permute-start.15) | collective-permute-done | bytes 131104 | tf_op jit(solution)/shard_map/ppermute | solution.py:132
  58.3 1.6 %collective-permute-done.16 = bf16[32,16,128]{2,1,0:T(8,128)(2,1)S(1)} collective-permute-done((bf16[32,16,128]{2,1,0:T(8,128)(2,1)S(1)}, bf16[32,16,128]{2,1,0:T(8,128)(2,1)S(1)}, u32[]{:S(2)}, u32[]{:S(2)}) %collective-permute-start.16) | collective-permute-done | bytes 131104 | tf_op jit(solution)/shard_map/ppermute | solution.py:132
  59.9 0.8 %select_add_fusion = f32[32,16,128]{2,1,0:T(8,128)} fusion(bf16[32,16,128]{2,1,0:T(8,128)(2,1)S(1)} %collective-permute-done.16, bf16[32,16,128]{2,1,0:T(8,128)(2,1)S(1)} %collective-permute-done.15, f32[32,16,128]{2,1,0:T(8,128)S(1)} %get-tuple-element.17, bf16[32,16,128]{2,1,0:T(8,128)(2,1)S(1)} %collective-permute-done.14, s32[32,128]{1,0:T(8,128)S(1)} %copy-done.3, ...), kind=kLoop, calls=%fused_computation | loop fusion | flops 655360 | bytes 950272 | tf_op jit(solution)/shard_map/add | solution.py:150
  (2 shorter events, 0.0 us)
Async XLA Ops:
  0.0 31.5 %copy-start.3 = (s32[32,128]{1,0:T(8,128)S(1)}, s32[32,128]{1,0:T(8,128)}, u32[]{:S(2)}) copy-start(s32[32,128]{1,0:T(8,128)} %param.11) | copy-start | bytes 49156
  1.5 5.8 %collective-permute-start.1 = (bf16[2,32,128]{2,1,0:T(8,128)(2,1)S(1)}, bf16[2,32,128]{2,1,0:T(8,128)(2,1)S(1)}, u32[]{:S(2)}, u32[]{:S(2)}) collective-permute-start(bf16[2,32,128]{2,1,0:T(8,128)(2,1)S(1)} %get-tuple-element.25), channel_id=1, source_target_pairs={{0,16},{4,20},{8,24},{12,28},{16,0},{20,4},{24,8},{28,12},{1,17},{... | collective-permute-start | bytes 49160 | tf_op jit(solution)/shard_map/ppermute | solution.py:129
  5.6 3.7 %collective-permute-start = (bf16[2,32,128]{2,1,0:T(8,128)(2,1)S(1)}, bf16[2,32,128]{2,1,0:T(8,128)(2,1)S(1)}, u32[]{:S(2)}, u32[]{:S(2)}) collective-permute-start(bf16[2,32,128]{2,1,0:T(8,128)(2,1)S(1)} %get-tuple-element.25), channel_id=1, source_target_pairs={{0,8},{4,12},{8,0},{12,4},{16,24},{20,28},{24,16},{28,20},{1,9},{5... | collective-permute-start | bytes 49160 | tf_op jit(solution)/shard_map/ppermute | solution.py:129
  7.2 5.5 %collective-permute-start.2 = (bf16[2,32,128]{2,1,0:T(8,128)(2,1)S(1)}, bf16[2,32,128]{2,1,0:T(8,128)(2,1)S(1)}, u32[]{:S(2)}, u32[]{:S(2)}) collective-permute-start(bf16[2,32,128]{2,1,0:T(8,128)(2,1)S(1)} %get-tuple-element.25), channel_id=1, source_target_pairs={{0,24},{4,28},{8,16},{12,20},{16,8},{20,12},{24,0},{28,4},{1,25},{... | collective-permute-start | bytes 49160 | tf_op jit(solution)/shard_map/ppermute | solution.py:129
  12.8 1.3 %collective-permute-start.3 = (bf16[4,2,32,128]{3,2,1,0:T(8,128)(2,1)S(1)}, bf16[4,2,32,128]{3,2,1,0:T(8,128)(2,1)S(1)}, u32[]{:S(2)}, u32[]{:S(2)}) collective-permute-start(bf16[4,2,32,128]{3,2,1,0:T(8,128)(2,1)S(1)} %pad_maximum_fusion.refs_4_), channel_id=1, source_target_pairs={{0,4},{4,0},{8,12},{12,8},{16,20},{20,16},{24,28},{28,24},{1,5},{5... | collective-permute-start | bytes 196616 | tf_op jit(solution)/shard_map/ppermute | solution.py:129
  14.1 2.2 %copy-start = (bf16[128,128,128]{2,1,0:T(8,128)(2,1)S(1)}, bf16[128,128,128]{2,1,0:T(8,128)(2,1)}, u32[]{:S(2)}) copy-start(bf16[128,128,128]{2,1,0:T(8,128)(2,1)} %refs_3_.3) | copy-start | bytes 12582916
  16.3 0.7 %copy-start.1 = (s32[128]{0:T(128)S(1)}, s32[128]{0:T(128)}, u32[]{:S(2)}) copy-start(s32[128]{0:T(128)} %refs_0_.3) | copy-start | bytes 1540
  16.9 0.7 %copy-start.2 = (s32[128]{0:T(128)S(1)}, s32[128]{0:T(128)}, u32[]{:S(2)}) copy-start(s32[128]{0:T(128)} %refs_1_.3) | copy-start | bytes 1540
  21.9 6.0 %collective-permute-start.4 = (bf16[32,16,128]{2,1,0:T(8,128)(2,1)S(1)}, bf16[32,16,128]{2,1,0:T(8,128)(2,1)S(1)}, u32[]{:S(2)}, u32[]{:S(2)}) collective-permute-start(bf16[32,16,128]{2,1,0:T(8,128)(2,1)S(1)} %get-tuple-element.14), channel_id=1, source_target_pairs={{0,1},{1,0},{2,3},{3,2},{4,5},{5,4},{6,7},{7,6},{8,9},{9,8},{10,11... | collective-permute-start | bytes 393224 | tf_op jit(solution)/shard_map/ppermute | solution.py:132
  23.4 8.1 %collective-permute-start.5 = (bf16[32,16,128]{2,1,0:T(8,128)(2,1)S(1)}, bf16[32,16,128]{2,1,0:T(8,128)(2,1)S(1)}, u32[]{:S(2)}, u32[]{:S(2)}) collective-permute-start(bf16[32,16,128]{2,1,0:T(8,128)(2,1)S(1)} %get-tuple-element.15), channel_id=1, source_target_pairs={{0,2},{1,3},{2,0},{3,1},{4,6},{5,7},{6,4},{7,5},{8,10},{9,11},{10,... | collective-permute-start | bytes 393224 | tf_op jit(solution)/shard_map/ppermute | solution.py:132
  25.0 6.5 %collective-permute-start.6 = (bf16[32,16,128]{2,1,0:T(8,128)(2,1)S(1)}, bf16[32,16,128]{2,1,0:T(8,128)(2,1)S(1)}, u32[]{:S(2)}, u32[]{:S(2)}) collective-permute-start(bf16[32,16,128]{2,1,0:T(8,128)(2,1)S(1)} %get-tuple-element.16), channel_id=1, source_target_pairs={{0,3},{1,2},{2,1},{3,0},{4,7},{5,6},{6,5},{7,4},{8,11},{9,10},{10,... | collective-permute-start | bytes 393224 | tf_op jit(solution)/shard_map/ppermute | solution.py:132
  31.6 8.4 %collective-permute-start.9 = (bf16[32,16,128]{2,1,0:T(8,128)(2,1)S(1)}, bf16[32,16,128]{2,1,0:T(8,128)(2,1)S(1)}, u32[]{:S(2)}, u32[]{:S(2)}) collective-permute-start(bf16[32,16,128]{2,1,0:T(8,128)(2,1)S(1)} %fusion.1.refs_4_), channel_id=1, source_target_pairs={{0,24},{4,28},{8,16},{12,20},{16,8},{20,12},{24,0},{28,4},{1,25},{... | collective-permute-start | bytes 393224 | tf_op jit(solution)/shard_map/ppermute | solution.py:129
  31.9 11.3 %collective-permute-start.8 = (bf16[32,16,128]{2,1,0:T(8,128)(2,1)S(1)}, bf16[32,16,128]{2,1,0:T(8,128)(2,1)S(1)}, u32[]{:S(2)}, u32[]{:S(2)}) collective-permute-start(bf16[32,16,128]{2,1,0:T(8,128)(2,1)S(1)} %fusion.1.refs_4_), channel_id=1, source_target_pairs={{0,16},{4,20},{8,24},{12,28},{16,0},{20,4},{24,8},{28,12},{1,17},{... | collective-permute-start | bytes 393224 | tf_op jit(solution)/shard_map/ppermute | solution.py:129
  31.9 11.3 %collective-permute-start.7 = (bf16[32,16,128]{2,1,0:T(8,128)(2,1)S(1)}, bf16[32,16,128]{2,1,0:T(8,128)(2,1)S(1)}, u32[]{:S(2)}, u32[]{:S(2)}) collective-permute-start(bf16[32,16,128]{2,1,0:T(8,128)(2,1)S(1)} %fusion.1.refs_4_), channel_id=1, source_target_pairs={{0,8},{4,12},{8,0},{12,4},{16,24},{20,28},{24,16},{28,20},{1,9},{5... | collective-permute-start | bytes 393224 | tf_op jit(solution)/shard_map/ppermute | solution.py:129
  36.1 7.6 %collective-permute-start.10 = (bf16[32,16,128]{2,1,0:T(8,128)(2,1)S(1)}, bf16[32,16,128]{2,1,0:T(8,128)(2,1)S(1)}, u32[]{:S(2)}, u32[]{:S(2)}) collective-permute-start(bf16[32,16,128]{2,1,0:T(8,128)(2,1)S(1)} %fusion.1.refs_4_), channel_id=1, source_target_pairs={{0,4},{4,0},{8,12},{12,8},{16,20},{20,16},{24,28},{28,24},{1,5},{5... | collective-permute-start | bytes 393224 | tf_op jit(solution)/shard_map/ppermute | solution.py:129
  40.0 3.7 %collective-permute-start.13 = (bf16[32,16,128]{2,1,0:T(8,128)(2,1)S(1)}, bf16[32,16,128]{2,1,0:T(8,128)(2,1)S(1)}, u32[]{:S(2)}, u32[]{:S(2)}) collective-permute-start(bf16[32,16,128]{2,1,0:T(8,128)(2,1)S(1)} %collective-permute-done.9.refs_7_), channel_id=1, source_target_pairs={{0,4},{4,0},{8,12},{12,8},{16,20},{20,16},{24,28},{28,24},{1,5},{5... | collective-permute-start | bytes 393224 | tf_op jit(solution)/shard_map/ppermute | solution.py:129
  43.2 1.3 %collective-permute-start.12 = (bf16[32,16,128]{2,1,0:T(8,128)(2,1)S(1)}, bf16[32,16,128]{2,1,0:T(8,128)(2,1)S(1)}, u32[]{:S(2)}, u32[]{:S(2)}) collective-permute-start(bf16[32,16,128]{2,1,0:T(8,128)(2,1)S(1)} %collective-permute-done.8.refs_6_), channel_id=1, source_target_pairs={{0,4},{4,0},{8,12},{12,8},{16,20},{20,16},{24,28},{28,24},{1,5},{5... | collective-permute-start | bytes 393224 | tf_op jit(solution)/shard_map/ppermute | solution.py:129
  43.2 1.5 %collective-permute-start.11 = (bf16[32,16,128]{2,1,0:T(8,128)(2,1)S(1)}, bf16[32,16,128]{2,1,0:T(8,128)(2,1)S(1)}, u32[]{:S(2)}, u32[]{:S(2)}) collective-permute-start(bf16[32,16,128]{2,1,0:T(8,128)(2,1)S(1)} %collective-permute-done.7.refs_5_), channel_id=1, source_target_pairs={{0,4},{4,0},{8,12},{12,8},{16,20},{20,16},{24,28},{28,24},{1,5},{5... | collective-permute-start | bytes 393224 | tf_op jit(solution)/shard_map/ppermute | solution.py:129
  50.4 6.4 %collective-permute-start.14 = (bf16[32,16,128]{2,1,0:T(8,128)(2,1)S(1)}, bf16[32,16,128]{2,1,0:T(8,128)(2,1)S(1)}, u32[]{:S(2)}, u32[]{:S(2)}) collective-permute-start(bf16[32,16,128]{2,1,0:T(8,128)(2,1)S(1)} %get-tuple-element.18), channel_id=1, source_target_pairs={{0,1},{1,0},{2,3},{3,2},{4,5},{5,4},{6,7},{7,6},{8,9},{9,8},{10,11... | collective-permute-start | bytes 393224 | tf_op jit(solution)/shard_map/ppermute | solution.py:132
  51.7 6.6 %collective-permute-start.15 = (bf16[32,16,128]{2,1,0:T(8,128)(2,1)S(1)}, bf16[32,16,128]{2,1,0:T(8,128)(2,1)S(1)}, u32[]{:S(2)}, u32[]{:S(2)}) collective-permute-start(bf16[32,16,128]{2,1,0:T(8,128)(2,1)S(1)} %get-tuple-element.19), channel_id=1, source_target_pairs={{0,2},{1,3},{2,0},{3,1},{4,6},{5,7},{6,4},{7,5},{8,10},{9,11},{10,... | collective-permute-start | bytes 393224 | tf_op jit(solution)/shard_map/ppermute | solution.py:132
  52.5 7.4 %collective-permute-start.16 = (bf16[32,16,128]{2,1,0:T(8,128)(2,1)S(1)}, bf16[32,16,128]{2,1,0:T(8,128)(2,1)S(1)}, u32[]{:S(2)}, u32[]{:S(2)}) collective-permute-start(bf16[32,16,128]{2,1,0:T(8,128)(2,1)S(1)} %get-tuple-element.20), channel_id=1, source_target_pairs={{0,3},{1,2},{2,1},{3,0},{4,7},{5,6},{6,5},{7,4},{8,11},{9,10},{10,... | collective-permute-start | bytes 393224 | tf_op jit(solution)/shard_map/ppermute | solution.py:132

commit v2 on v1

v2 whole, which is shorter than its diff:
```python
import functools

import jax
import jax.numpy as jnp
from jax import lax
from jax.experimental import pallas as pl
from jax.experimental.pallas import tpu as pltpu
from jax.sharding import PartitionSpec as P

QC = 16
ITERS = 2
COPY = 16
UNROLL = 64

HBM = pltpu.HBM
VMEM = pltpu.VMEM


def div(value, size):
    if size & (size - 1) == 0:
        return lax.shift_right_logical(value, size.bit_length() - 1)
    return lax.div(value, size)


def prepare(degree, labels, scale_ref, own_ref):
    scale = 1.0 / jnp.sqrt(degree[...].astype(jnp.float32))
    scale_ref[...] = scale
    own_ref[0] = labels[...].astype(jnp.float32).astype(jnp.bfloat16)
    own_ref[1] = scale.astype(jnp.bfloat16)


def spread(seeded, nrow, ncol, blk, *refs):
    nz = nrow // 2
    tables_hbm, tiles_hbm, refs = refs[:3], refs[3], refs[4:]
    nfields = 2 if seeded else nrow
    fields, refs = refs[:nfields], refs[nfields:]
    outs, refs = refs[:ncol], refs[ncol:]
    tiles, total, picks, rows, cols, counts, tile_sem, table_sem = refs
    nt = tiles.shape[0]
    row_pos, col_pos = lax.axis_index("row"), lax.axis_index("col")

    tables = [
        pltpu.make_async_copy(source, target, table_sem.at[i])
        for i, (source, target) in enumerate(zip(tables_hbm, (rows, cols, counts)))
    ]
    for c in tables:
        c.start()

    def tile_copy(i):
        part = pl.ds(i * COPY, COPY)
        return pltpu.make_async_copy(tiles_hbm.at[part], tiles.at[part], tile_sem.at[i])

    for i in range(nt // COPY):
        tile_copy(i).start()
    total[...] = jnp.zeros_like(total)
    if seeded:
        for half, f in enumerate(fields):
            for i in range(nz):
                for kind in range(2):
                    picks[kind, pl.ds((half * nz + i) * blk, blk), :] = f[i, kind].astype(jnp.float32)
    else:
        for i, f in enumerate(fields):
            picks[pl.ds(i * blk, blk)] = f[...]
    query = lax.broadcasted_iota(jnp.int32, (QC, 128), 0).astype(jnp.float32)
    for c in tables:
        c.wait()
    count = counts[0]
    base = row_pos * blk * ncol

    def pick(t):
        owner = div(cols[t], blk)
        offset = cols[t] - owner * blk
        far = div(owner, ncol) ^ row_pos
        slot = (far & 1) * nz + lax.shift_right_logical(far, 1)
        place = slot * blk + offset
        if seeded:
            label = picks[0, pl.ds(place, 1), :]
            scale = picks[1, pl.ds(place, 1), :]
            return jnp.where(label == query, scale, 0.0).astype(jnp.bfloat16)
        return picks[place]

    def step(i, carry):
        for j in range(UNROLL // COPY):
            tile_copy(i * (UNROLL // COPY) + j).wait()
        terms = []
        for u in range(0, UNROLL, 2):
            t = i * UNROLL + u
            pair = lax.dot_general(
                jnp.concatenate([pick(t), pick(t + 1)], 0),
                tiles[pl.ds(t, 2)].reshape(256, 128),
                (((1,), (1,)), ((), ())),
                preferred_element_type=jnp.float32,
            )
            terms += [pair[:QC, :128], pair[QC:, 128:]]
        for u in range(UNROLL):
            t = i * UNROLL + u
            row = jnp.where(t < count, rows[t] - base, total.shape[0] - 1)
            total[row] += terms[u]
        return carry

    lax.fori_loop(0, nt // UNROLL, step, 0)
    for k in range(ncol):
        part = total[pl.ds((col_pos ^ k) * blk, blk)]
        outs[k][...] = part.astype(outs[k].dtype)


def spread_call(seeded, nrow, ncol, blk, tables, tiles, fields):
    nt = tiles.shape[0]
    slots = nrow * blk
    shape = (blk, QC, 128)
    picks = pltpu.VMEM((2, slots, 128), jnp.float32) if seeded else pltpu.VMEM((slots, QC, 128), jnp.bfloat16)
    return pl.pallas_call(
        functools.partial(spread, seeded, nrow, ncol, blk),
        out_shape=[jax.ShapeDtypeStruct(shape, jnp.float32)]
        + [jax.ShapeDtypeStruct(shape, jnp.bfloat16)] * (ncol - 1),
        in_specs=[pl.BlockSpec(memory_space=HBM)] * 4 + [pl.BlockSpec(memory_space=VMEM)] * len(fields),
        out_specs=[pl.BlockSpec(memory_space=VMEM)] * ncol,
        scratch_shapes=[
            pltpu.VMEM(tiles.shape, tiles.dtype),
            pltpu.VMEM((blk * ncol + 1, QC, 128), jnp.float32),
            picks,
            *(pltpu.SMEM(x.shape, x.dtype) for x in tables),
            pltpu.SemaphoreType.DMA((nt // COPY,)),
            pltpu.SemaphoreType.DMA((len(tables),)),
        ],
        compiler_params=pltpu.CompilerParams(vmem_limit_bytes=24 << 20),
        cost_estimate=pl.CostEstimate(
            flops=2 * nt * QC * 128 * 128, bytes_accessed=tiles.size * 2 + slots * QC * 256, transcendentals=0
        ),
    )(*tables, tiles, *fields)


def local(nrow, ncol, tiles, tile_rows, tile_cols, tile_count, degree, labels):
    blk = labels.shape[0]
    nz = nrow // 2

    def from_row(x, d):
        return lax.ppermute(x, "row", [(i, i ^ d) for i in range(nrow)])

    def from_col(x, k):
        return lax.ppermute(x, "col", [(i, i ^ k) for i in range(ncol)])

    scale, seeds = pl.pallas_call(
        prepare,
        out_shape=[
            jax.ShapeDtypeStruct((blk, 128), jnp.float32),
            jax.ShapeDtypeStruct((2, blk, 128), jnp.bfloat16),
        ],
        in_specs=[pl.BlockSpec(memory_space=VMEM)] * 2,
        out_specs=[pl.BlockSpec(memory_space=VMEM)] * 2,
    )(degree, labels)
    qidx = jnp.arange(QC, dtype=jnp.int32)
    prior = (labels[:, None, :] == qidx[None, :, None]).astype(jnp.float32)
    for step in range(ITERS):
        if step == 0:
            near = jnp.stack([seeds] + [from_row(seeds, 2 * m) for m in range(1, nz)])
            fields = [near, from_row(near, 1)]
        else:
            own = (field * scale[:, None, :]).astype(jnp.bfloat16)
            near = [own] + [from_row(own, 2 * m) for m in range(1, nz)]
            fields = near + [from_row(x, 1) for x in near]
        outs = spread_call(step == 0, nrow, ncol, blk, (tile_rows, tile_cols, tile_count), tiles, fields)
        summed = outs[0]
        for k in range(1, ncol):
            summed = summed + from_col(outs[k], k).astype(jnp.float32)
        field = 0.8 * scale[:, None, :] * summed + 0.2 * prior
    return field


def solution(mesh):
    nrow, ncol = mesh.shape["row"], mesh.shape["col"]
    return jax.shard_map(
        functools.partial(local, nrow, ncol),
        mesh=mesh,
        in_specs=(
            P(("row", "col"), None, None),
            P(("row", "col")),
            P(("row", "col")),
            P(("row", "col")),
            P(("row", "col"), None),
            P(("row", "col"), None),
        ),
        out_specs=P(("row", "col"), None, None),
        check_vma=False,
    )
```

time: 61.1 us -> 57.3 us (0.938)
  Pallas kernels: 9.93 us -> 6.22 us
  waiting for transfers between devices: 26.3 us -> 27.1 us
  other arithmetic: 2.44 us -> 1.65 us
    pallas_call x2, Pallas kernels: 9.93 us -> 4.81 us  [spread_call(): pl.pallas_call(functools.partial(spread, seeded, nrow, ncol, blk), out_sh...]
    pallas_call x0 -> x1, Pallas kernels: none -> 1.41 us  [local(): pl.pallas_call(prepare, out_shape=[jax.ShapeDtypeStruct((blk, 128), jnp.f...]
    mul x1, other arithmetic: 0.72 us -> 0.01 us  [local(): field = 0.8 * scale[:, None, :] * summed + 0.2 * prior]
    unnamed x8 -> x10, local copies, waits for them, and re-layouts: 3.5 us -> 3.5 us
  transfers between devices with their start and end apart: 17 -> 17, of which waited for: 13 -> 11; matrix products, arithmetic and copies ran while one was open for 0% -> 0% of each run, Pallas kernels for 0% -> 0%
where the time goes in v2:
time: 57.3 us; the launch traced here: 57 us
  waiting for transfers between devices  27.1 us (47%)
  starting transfers between devices  17.8 us (31%)
  Pallas kernels  6.22 us (11%)
  local copies, waits for them, and re-layouts  3.5 us (6%)
  other arithmetic  1.65 us (3%)
  between operations  0.7 us (1%)
    ppermute x11, waiting for transfers between devices, from_row(): return lax.ppermute(x, 'row', [(i, i ^ d) for i in range(nrow)])  14.5 us
    ppermute x6, waiting for transfers between devices, from_col(): return lax.ppermute(x, 'col', [(i, i ^ k) for i in range(ncol)])  12.5 us
    ppermute x11, starting transfers between devices, from_row(): return lax.ppermute(x, 'row', [(i, i ^ d) for i in range(nrow)])  10.7 us
    ppermute x6, starting transfers between devices, from_col(): return lax.ppermute(x, 'col', [(i, i ^ k) for i in range(ncol)])  7.12 us
    pallas_call x2, Pallas kernels, spread_call(): pl.pallas_call(functools.partial(spread, seeded, nrow, ncol, blk), out_sh...  4.81 us
    unnamed x10, local copies, waits for them, and re-layouts  3.5 us
    pallas_call x1, Pallas kernels, local(): pl.pallas_call(prepare, out_shape=[jax.ShapeDtypeStruct((blk, 128), jnp.f...  1.41 us
  transfers between devices with their start and end apart: 17, of which 11 were waited for; matrix products, arithmetic and copies ran while one was open for 0% of the time, Pallas kernels for 0%

profile of v2, /device:TPU:0, one launch (start us, length us, event | category | flops | bytes accessed | tf_op | source)
XLA Modules:
  0.0 57.0 jit_solution(12944708495307531575)
XLA Ops:
  0.0 0.0 copy-start.3
  0.0 1.4 %shard_map.64 = (f32[32,128]{1,0:T(8,128)}, bf16[2,32,128]{2,1,0:T(8,128)(2,1)}) custom-call(s32[32,128]{1,0:T(8,128)} %degree.1, s32[32,128]{1,0:T(8,128)} %labels.1), custom_call_target="tpu_custom_call" | custom-call | tf_op jit(solution)/shard_map/pallas_call | solution.py:143
  1.4 0.0 copy-start.4
  1.4 5.0 %collective-permute-start.2 = (bf16[2,32,128]{2,1,0:T(8,128)(2,1)}, bf16[2,32,128]{2,1,0:T(8,128)(2,1)S(1)}, u32[]{:S(2)}, u32[]{:S(2)}) collective-permute-start(bf16[2,32,128]{2,1,0:T(8,128)(2,1)} %get-tuple-element.16), channel_id=1, source_target_pairs={{0,24},{4,28},{8,16},{12,20},{16,8},{20,12},{24,0},{28,4},{1,25},{... | collective-permute-start | bytes 49160 | tf_op jit(solution)/shard_map/ppermute | solution.py:138
  6.5 0.0 collective-permute-start.1
  6.5 0.6 %collective-permute-start = (bf16[2,32,128]{2,1,0:T(8,128)(2,1)}, bf16[2,32,128]{2,1,0:T(8,128)(2,1)S(1)}, u32[]{:S(2)}, u32[]{:S(2)}) collective-permute-start(bf16[2,32,128]{2,1,0:T(8,128)(2,1)} %get-tuple-element.16), channel_id=1, source_target_pairs={{0,8},{4,12},{8,0},{12,4},{16,24},{20,28},{24,16},{28,20},{1,9},{5... | collective-permute-start | bytes 49160 | tf_op jit(solution)/shard_map/ppermute | solution.py:138
  7.1 1.3 %collective-permute-done.2 = bf16[2,32,128]{2,1,0:T(8,128)(2,1)S(1)} collective-permute-done((bf16[2,32,128]{2,1,0:T(8,128)(2,1)}, bf16[2,32,128]{2,1,0:T(8,128)(2,1)S(1)}, u32[]{:S(2)}, u32[]{:S(2)}) %collective-permute-start.2) | collective-permute-done | bytes 16416 | tf_op jit(solution)/shard_map/ppermute | solution.py:138
  8.4 2.9 %collective-permute-done.1 = bf16[2,32,128]{2,1,0:T(8,128)(2,1)S(1)} collective-permute-done((bf16[2,32,128]{2,1,0:T(8,128)(2,1)}, bf16[2,32,128]{2,1,0:T(8,128)(2,1)S(1)}, u32[]{:S(2)}, u32[]{:S(2)}) %collective-permute-start.1) | collective-permute-done | bytes 16416 | tf_op jit(solution)/shard_map/ppermute | solution.py:138
  11.3 0.0 collective-permute-done
  11.3 0.7 %pad_maximum_fusion.refs_4_ = bf16[4,2,32,128]{3,2,1,0:T(8,128)(2,1)S(1)} fusion(bf16[1,2,32,128]{3,2,1,0:T(8,128)(2,1)S(1)} %bitcast.5, bf16[1,2,32,128]{3,2,1,0:T(8,128)(2,1)S(1)} %bitcast.6, bf16[1,2,32,128]{3,2,1,0:T(8,128)(2,1)S(1)} %bitcast.7, bf16[1,2,32,128]{3,2,1,0:T(8,128)(2,1)} %bitcast.4), kind=kLoop, calls=%fused_computation.5 | loop fusion | flops 98304 | bytes 131072 | tf_op jit(solution)/shard_map/stack | solution.py:156
  12.1 0.1 collective-permute-start.3
  12.8 0.6 %collective-permute-done.3.refs_5_ = bf16[4,2,32,128]{3,2,1,0:T(8,128)(2,1)S(1)} collective-permute-done((bf16[4,2,32,128]{3,2,1,0:T(8,128)(2,1)S(1)}, bf16[4,2,32,128]{3,2,1,0:T(8,128)(2,1)S(1)}, u32[]{:S(2)}, u32[]{:S(2)}) %collective-permute-start.3) | collective-permute-done | bytes 65568 | tf_op jit(solution)/shard_map/ppermute | solution.py:138
  13.4 0.0 copy-start
  13.4 2.2 %copy-done = bf16[128,128,128]{2,1,0:T(8,128)(2,1)S(1)} copy-done((bf16[128,128,128]{2,1,0:T(8,128)(2,1)S(1)}, bf16[128,128,128]{2,1,0:T(8,128)(2,1)}, u32[]{:S(2)}) %copy-start) | copy-done | bytes 4194328
  15.6 0.0 copy-start.1
  15.6 0.7 %copy-done.1 = s32[128]{0:T(128)S(1)} copy-done((s32[128]{0:T(128)S(1)}, s32[128]{0:T(128)}, u32[]{:S(2)}) %copy-start.1) | copy-done | bytes 536
  16.2 0.0 copy-start.2
  16.2 0.7 %copy-done.2 = s32[128]{0:T(128)S(1)} copy-done((s32[128]{0:T(128)S(1)}, s32[128]{0:T(128)}, u32[]{:S(2)}) %copy-start.2) | copy-done | bytes 536
  16.9 2.4 %shard_map.65 = (f32[32,16,128]{2,1,0:T(8,128)S(1)}, bf16[32,16,128]{2,1,0:T(8,128)(2,1)S(1)}, bf16[32,16,128]{2,1,0:T(8,128)(2,1)S(1)}, bf16[32,16,128]{2,1,0:T(8,128)(2,1)S(1)}) custom-call(s32[128]{0:T(128)S(1)} %copy-done.1, s32[128]{0:T(128)S(1)} %copy-done.2, s32[1]{0:T(128)S(6)} %copy.7.refs_2_, bf16[128,128,128]{2,1,0:T(8,128)(2,1)S(1)} %copy-done, ...), custom_call_target="tpu_custom_call" | custom-call | flops 67108864 | bytes 5242880 | tf_op jit(solution)/shard_map/pallas_call | solution.py:112
  19.3 1.6 %collective-permute-start.4 = (bf16[32,16,128]{2,1,0:T(8,128)(2,1)S(1)}, bf16[32,16,128]{2,1,0:T(8,128)(2,1)S(1)}, u32[]{:S(2)}, u32[]{:S(2)}) collective-permute-start(bf16[32,16,128]{2,1,0:T(8,128)(2,1)S(1)} %get-tuple-element.18), channel_id=1, source_target_pairs={{0,1},{1,0},{2,3},{3,2},{4,5},{5,4},{6,7},{7,6},{8,9},{9,8},{10,11... | collective-permute-start | bytes 393224 | tf_op jit(solution)/shard_map/ppermute | solution.py:141
  20.8 1.5 %collective-permute-start.5 = (bf16[32,16,128]{2,1,0:T(8,128)(2,1)S(1)}, bf16[32,16,128]{2,1,0:T(8,128)(2,1)S(1)}, u32[]{:S(2)}, u32[]{:S(2)}) collective-permute-start(bf16[32,16,128]{2,1,0:T(8,128)(2,1)S(1)} %get-tuple-element.19), channel_id=1, source_target_pairs={{0,2},{1,3},{2,0},{3,1},{4,6},{5,7},{6,4},{7,5},{8,10},{9,11},{10,... | collective-permute-start | bytes 393224 | tf_op jit(solution)/shard_map/ppermute | solution.py:141
  22.4 0.5 collective-permute-start.6
  22.8 0.0 copy-done.4
  22.9 2.5 %collective-permute-done.4 = bf16[32,16,128]{2,1,0:T(8,128)(2,1)S(1)} collective-permute-done((bf16[32,16,128]{2,1,0:T(8,128)(2,1)S(1)}, bf16[32,16,128]{2,1,0:T(8,128)(2,1)S(1)}, u32[]{:S(2)}, u32[]{:S(2)}) %collective-permute-start.4) | collective-permute-done | bytes 131104 | tf_op jit(solution)/shard_map/ppermute | solution.py:141
  25.3 3.7 %collective-permute-done.5 = bf16[32,16,128]{2,1,0:T(8,128)(2,1)S(1)} collective-permute-done((bf16[32,16,128]{2,1,0:T(8,128)(2,1)S(1)}, bf16[32,16,128]{2,1,0:T(8,128)(2,1)S(1)}, u32[]{:S(2)}, u32[]{:S(2)}) %collective-permute-start.5) | collective-permute-done | bytes 131104 | tf_op jit(solution)/shard_map/ppermute | solution.py:141
  29.0 0.0 collective-permute-done.6
  29.0 0.0 copy-done.3
  29.0 0.1 fusion.1.refs_4_
  29.1 1.6 %collective-permute-start.9 = (bf16[32,16,128]{2,1,0:T(8,128)(2,1)S(1)}, bf16[32,16,128]{2,1,0:T(8,128)(2,1)S(1)}, u32[]{:S(2)}, u32[]{:S(2)}) collective-permute-start(bf16[32,16,128]{2,1,0:T(8,128)(2,1)S(1)} %fusion.1.refs_4_), channel_id=1, source_target_pairs={{0,24},{4,28},{8,16},{12,20},{16,8},{20,12},{24,0},{28,4},{1,25},{... | collective-permute-start | bytes 393224 | tf_op jit(solution)/shard_map/ppermute | solution.py:138
  30.7 0.5 collective-permute-start.8
  31.2 2.4 %collective-permute-start.7 = (bf16[32,16,128]{2,1,0:T(8,128)(2,1)S(1)}, bf16[32,16,128]{2,1,0:T(8,128)(2,1)S(1)}, u32[]{:S(2)}, u32[]{:S(2)}) collective-permute-start(bf16[32,16,128]{2,1,0:T(8,128)(2,1)S(1)} %fusion.1.refs_4_), channel_id=1, source_target_pairs={{0,8},{4,12},{8,0},{12,4},{16,24},{20,28},{24,16},{28,20},{1,9},{5... | collective-permute-start | bytes 393224 | tf_op jit(solution)/shard_map/ppermute | solution.py:138
  33.6 0.0 collective-permute-start.10
  33.6 3.8 %collective-permute-done.9.refs_7_ = bf16[32,16,128]{2,1,0:T(8,128)(2,1)S(1)} collective-permute-done((bf16[32,16,128]{2,1,0:T(8,128)(2,1)S(1)}, bf16[32,16,128]{2,1,0:T(8,128)(2,1)S(1)}, u32[]{:S(2)}, u32[]{:S(2)}) %collective-permute-start.9) | collective-permute-done | bytes 131104 | tf_op jit(solution)/shard_map/ppermute | solution.py:138
  37.4 0.0 collective-permute-start.13
  37.4 4.8 %collective-permute-done.8.refs_6_ = bf16[32,16,128]{2,1,0:T(8,128)(2,1)S(1)} collective-permute-done((bf16[32,16,128]{2,1,0:T(8,128)(2,1)S(1)}, bf16[32,16,128]{2,1,0:T(8,128)(2,1)S(1)}, u32[]{:S(2)}, u32[]{:S(2)}) %collective-permute-start.8) | collective-permute-done | bytes 131104 | tf_op jit(solution)/shard_map/ppermute | solution.py:138
  42.3 0.0 collective-permute-start.12
  42.3 0.0 collective-permute-done.7.refs_5_
  42.3 0.5 collective-permute-start.11
  42.8 0.0 collective-permute-done.10.refs_8_
  42.8 0.0 collective-permute-done.13.refs_11_
  42.8 0.8 %collective-permute-done.12.refs_10_ = bf16[32,16,128]{2,1,0:T(8,128)(2,1)S(1)} collective-permute-done((bf16[32,16,128]{2,1,0:T(8,128)(2,1)S(1)}, bf16[32,16,128]{2,1,0:T(8,128)(2,1)S(1)}, u32[]{:S(2)}, u32[]{:S(2)}) %collective-permute-start.12) | collective-permute-done | bytes 131104 | tf_op jit(solution)/shard_map/ppermute | solution.py:138
  43.6 0.2 collective-permute-done.11.refs_9_
  43.8 2.4 %shard_map.66 = (f32[32,16,128]{2,1,0:T(8,128)S(1)}, bf16[32,16,128]{2,1,0:T(8,128)(2,1)S(1)}, bf16[32,16,128]{2,1,0:T(8,128)(2,1)S(1)}, bf16[32,16,128]{2,1,0:T(8,128)(2,1)S(1)}) custom-call(s32[128]{0:T(128)S(1)} %copy-done.1, s32[128]{0:T(128)S(1)} %copy-done.2, s32[1]{0:T(128)S(6)} %copy.7.refs_2_, bf16[128,128,128]{2,1,0:T(8,128)(2,1)S(1)} %copy-done, ...), custom_call_target="tpu_custom_call" | custom-call | flops 67108864 | bytes 5242880 | tf_op jit(solution)/shard_map/pallas_call | solution.py:112
  46.2 1.7 %collective-permute-start.14 = (bf16[32,16,128]{2,1,0:T(8,128)(2,1)S(1)}, bf16[32,16,128]{2,1,0:T(8,128)(2,1)S(1)}, u32[]{:S(2)}, u32[]{:S(2)}) collective-permute-start(bf16[32,16,128]{2,1,0:T(8,128)(2,1)S(1)} %get-tuple-element.22), channel_id=1, source_target_pairs={{0,1},{1,0},{2,3},{3,2},{4,5},{5,4},{6,7},{7,6},{8,9},{9,8},{10,11... | collective-permute-start | bytes 393224 | tf_op jit(solution)/shard_map/ppermute | solution.py:141
  47.9 0.7 %collective-permute-start.15 = (bf16[32,16,128]{2,1,0:T(8,128)(2,1)S(1)}, bf16[32,16,128]{2,1,0:T(8,128)(2,1)S(1)}, u32[]{:S(2)}, u32[]{:S(2)}) collective-permute-start(bf16[32,16,128]{2,1,0:T(8,128)(2,1)S(1)} %get-tuple-element.23), channel_id=1, source_target_pairs={{0,2},{1,3},{2,0},{3,1},{4,6},{5,7},{6,4},{7,5},{8,10},{9,11},{10,... | collective-permute-start | bytes 393224 | tf_op jit(solution)/shard_map/ppermute | solution.py:141
  48.5 1.2 %collective-permute-start.16 = (bf16[32,16,128]{2,1,0:T(8,128)(2,1)S(1)}, bf16[32,16,128]{2,1,0:T(8,128)(2,1)S(1)}, u32[]{:S(2)}, u32[]{:S(2)}) collective-permute-start(bf16[32,16,128]{2,1,0:T(8,128)(2,1)S(1)} %get-tuple-element.24), channel_id=1, source_target_pairs={{0,3},{1,2},{2,1},{3,0},{4,7},{5,6},{6,5},{7,4},{8,11},{9,10},{10,... | collective-permute-start | bytes 393224 | tf_op jit(solution)/shard_map/ppermute | solution.py:141
  49.8 2.5 %collective-permute-done.14 = bf16[32,16,128]{2,1,0:T(8,128)(2,1)S(1)} collective-permute-done((bf16[32,16,128]{2,1,0:T(8,128)(2,1)S(1)}, bf16[32,16,128]{2,1,0:T(8,128)(2,1)S(1)}, u32[]{:S(2)}, u32[]{:S(2)}) %collective-permute-start.14) | collective-permute-done | bytes 131104 | tf_op jit(solution)/shard_map/ppermute | solution.py:141
  52.3 3.9 %collective-permute-done.15 = bf16[32,16,128]{2,1,0:T(8,128)(2,1)S(1)} collective-permute-done((bf16[32,16,128]{2,1,0:T(8,128)(2,1)S(1)}, bf16[32,16,128]{2,1,0:T(8,128)(2,1)S(1)}, u32[]{:S(2)}, u32[]{:S(2)}) %collective-permute-start.15) | collective-permute-done | bytes 131104 | tf_op jit(solution)/shard_map/ppermute | solution.py:141
  56.2 0.0 collective-permute-done.16
  56.2 0.8 %select_add_fusion = f32[32,16,128]{2,1,0:T(8,128)} fusion(bf16[32,16,128]{2,1,0:T(8,128)(2,1)S(1)} %collective-permute-done.16, bf16[32,16,128]{2,1,0:T(8,128)(2,1)S(1)} %collective-permute-done.15, f32[32,16,128]{2,1,0:T(8,128)S(1)} %get-tuple-element.21, bf16[32,16,128]{2,1,0:T(8,128)(2,1)S(1)} %collective-permute-done.14, s32[32,128]{1,0:T(8,128)S(1)} %copy-done.3, ...), kind=kLoop, calls=%fused_computation | loop fusion | flops 655360 | bytes 950272 | tf_op jit(solution)/shard_map/add | solution.py:166
  (1 shorter events, 0.0 us)
Async XLA Ops:
  0.0 29.0 %copy-start.3 = (s32[32,128]{1,0:T(8,128)S(1)}, s32[32,128]{1,0:T(8,128)}, u32[]{:S(2)}) copy-start(s32[32,128]{1,0:T(8,128)} %labels.1) | copy-start | bytes 49156
  1.4 21.4 %copy-start.4 = (f32[32,128]{1,0:T(8,128)S(1)}, f32[32,128]{1,0:T(8,128)}, u32[]{:S(2)}) copy-start(f32[32,128]{1,0:T(8,128)} %get-tuple-element.15) | copy-start | bytes 49156
  1.4 7.0 %collective-permute-start.2 = (bf16[2,32,128]{2,1,0:T(8,128)(2,1)}, bf16[2,32,128]{2,1,0:T(8,128)(2,1)S(1)}, u32[]{:S(2)}, u32[]{:S(2)}) collective-permute-start(bf16[2,32,128]{2,1,0:T(8,128)(2,1)} %get-tuple-element.16), channel_id=1, source_target_pairs={{0,24},{4,28},{8,16},{12,20},{16,8},{20,12},{24,0},{28,4},{1,25},{... | collective-permute-start | bytes 49160 | tf_op jit(solution)/shard_map/ppermute | solution.py:138
  6.5 4.8 %collective-permute-start.1 = (bf16[2,32,128]{2,1,0:T(8,128)(2,1)}, bf16[2,32,128]{2,1,0:T(8,128)(2,1)S(1)}, u32[]{:S(2)}, u32[]{:S(2)}) collective-permute-start(bf16[2,32,128]{2,1,0:T(8,128)(2,1)} %get-tuple-element.16), channel_id=1, source_target_pairs={{0,16},{4,20},{8,24},{12,28},{16,0},{20,4},{24,8},{28,12},{1,17},{... | collective-permute-start | bytes 49160 | tf_op jit(solution)/shard_map/ppermute | solution.py:138
  6.5 4.8 %collective-permute-start = (bf16[2,32,128]{2,1,0:T(8,128)(2,1)}, bf16[2,32,128]{2,1,0:T(8,128)(2,1)S(1)}, u32[]{:S(2)}, u32[]{:S(2)}) collective-permute-start(bf16[2,32,128]{2,1,0:T(8,128)(2,1)} %get-tuple-element.16), channel_id=1, source_target_pairs={{0,8},{4,12},{8,0},{12,4},{16,24},{20,28},{24,16},{28,20},{1,9},{5... | collective-permute-start | bytes 49160 | tf_op jit(solution)/shard_map/ppermute | solution.py:138
  12.1 1.3 %collective-permute-start.3 = (bf16[4,2,32,128]{3,2,1,0:T(8,128)(2,1)S(1)}, bf16[4,2,32,128]{3,2,1,0:T(8,128)(2,1)S(1)}, u32[]{:S(2)}, u32[]{:S(2)}) collective-permute-start(bf16[4,2,32,128]{3,2,1,0:T(8,128)(2,1)S(1)} %pad_maximum_fusion.refs_4_), channel_id=1, source_target_pairs={{0,4},{4,0},{8,12},{12,8},{16,20},{20,16},{24,28},{28,24},{1,5},{5... | collective-permute-start | bytes 196616 | tf_op jit(solution)/shard_map/ppermute | solution.py:138
  13.4 2.2 %copy-start = (bf16[128,128,128]{2,1,0:T(8,128)(2,1)S(1)}, bf16[128,128,128]{2,1,0:T(8,128)(2,1)}, u32[]{:S(2)}) copy-start(bf16[128,128,128]{2,1,0:T(8,128)(2,1)} %refs_3_.3) | copy-start | bytes 12582916
  15.6 0.7 %copy-start.1 = (s32[128]{0:T(128)S(1)}, s32[128]{0:T(128)}, u32[]{:S(2)}) copy-start(s32[128]{0:T(128)} %refs_0_.3) | copy-start | bytes 1540
  16.2 0.7 %copy-start.2 = (s32[128]{0:T(128)S(1)}, s32[128]{0:T(128)}, u32[]{:S(2)}) copy-start(s32[128]{0:T(128)} %refs_1_.3) | copy-start | bytes 1540
  19.3 6.0 %collective-permute-start.4 = (bf16[32,16,128]{2,1,0:T(8,128)(2,1)S(1)}, bf16[32,16,128]{2,1,0:T(8,128)(2,1)S(1)}, u32[]{:S(2)}, u32[]{:S(2)}) collective-permute-start(bf16[32,16,128]{2,1,0:T(8,128)(2,1)S(1)} %get-tuple-element.18), channel_id=1, source_target_pairs={{0,1},{1,0},{2,3},{3,2},{4,5},{5,4},{6,7},{7,6},{8,9},{9,8},{10,11... | collective-permute-start | bytes 393224 | tf_op jit(solution)/shard_map/ppermute | solution.py:141
  20.8 8.1 %collective-permute-start.5 = (bf16[32,16,128]{2,1,0:T(8,128)(2,1)S(1)}, bf16[32,16,128]{2,1,0:T(8,128)(2,1)S(1)}, u32[]{:S(2)}, u32[]{:S(2)}) collective-permute-start(bf16[32,16,128]{2,1,0:T(8,128)(2,1)S(1)} %get-tuple-element.19), channel_id=1, source_target_pairs={{0,2},{1,3},{2,0},{3,1},{4,6},{5,7},{6,4},{7,5},{8,10},{9,11},{10,... | collective-permute-start | bytes 393224 | tf_op jit(solution)/shard_map/ppermute | solution.py:141
  22.4 6.6 %collective-permute-start.6 = (bf16[32,16,128]{2,1,0:T(8,128)(2,1)S(1)}, bf16[32,16,128]{2,1,0:T(8,128)(2,1)S(1)}, u32[]{:S(2)}, u32[]{:S(2)}) collective-permute-start(bf16[32,16,128]{2,1,0:T(8,128)(2,1)S(1)} %get-tuple-element.20), channel_id=1, source_target_pairs={{0,3},{1,2},{2,1},{3,0},{4,7},{5,6},{6,5},{7,4},{8,11},{9,10},{10,... | collective-permute-start | bytes 393224 | tf_op jit(solution)/shard_map/ppermute | solution.py:141
  29.1 8.3 %collective-permute-start.9 = (bf16[32,16,128]{2,1,0:T(8,128)(2,1)S(1)}, bf16[32,16,128]{2,1,0:T(8,128)(2,1)S(1)}, u32[]{:S(2)}, u32[]{:S(2)}) collective-permute-start(bf16[32,16,128]{2,1,0:T(8,128)(2,1)S(1)} %fusion.1.refs_4_), channel_id=1, source_target_pairs={{0,24},{4,28},{8,16},{12,20},{16,8},{20,12},{24,0},{28,4},{1,25},{... | collective-permute-start | bytes 393224 | tf_op jit(solution)/shard_map/ppermute | solution.py:138
  30.7 11.6 %collective-permute-start.8 = (bf16[32,16,128]{2,1,0:T(8,128)(2,1)S(1)}, bf16[32,16,128]{2,1,0:T(8,128)(2,1)S(1)}, u32[]{:S(2)}, u32[]{:S(2)}) collective-permute-start(bf16[32,16,128]{2,1,0:T(8,128)(2,1)S(1)} %fusion.1.refs_4_), channel_id=1, source_target_pairs={{0,16},{4,20},{8,24},{12,28},{16,0},{20,4},{24,8},{28,12},{1,17},{... | collective-permute-start | bytes 393224 | tf_op jit(solution)/shard_map/ppermute | solution.py:138
  31.2 11.1 %collective-permute-start.7 = (bf16[32,16,128]{2,1,0:T(8,128)(2,1)S(1)}, bf16[32,16,128]{2,1,0:T(8,128)(2,1)S(1)}, u32[]{:S(2)}, u32[]{:S(2)}) collective-permute-start(bf16[32,16,128]{2,1,0:T(8,128)(2,1)S(1)} %fusion.1.refs_4_), channel_id=1, source_target_pairs={{0,8},{4,12},{8,0},{12,4},{16,24},{20,28},{24,16},{28,20},{1,9},{5... | collective-permute-start | bytes 393224 | tf_op jit(solution)/shard_map/ppermute | solution.py:138
  33.6 9.2 %collective-permute-start.10 = (bf16[32,16,128]{2,1,0:T(8,128)(2,1)S(1)}, bf16[32,16,128]{2,1,0:T(8,128)(2,1)S(1)}, u32[]{:S(2)}, u32[]{:S(2)}) collective-permute-start(bf16[32,16,128]{2,1,0:T(8,128)(2,1)S(1)} %fusion.1.refs_4_), channel_id=1, source_target_pairs={{0,4},{4,0},{8,12},{12,8},{16,20},{20,16},{24,28},{28,24},{1,5},{5... | collective-permute-start | bytes 393224 | tf_op jit(solution)/shard_map/ppermute | solution.py:138
  37.4 5.4 %collective-permute-start.13 = (bf16[32,16,128]{2,1,0:T(8,128)(2,1)S(1)}, bf16[32,16,128]{2,1,0:T(8,128)(2,1)S(1)}, u32[]{:S(2)}, u32[]{:S(2)}) collective-permute-start(bf16[32,16,128]{2,1,0:T(8,128)(2,1)S(1)} %collective-permute-done.9.refs_7_), channel_id=1, source_target_pairs={{0,4},{4,0},{8,12},{12,8},{16,20},{20,16},{24,28},{28,24},{1,5},{5... | collective-permute-start | bytes 393224 | tf_op jit(solution)/shard_map/ppermute | solution.py:138
  42.3 1.3 %collective-permute-start.12 = (bf16[32,16,128]{2,1,0:T(8,128)(2,1)S(1)}, bf16[32,16,128]{2,1,0:T(8,128)(2,1)S(1)}, u32[]{:S(2)}, u32[]{:S(2)}) collective-permute-start(bf16[32,16,128]{2,1,0:T(8,128)(2,1)S(1)} %collective-permute-done.8.refs_6_), channel_id=1, source_target_pairs={{0,4},{4,0},{8,12},{12,8},{16,20},{20,16},{24,28},{28,24},{1,5},{5... | collective-permute-start | bytes 393224 | tf_op jit(solution)/shard_map/ppermute | solution.py:138
  42.3 1.5 %collective-permute-start.11 = (bf16[32,16,128]{2,1,0:T(8,128)(2,1)S(1)}, bf16[32,16,128]{2,1,0:T(8,128)(2,1)S(1)}, u32[]{:S(2)}, u32[]{:S(2)}) collective-permute-start(bf16[32,16,128]{2,1,0:T(8,128)(2,1)S(1)} %collective-permute-done.7.refs_5_), channel_id=1, source_target_pairs={{0,4},{4,0},{8,12},{12,8},{16,20},{20,16},{24,28},{28,24},{1,5},{5... | collective-permute-start | bytes 393224 | tf_op jit(solution)/shard_map/ppermute | solution.py:138
  46.2 6.1 %collective-permute-start.14 = (bf16[32,16,128]{2,1,0:T(8,128)(2,1)S(1)}, bf16[32,16,128]{2,1,0:T(8,128)(2,1)S(1)}, u32[]{:S(2)}, u32[]{:S(2)}) collective-permute-start(bf16[32,16,128]{2,1,0:T(8,128)(2,1)S(1)} %get-tuple-element.22), channel_id=1, source_target_pairs={{0,1},{1,0},{2,3},{3,2},{4,5},{5,4},{6,7},{7,6},{8,9},{9,8},{10,11... | collective-permute-start | bytes 393224 | tf_op jit(solution)/shard_map/ppermute | solution.py:141
  47.9 8.3 %collective-permute-start.15 = (bf16[32,16,128]{2,1,0:T(8,128)(2,1)S(1)}, bf16[32,16,128]{2,1,0:T(8,128)(2,1)S(1)}, u32[]{:S(2)}, u32[]{:S(2)}) collective-permute-start(bf16[32,16,128]{2,1,0:T(8,128)(2,1)S(1)} %get-tuple-element.23), channel_id=1, source_target_pairs={{0,2},{1,3},{2,0},{3,1},{4,6},{5,7},{6,4},{7,5},{8,10},{9,11},{10,... | collective-permute-start | bytes 393224 | tf_op jit(solution)/shard_map/ppermute | solution.py:141
  48.5 7.6 %collective-permute-start.16 = (bf16[32,16,128]{2,1,0:T(8,128)(2,1)S(1)}, bf16[32,16,128]{2,1,0:T(8,128)(2,1)S(1)}, u32[]{:S(2)}, u32[]{:S(2)}) collective-permute-start(bf16[32,16,128]{2,1,0:T(8,128)(2,1)S(1)} %get-tuple-element.24), channel_id=1, source_target_pairs={{0,3},{1,2},{2,1},{3,0},{4,7},{5,6},{6,5},{7,4},{8,11},{9,10},{10,... | collective-permute-start | bytes 393224 | tf_op jit(solution)/shard_map/ppermute | solution.py:141

commit v3 on v2

--- a/solution.py
+++ b/solution.py
@@ -22,26 +22,18 @@
     return lax.div(value, size)
 
 
-def prepare(degree, labels, scale_ref, own_ref):
-    scale = 1.0 / jnp.sqrt(degree[...].astype(jnp.float32))
-    scale_ref[...] = scale
-    own_ref[0] = labels[...].astype(jnp.float32).astype(jnp.bfloat16)
-    own_ref[1] = scale.astype(jnp.bfloat16)
-
-
 def spread(seeded, nrow, ncol, blk, *refs):
     nz = nrow // 2
-    tables_hbm, tiles_hbm, refs = refs[:3], refs[3], refs[4:]
-    nfields = 2 if seeded else nrow
-    fields, refs = refs[:nfields], refs[nfields:]
+    tables_hbm, tiles_hbm, counts, refs = refs[:2], refs[2], refs[3], refs[4:]
+    fields, refs = refs[:nrow], refs[nrow:]
     outs, refs = refs[:ncol], refs[ncol:]
-    tiles, total, picks, rows, cols, counts, tile_sem, table_sem = refs
+    tiles, total, picks, rows, cols, tile_sem, table_sem = refs
     nt = tiles.shape[0]
     row_pos, col_pos = lax.axis_index("row"), lax.axis_index("col")
 
     tables = [
         pltpu.make_async_copy(source, target, table_sem.at[i])
-        for i, (source, target) in enumerate(zip(tables_hbm, (rows, cols, counts)))
+        for i, (source, target) in enumerate(zip(tables_hbm, (rows, cols)))
     ]
     for c in tables:
         c.start()
@@ -54,10 +46,9 @@
         tile_copy(i).start()
     total[...] = jnp.zeros_like(total)
     if seeded:
-        for half, f in enumerate(fields):
-            for i in range(nz):
-                for kind in range(2):
-                    picks[kind, pl.ds((half * nz + i) * blk, blk), :] = f[i, kind].astype(jnp.float32)
+        for i, f in enumerate(fields):
+            for kind in range(2):
+                picks[kind, pl.ds(i * blk, blk), :] = f[kind].astype(jnp.float32)
     else:
         for i, f in enumerate(fields):
             picks[pl.ds(i * blk, blk)] = f[...]
@@ -113,21 +104,21 @@
         functools.partial(spread, seeded, nrow, ncol, blk),
         out_shape=[jax.ShapeDtypeStruct(shape, jnp.float32)]
         + [jax.ShapeDtypeStruct(shape, jnp.bfloat16)] * (ncol - 1),
-        in_specs=[pl.BlockSpec(memory_space=HBM)] * 4 + [pl.BlockSpec(memory_space=VMEM)] * len(fields),
+        in_specs=[pl.BlockSpec(memory_space=HBM)] * 3 + [pl.BlockSpec(memory_space=pltpu.SMEM)] + [pl.BlockSpec(memory_space=VMEM)] * len(fields),
         out_specs=[pl.BlockSpec(memory_space=VMEM)] * ncol,
         scratch_shapes=[
             pltpu.VMEM(tiles.shape, tiles.dtype),
             pltpu.VMEM((blk * ncol + 1, QC, 128), jnp.float32),
             picks,
-            *(pltpu.SMEM(x.shape, x.dtype) for x in tables),
+            *(pltpu.SMEM(x.shape, x.dtype) for x in tables[:2]),
             pltpu.SemaphoreType.DMA((nt // COPY,)),
-            pltpu.SemaphoreType.DMA((len(tables),)),
+            pltpu.SemaphoreType.DMA((2,)),
         ],
         compiler_params=pltpu.CompilerParams(vmem_limit_bytes=24 << 20),
         cost_estimate=pl.CostEstimate(
             flops=2 * nt * QC * 128 * 128, bytes_accessed=tiles.size * 2 + slots * QC * 256, transcendentals=0
         ),
-    )(*tables, tiles, *fields)
+    )(*(pltpu.with_memory_space_constraint(x, HBM) for x in (*tables[:2], tiles)), tables[2], *fields)
 
 
 def local(nrow, ncol, tiles, tile_rows, tile_cols, tile_count, degree, labels):
@@ -140,25 +131,17 @@
     def from_col(x, k):
         return lax.ppermute(x, "col", [(i, i ^ k) for i in range(ncol)])
 
-    scale, seeds = pl.pallas_call(
-        prepare,
-        out_shape=[
-            jax.ShapeDtypeStruct((blk, 128), jnp.float32),
-            jax.ShapeDtypeStruct((2, blk, 128), jnp.bfloat16),
-        ],
-        in_specs=[pl.BlockSpec(memory_space=VMEM)] * 2,
-        out_specs=[pl.BlockSpec(memory_space=VMEM)] * 2,
-    )(degree, labels)
+    scale = 1.0 / jnp.sqrt(degree.astype(jnp.float32))
+    seeds = jnp.stack([labels.astype(jnp.bfloat16), scale.astype(jnp.bfloat16)])
     qidx = jnp.arange(QC, dtype=jnp.int32)
     prior = (labels[:, None, :] == qidx[None, :, None]).astype(jnp.float32)
     for step in range(ITERS):
         if step == 0:
-            near = jnp.stack([seeds] + [from_row(seeds, 2 * m) for m in range(1, nz)])
-            fields = [near, from_row(near, 1)]
+            own = seeds
         else:
             own = (field * scale[:, None, :]).astype(jnp.bfloat16)
-            near = [own] + [from_row(own, 2 * m) for m in range(1, nz)]
-            fields = near + [from_row(x, 1) for x in near]
+        near = [own] + [from_row(own, 2 * m) for m in range(1, nz)]
+        fields = near + [from_row(x, 1) for x in near]
         outs = spread_call(step == 0, nrow, ncol, blk, (tile_rows, tile_cols, tile_count), tiles, fields)
         summed = outs[0]
         for k in range(1, ncol):

time: 57.3 us -> 54.7 us (0.955)
  local copies, waits for them, and re-layouts: 3.5 us -> 0.01 us
  waiting for transfers between devices: 27.1 us -> 26.2 us
  other arithmetic: 1.65 us -> 2.43 us
  starting transfers between devices: 17.8 us -> 18.4 us
    unnamed x10 -> x2, local copies, waits for them, and re-layouts: 3.5 us -> 0.01 us
    pallas_call x2, Pallas kernels: 4.81 us -> 6.68 us  [spread_call(): pl.pallas_call(functools.partial(spread, seeded, nrow, ncol, blk), out_sh...]
    pallas_call x1 -> x0, Pallas kernels: 1.41 us -> none  [local(): pl.pallas_call(prepare, out_shape=[jax.ShapeDtypeStruct((blk, 128), jnp.f...]
    ppermute x11 -> x14, waiting for transfers between devices: 14.5 us -> 13.8 us  [from_row(): return lax.ppermute(x, 'row', [(i, i ^ d) for i in range(nrow)])]
    mul x1, other arithmetic: 0.01 us -> 0.72 us  [local(): field = 0.8 * scale[:, None, :] * summed + 0.2 * prior]
    ppermute x11 -> x14, starting transfers between devices: 10.7 us -> 11.2 us  [from_row(): return lax.ppermute(x, 'row', [(i, i ^ d) for i in range(nrow)])]
  transfers between devices with their start and end apart: 17 -> 20, of which waited for: 11 -> 12; matrix products, arithmetic and copies ran while one was open for 0% -> 0% of each run, Pallas kernels for 0% -> 0%
where the time goes in v3:
time: 54.7 us; the launch traced here: 54.4 us
  waiting for transfers between devices  26.2 us (48%)
  starting transfers between devices  18.4 us (34%)
  Pallas kernels  6.68 us (12%)
  other arithmetic  2.43 us (4%)
  between operations  0.72 us (1%)
    ppermute x14, waiting for transfers between devices, from_row(): return lax.ppermute(x, 'row', [(i, i ^ d) for i in range(nrow)])  13.8 us
    ppermute x6, waiting for transfers between devices, from_col(): return lax.ppermute(x, 'col', [(i, i ^ k) for i in range(ncol)])  12.4 us
    ppermute x14, starting transfers between devices, from_row(): return lax.ppermute(x, 'row', [(i, i ^ d) for i in range(nrow)])  11.2 us
    ppermute x6, starting transfers between devices, from_col(): return lax.ppermute(x, 'col', [(i, i ^ k) for i in range(ncol)])  7.14 us
    pallas_call x2, Pallas kernels, spread_call(): pl.pallas_call(functools.partial(spread, seeded, nrow, ncol, blk), out_sh...  6.68 us
  transfers between devices with their start and end apart: 20, of which 12 were waited for; matrix products, arithmetic and copies ran while one was open for 0% of the time, Pallas kernels for 0%

profile of v3, /device:TPU:0, one launch (start us, length us, event | category | flops | bytes accessed | tf_op | source)
XLA Modules:
  0.0 54.4 jit_solution(5032116585036526085)
XLA Ops:
  0.0 0.0 copy-start
  0.0 0.8 %convert_bitcast_fusion.1 = bf16[1,32,128]{2,1,0:T(8,128)(2,1)S(1)} fusion(s32[32,128]{1,0:T(8,128)} %param.11), kind=kLoop, calls=%fused_computation.8 | loop fusion | flops 4096 | bytes 24576 | tf_op jit(solution)/shard_map/stack | solution.py:135
  0.8 0.7 %broadcast_multiply_fusion = (f32[32,128]{1,0:T(8,128)S(1)}, bf16[1,32,128]{2,1,0:T(8,128)(2,1)S(1)}, f32[32,128]{1,0:T(8,128)S(1)}) fusion(s32[32,128]{1,0:T(8,128)} %param.10), kind=kLoop, calls=%fused_computation.9 | loop fusion | flops 12288 | bytes 57344 | tf_op jit(solution)/shard_map/mul | solution.py:149
  1.5 5.1 %collective-permute-start.2 = (bf16[2,32,128]{2,1,0:T(8,128)(2,1)S(1)}, bf16[2,32,128]{2,1,0:T(8,128)(2,1)S(1)}, u32[]{:S(2)}, u32[]{:S(2)}) collective-permute-start(bf16[2,32,128]{2,1,0:T(8,128)(2,1)S(1)} %pad_maximum_fusion.refs_4_), channel_id=1, source_target_pairs={{0,24},{4,28},{8,16},{12,20},{16,8},{20,12},{24,0},{28,4},{1,25},{... | collective-permute-start | bytes 49160 | tf_op jit(solution)/shard_map/ppermute | solution.py:129
  6.6 0.0 collective-permute-start.1
  6.6 0.6 %collective-permute-start = (bf16[2,32,128]{2,1,0:T(8,128)(2,1)S(1)}, bf16[2,32,128]{2,1,0:T(8,128)(2,1)S(1)}, u32[]{:S(2)}, u32[]{:S(2)}) collective-permute-start(bf16[2,32,128]{2,1,0:T(8,128)(2,1)S(1)} %pad_maximum_fusion.refs_4_), channel_id=1, source_target_pairs={{0,8},{4,12},{8,0},{12,4},{16,24},{20,28},{24,16},{28,20},{1,9},{5... | collective-permute-start | bytes 49160 | tf_op jit(solution)/shard_map/ppermute | solution.py:129
  7.3 0.0 collective-permute-start.3
  7.3 1.1 %collective-permute-done.2.refs_7_ = bf16[2,32,128]{2,1,0:T(8,128)(2,1)S(1)} collective-permute-done((bf16[2,32,128]{2,1,0:T(8,128)(2,1)S(1)}, bf16[2,32,128]{2,1,0:T(8,128)(2,1)S(1)}, u32[]{:S(2)}, u32[]{:S(2)}) %collective-permute-start.2) | collective-permute-done | bytes 16416 | tf_op jit(solution)/shard_map/ppermute | solution.py:129
  8.4 0.0 collective-permute-start.6
  8.4 2.9 %collective-permute-done.1.refs_6_ = bf16[2,32,128]{2,1,0:T(8,128)(2,1)S(1)} collective-permute-done((bf16[2,32,128]{2,1,0:T(8,128)(2,1)S(1)}, bf16[2,32,128]{2,1,0:T(8,128)(2,1)S(1)}, u32[]{:S(2)}, u32[]{:S(2)}) %collective-permute-start.1) | collective-permute-done | bytes 16416 | tf_op jit(solution)/shard_map/ppermute | solution.py:129
  11.3 0.0 collective-permute-start.5
  11.3 0.0 collective-permute-done.refs_5_
  11.3 0.5 collective-permute-start.4
  12.4 0.0 collective-permute-done.3.refs_8_
  12.5 0.0 collective-permute-done.6.refs_11_
  12.5 0.0 collective-permute-done.5.refs_10_
  12.5 0.2 collective-permute-done.4.refs_9_
  12.6 3.3 %shard_map.64 = (f32[32,16,128]{2,1,0:T(8,128)S(1)}, bf16[32,16,128]{2,1,0:T(8,128)(2,1)S(1)}, bf16[32,16,128]{2,1,0:T(8,128)(2,1)S(1)}, bf16[32,16,128]{2,1,0:T(8,128)(2,1)S(1)}) custom-call(s32[128]{0:T(128)} %refs_0_.3, s32[128]{0:T(128)} %refs_1_.3, bf16[128,128,128]{2,1,0:T(8,128)(2,1)} %refs_2_.3, s32[1]{0:T(128)S(6)} %copy.7.refs_3_, ...), custom_call_target="tpu_custom_call" | custom-call | flops 67108864 | bytes 5242880 | tf_op jit(solution)/shard_map/pallas_call | solution.py:103
  16.0 1.6 %collective-permute-start.7 = (bf16[32,16,128]{2,1,0:T(8,128)(2,1)S(1)}, bf16[32,16,128]{2,1,0:T(8,128)(2,1)S(1)}, u32[]{:S(2)}, u32[]{:S(2)}) collective-permute-start(bf16[32,16,128]{2,1,0:T(8,128)(2,1)S(1)} %get-tuple-element.14), channel_id=1, source_target_pairs={{0,1},{1,0},{2,3},{3,2},{4,5},{5,4},{6,7},{7,6},{8,9},{9,8},{10,11... | collective-permute-start | bytes 393224 | tf_op jit(solution)/shard_map/ppermute | solution.py:132
  17.6 1.5 %collective-permute-start.8 = (bf16[32,16,128]{2,1,0:T(8,128)(2,1)S(1)}, bf16[32,16,128]{2,1,0:T(8,128)(2,1)S(1)}, u32[]{:S(2)}, u32[]{:S(2)}) collective-permute-start(bf16[32,16,128]{2,1,0:T(8,128)(2,1)S(1)} %get-tuple-element.15), channel_id=1, source_target_pairs={{0,2},{1,3},{2,0},{3,1},{4,6},{5,7},{6,4},{7,5},{8,10},{9,11},{10,... | collective-permute-start | bytes 393224 | tf_op jit(solution)/shard_map/ppermute | solution.py:132
  19.1 0.5 collective-permute-start.9
  19.6 2.6 %collective-permute-done.7 = bf16[32,16,128]{2,1,0:T(8,128)(2,1)S(1)} collective-permute-done((bf16[32,16,128]{2,1,0:T(8,128)(2,1)S(1)}, bf16[32,16,128]{2,1,0:T(8,128)(2,1)S(1)}, u32[]{:S(2)}, u32[]{:S(2)}) %collective-permute-start.7) | collective-permute-done | bytes 131104 | tf_op jit(solution)/shard_map/ppermute | solution.py:132
  22.1 3.7 %collective-permute-done.8 = bf16[32,16,128]{2,1,0:T(8,128)(2,1)S(1)} collective-permute-done((bf16[32,16,128]{2,1,0:T(8,128)(2,1)S(1)}, bf16[32,16,128]{2,1,0:T(8,128)(2,1)S(1)}, u32[]{:S(2)}, u32[]{:S(2)}) %collective-permute-start.8) | collective-permute-done | bytes 131104 | tf_op jit(solution)/shard_map/ppermute | solution.py:132
  25.9 0.0 collective-permute-done.9
  25.9 0.0 copy-done
  25.9 0.1 fusion.1.refs_4_
  26.0 1.1 %collective-permute-start.12 = (bf16[32,16,128]{2,1,0:T(8,128)(2,1)S(1)}, bf16[32,16,128]{2,1,0:T(8,128)(2,1)S(1)}, u32[]{:S(2)}, u32[]{:S(2)}) collective-permute-start(bf16[32,16,128]{2,1,0:T(8,128)(2,1)S(1)} %fusion.1.refs_4_), channel_id=1, source_target_pairs={{0,24},{4,28},{8,16},{12,20},{16,8},{20,12},{24,0},{28,4},{1,25},{... | collective-permute-start | bytes 393224 | tf_op jit(solution)/shard_map/ppermute | solution.py:129
  27.1 0.7 %collective-permute-start.11 = (bf16[32,16,128]{2,1,0:T(8,128)(2,1)S(1)}, bf16[32,16,128]{2,1,0:T(8,128)(2,1)S(1)}, u32[]{:S(2)}, u32[]{:S(2)}) collective-permute-start(bf16[32,16,128]{2,1,0:T(8,128)(2,1)S(1)} %fusion.1.refs_4_), channel_id=1, source_target_pairs={{0,16},{4,20},{8,24},{12,28},{16,0},{20,4},{24,8},{28,12},{1,17},{... | collective-permute-start | bytes 393224 | tf_op jit(solution)/shard_map/ppermute | solution.py:129
  27.8 2.7 %collective-permute-start.10 = (bf16[32,16,128]{2,1,0:T(8,128)(2,1)S(1)}, bf16[32,16,128]{2,1,0:T(8,128)(2,1)S(1)}, u32[]{:S(2)}, u32[]{:S(2)}) collective-permute-start(bf16[32,16,128]{2,1,0:T(8,128)(2,1)S(1)} %fusion.1.refs_4_), channel_id=1, source_target_pairs={{0,8},{4,12},{8,0},{12,4},{16,24},{20,28},{24,16},{28,20},{1,9},{5... | collective-permute-start | bytes 393224 | tf_op jit(solution)/shard_map/ppermute | solution.py:129
  30.5 0.0 collective-permute-start.13
  30.5 3.8 %collective-permute-done.12.refs_7_ = bf16[32,16,128]{2,1,0:T(8,128)(2,1)S(1)} collective-permute-done((bf16[32,16,128]{2,1,0:T(8,128)(2,1)S(1)}, bf16[32,16,128]{2,1,0:T(8,128)(2,1)S(1)}, u32[]{:S(2)}, u32[]{:S(2)}) %collective-permute-start.12) | collective-permute-done | bytes 131104 | tf_op jit(solution)/shard_map/ppermute | solution.py:129
  34.3 0.0 collective-permute-start.16
  34.3 4.8 %collective-permute-done.11.refs_6_ = bf16[32,16,128]{2,1,0:T(8,128)(2,1)S(1)} collective-permute-done((bf16[32,16,128]{2,1,0:T(8,128)(2,1)S(1)}, bf16[32,16,128]{2,1,0:T(8,128)(2,1)S(1)}, u32[]{:S(2)}, u32[]{:S(2)}) %collective-permute-start.11) | collective-permute-done | bytes 131104 | tf_op jit(solution)/shard_map/ppermute | solution.py:129
  39.1 0.0 collective-permute-start.15
  39.1 0.0 collective-permute-done.10.refs_5_
  39.1 0.5 collective-permute-start.14
  39.6 0.0 collective-permute-done.13.refs_8_
  39.6 0.0 collective-permute-done.16.refs_11_
  39.6 0.8 %collective-permute-done.15.refs_10_ = bf16[32,16,128]{2,1,0:T(8,128)(2,1)S(1)} collective-permute-done((bf16[32,16,128]{2,1,0:T(8,128)(2,1)S(1)}, bf16[32,16,128]{2,1,0:T(8,128)(2,1)S(1)}, u32[]{:S(2)}, u32[]{:S(2)}) %collective-permute-start.15) | collective-permute-done | bytes 131104 | tf_op jit(solution)/shard_map/ppermute | solution.py:129
  40.4 0.2 collective-permute-done.14.refs_9_
  40.6 3.3 %shard_map.65 = (f32[32,16,128]{2,1,0:T(8,128)S(1)}, bf16[32,16,128]{2,1,0:T(8,128)(2,1)S(1)}, bf16[32,16,128]{2,1,0:T(8,128)(2,1)S(1)}, bf16[32,16,128]{2,1,0:T(8,128)(2,1)S(1)}) custom-call(s32[128]{0:T(128)} %refs_0_.3, s32[128]{0:T(128)} %refs_1_.3, bf16[128,128,128]{2,1,0:T(8,128)(2,1)} %refs_2_.3, s32[1]{0:T(128)S(6)} %copy.7.refs_3_, ...), custom_call_target="tpu_custom_call" | custom-call | flops 67108864 | bytes 5242880 | tf_op jit(solution)/shard_map/pallas_call | solution.py:103
  44.0 1.4 %collective-permute-start.17 = (bf16[32,16,128]{2,1,0:T(8,128)(2,1)S(1)}, bf16[32,16,128]{2,1,0:T(8,128)(2,1)S(1)}, u32[]{:S(2)}, u32[]{:S(2)}) collective-permute-start(bf16[32,16,128]{2,1,0:T(8,128)(2,1)S(1)} %get-tuple-element.18), channel_id=1, source_target_pairs={{0,1},{1,0},{2,3},{3,2},{4,5},{5,4},{6,7},{7,6},{8,9},{9,8},{10,11... | collective-permute-start | bytes 393224 | tf_op jit(solution)/shard_map/ppermute | solution.py:132
  45.4 0.7 %collective-permute-start.18 = (bf16[32,16,128]{2,1,0:T(8,128)(2,1)S(1)}, bf16[32,16,128]{2,1,0:T(8,128)(2,1)S(1)}, u32[]{:S(2)}, u32[]{:S(2)}) collective-permute-start(bf16[32,16,128]{2,1,0:T(8,128)(2,1)S(1)} %get-tuple-element.19), channel_id=1, source_target_pairs={{0,2},{1,3},{2,0},{3,1},{4,6},{5,7},{6,4},{7,5},{8,10},{9,11},{10,... | collective-permute-start | bytes 393224 | tf_op jit(solution)/shard_map/ppermute | solution.py:132
  46.1 1.4 %collective-permute-start.19 = (bf16[32,16,128]{2,1,0:T(8,128)(2,1)S(1)}, bf16[32,16,128]{2,1,0:T(8,128)(2,1)S(1)}, u32[]{:S(2)}, u32[]{:S(2)}) collective-permute-start(bf16[32,16,128]{2,1,0:T(8,128)(2,1)S(1)} %get-tuple-element.20), channel_id=1, source_target_pairs={{0,3},{1,2},{2,1},{3,0},{4,7},{5,6},{6,5},{7,4},{8,11},{9,10},{10,... | collective-permute-start | bytes 393224 | tf_op jit(solution)/shard_map/ppermute | solution.py:132
  47.5 2.8 %collective-permute-done.17 = bf16[32,16,128]{2,1,0:T(8,128)(2,1)S(1)} collective-permute-done((bf16[32,16,128]{2,1,0:T(8,128)(2,1)S(1)}, bf16[32,16,128]{2,1,0:T(8,128)(2,1)S(1)}, u32[]{:S(2)}, u32[]{:S(2)}) %collective-permute-start.17) | collective-permute-done | bytes 131104 | tf_op jit(solution)/shard_map/ppermute | solution.py:132
  50.3 1.6 %collective-permute-done.18 = bf16[32,16,128]{2,1,0:T(8,128)(2,1)S(1)} collective-permute-done((bf16[32,16,128]{2,1,0:T(8,128)(2,1)S(1)}, bf16[32,16,128]{2,1,0:T(8,128)(2,1)S(1)}, u32[]{:S(2)}, u32[]{:S(2)}) %collective-permute-start.18) | collective-permute-done | bytes 131104 | tf_op jit(solution)/shard_map/ppermute | solution.py:132
  51.9 1.7 %collective-permute-done.19 = bf16[32,16,128]{2,1,0:T(8,128)(2,1)S(1)} collective-permute-done((bf16[32,16,128]{2,1,0:T(8,128)(2,1)S(1)}, bf16[32,16,128]{2,1,0:T(8,128)(2,1)S(1)}, u32[]{:S(2)}, u32[]{:S(2)}) %collective-permute-start.19) | collective-permute-done | bytes 131104 | tf_op jit(solution)/shard_map/ppermute | solution.py:132
  53.6 0.8 %select_add_fusion = f32[32,16,128]{2,1,0:T(8,128)} fusion(bf16[32,16,128]{2,1,0:T(8,128)(2,1)S(1)} %collective-permute-done.19, bf16[32,16,128]{2,1,0:T(8,128)(2,1)S(1)} %collective-permute-done.18, f32[32,16,128]{2,1,0:T(8,128)S(1)} %get-tuple-element.17, bf16[32,16,128]{2,1,0:T(8,128)(2,1)S(1)} %collective-permute-done.17, s32[32,128]{1,0:T(8,128)S(1)} %copy-done, ...), kind=kLoop, calls=%fused_computation | loop fusion | flops 655360 | bytes 950272 | tf_op jit(solution)/shard_map/add | solution.py:149
  (1 shorter events, 0.0 us)
Async XLA Ops:
  0.0 25.9 %copy-start = (s32[32,128]{1,0:T(8,128)S(1)}, s32[32,128]{1,0:T(8,128)}, u32[]{:S(2)}) copy-start(s32[32,128]{1,0:T(8,128)} %param.11) | copy-start | bytes 49156
  1.5 6.8 %collective-permute-start.2 = (bf16[2,32,128]{2,1,0:T(8,128)(2,1)S(1)}, bf16[2,32,128]{2,1,0:T(8,128)(2,1)S(1)}, u32[]{:S(2)}, u32[]{:S(2)}) collective-permute-start(bf16[2,32,128]{2,1,0:T(8,128)(2,1)S(1)} %pad_maximum_fusion.refs_4_), channel_id=1, source_target_pairs={{0,24},{4,28},{8,16},{12,20},{16,8},{20,12},{24,0},{28,4},{1,25},{... | collective-permute-start | bytes 49160 | tf_op jit(solution)/shard_map/ppermute | solution.py:129
  6.6 4.6 %collective-permute-start.1 = (bf16[2,32,128]{2,1,0:T(8,128)(2,1)S(1)}, bf16[2,32,128]{2,1,0:T(8,128)(2,1)S(1)}, u32[]{:S(2)}, u32[]{:S(2)}) collective-permute-start(bf16[2,32,128]{2,1,0:T(8,128)(2,1)S(1)} %pad_maximum_fusion.refs_4_), channel_id=1, source_target_pairs={{0,16},{4,20},{8,24},{12,28},{16,0},{20,4},{24,8},{28,12},{1,17},{... | collective-permute-start | bytes 49160 | tf_op jit(solution)/shard_map/ppermute | solution.py:129
  6.6 4.6 %collective-permute-start = (bf16[2,32,128]{2,1,0:T(8,128)(2,1)S(1)}, bf16[2,32,128]{2,1,0:T(8,128)(2,1)S(1)}, u32[]{:S(2)}, u32[]{:S(2)}) collective-permute-start(bf16[2,32,128]{2,1,0:T(8,128)(2,1)S(1)} %pad_maximum_fusion.refs_4_), channel_id=1, source_target_pairs={{0,8},{4,12},{8,0},{12,4},{16,24},{20,28},{24,16},{28,20},{1,9},{5... | collective-permute-start | bytes 49160 | tf_op jit(solution)/shard_map/ppermute | solution.py:129
  7.3 5.2 %collective-permute-start.3 = (bf16[2,32,128]{2,1,0:T(8,128)(2,1)S(1)}, bf16[2,32,128]{2,1,0:T(8,128)(2,1)S(1)}, u32[]{:S(2)}, u32[]{:S(2)}) collective-permute-start(bf16[2,32,128]{2,1,0:T(8,128)(2,1)S(1)} %pad_maximum_fusion.refs_4_), channel_id=1, source_target_pairs={{0,4},{4,0},{8,12},{12,8},{16,20},{20,16},{24,28},{28,24},{1,5},{5... | collective-permute-start | bytes 49160 | tf_op jit(solution)/shard_map/ppermute | solution.py:129
  8.4 4.1 %collective-permute-start.6 = (bf16[2,32,128]{2,1,0:T(8,128)(2,1)S(1)}, bf16[2,32,128]{2,1,0:T(8,128)(2,1)S(1)}, u32[]{:S(2)}, u32[]{:S(2)}) collective-permute-start(bf16[2,32,128]{2,1,0:T(8,128)(2,1)S(1)} %collective-permute-done.2.refs_7_), channel_id=1, source_target_pairs={{0,4},{4,0},{8,12},{12,8},{16,20},{20,16},{24,28},{28,24},{1,5},{5... | collective-permute-start | bytes 49160 | tf_op jit(solution)/shard_map/ppermute | solution.py:129
  11.3 1.2 %collective-permute-start.5 = (bf16[2,32,128]{2,1,0:T(8,128)(2,1)S(1)}, bf16[2,32,128]{2,1,0:T(8,128)(2,1)S(1)}, u32[]{:S(2)}, u32[]{:S(2)}) collective-permute-start(bf16[2,32,128]{2,1,0:T(8,128)(2,1)S(1)} %collective-permute-done.1.refs_6_), channel_id=1, source_target_pairs={{0,4},{4,0},{8,12},{12,8},{16,20},{20,16},{24,28},{28,24},{1,5},{5... | collective-permute-start | bytes 49160 | tf_op jit(solution)/shard_map/ppermute | solution.py:129
  11.3 1.3 %collective-permute-start.4 = (bf16[2,32,128]{2,1,0:T(8,128)(2,1)S(1)}, bf16[2,32,128]{2,1,0:T(8,128)(2,1)S(1)}, u32[]{:S(2)}, u32[]{:S(2)}) collective-permute-start(bf16[2,32,128]{2,1,0:T(8,128)(2,1)S(1)} %collective-permute-done.refs_5_), channel_id=1, source_target_pairs={{0,4},{4,0},{8,12},{12,8},{16,20},{20,16},{24,28},{28,24},{1,5},{5... | collective-permute-start | bytes 49160 | tf_op jit(solution)/shard_map/ppermute | solution.py:129
  16.0 6.2 %collective-permute-start.7 = (bf16[32,16,128]{2,1,0:T(8,128)(2,1)S(1)}, bf16[32,16,128]{2,1,0:T(8,128)(2,1)S(1)}, u32[]{:S(2)}, u32[]{:S(2)}) collective-permute-start(bf16[32,16,128]{2,1,0:T(8,128)(2,1)S(1)} %get-tuple-element.14), channel_id=1, source_target_pairs={{0,1},{1,0},{2,3},{3,2},{4,5},{5,4},{6,7},{7,6},{8,9},{9,8},{10,11... | collective-permute-start | bytes 393224 | tf_op jit(solution)/shard_map/ppermute | solution.py:132
  17.6 8.3 %collective-permute-start.8 = (bf16[32,16,128]{2,1,0:T(8,128)(2,1)S(1)}, bf16[32,16,128]{2,1,0:T(8,128)(2,1)S(1)}, u32[]{:S(2)}, u32[]{:S(2)}) collective-permute-start(bf16[32,16,128]{2,1,0:T(8,128)(2,1)S(1)} %get-tuple-element.15), channel_id=1, source_target_pairs={{0,2},{1,3},{2,0},{3,1},{4,6},{5,7},{6,4},{7,5},{8,10},{9,11},{10,... | collective-permute-start | bytes 393224 | tf_op jit(solution)/shard_map/ppermute | solution.py:132
  19.1 6.8 %collective-permute-start.9 = (bf16[32,16,128]{2,1,0:T(8,128)(2,1)S(1)}, bf16[32,16,128]{2,1,0:T(8,128)(2,1)S(1)}, u32[]{:S(2)}, u32[]{:S(2)}) collective-permute-start(bf16[32,16,128]{2,1,0:T(8,128)(2,1)S(1)} %get-tuple-element.16), channel_id=1, source_target_pairs={{0,3},{1,2},{2,1},{3,0},{4,7},{5,6},{6,5},{7,4},{8,11},{9,10},{10,... | collective-permute-start | bytes 393224 | tf_op jit(solution)/shard_map/ppermute | solution.py:132
  26.0 8.3 %collective-permute-start.12 = (bf16[32,16,128]{2,1,0:T(8,128)(2,1)S(1)}, bf16[32,16,128]{2,1,0:T(8,128)(2,1)S(1)}, u32[]{:S(2)}, u32[]{:S(2)}) collective-permute-start(bf16[32,16,128]{2,1,0:T(8,128)(2,1)S(1)} %fusion.1.refs_4_), channel_id=1, source_target_pairs={{0,24},{4,28},{8,16},{12,20},{16,8},{20,12},{24,0},{28,4},{1,25},{... | collective-permute-start | bytes 393224 | tf_op jit(solution)/shard_map/ppermute | solution.py:129
  27.1 12.0 %collective-permute-start.11 = (bf16[32,16,128]{2,1,0:T(8,128)(2,1)S(1)}, bf16[32,16,128]{2,1,0:T(8,128)(2,1)S(1)}, u32[]{:S(2)}, u32[]{:S(2)}) collective-permute-start(bf16[32,16,128]{2,1,0:T(8,128)(2,1)S(1)} %fusion.1.refs_4_), channel_id=1, source_target_pairs={{0,16},{4,20},{8,24},{12,28},{16,0},{20,4},{24,8},{28,12},{1,17},{... | collective-permute-start | bytes 393224 | tf_op jit(solution)/shard_map/ppermute | solution.py:129
  27.8 11.3 %collective-permute-start.10 = (bf16[32,16,128]{2,1,0:T(8,128)(2,1)S(1)}, bf16[32,16,128]{2,1,0:T(8,128)(2,1)S(1)}, u32[]{:S(2)}, u32[]{:S(2)}) collective-permute-start(bf16[32,16,128]{2,1,0:T(8,128)(2,1)S(1)} %fusion.1.refs_4_), channel_id=1, source_target_pairs={{0,8},{4,12},{8,0},{12,4},{16,24},{20,28},{24,16},{28,20},{1,9},{5... | collective-permute-start | bytes 393224 | tf_op jit(solution)/shard_map/ppermute | solution.py:129
  30.5 9.1 %collective-permute-start.13 = (bf16[32,16,128]{2,1,0:T(8,128)(2,1)S(1)}, bf16[32,16,128]{2,1,0:T(8,128)(2,1)S(1)}, u32[]{:S(2)}, u32[]{:S(2)}) collective-permute-start(bf16[32,16,128]{2,1,0:T(8,128)(2,1)S(1)} %fusion.1.refs_4_), channel_id=1, source_target_pairs={{0,4},{4,0},{8,12},{12,8},{16,20},{20,16},{24,28},{28,24},{1,5},{5... | collective-permute-start | bytes 393224 | tf_op jit(solution)/shard_map/ppermute | solution.py:129
  34.3 5.3 %collective-permute-start.16 = (bf16[32,16,128]{2,1,0:T(8,128)(2,1)S(1)}, bf16[32,16,128]{2,1,0:T(8,128)(2,1)S(1)}, u32[]{:S(2)}, u32[]{:S(2)}) collective-permute-start(bf16[32,16,128]{2,1,0:T(8,128)(2,1)S(1)} %collective-permute-done.12.refs_7_), channel_id=1, source_target_pairs={{0,4},{4,0},{8,12},{12,8},{16,20},{20,16},{24,28},{28,24},{1,5},{5... | collective-permute-start | bytes 393224 | tf_op jit(solution)/shard_map/ppermute | solution.py:129
  39.1 1.3 %collective-permute-start.15 = (bf16[32,16,128]{2,1,0:T(8,128)(2,1)S(1)}, bf16[32,16,128]{2,1,0:T(8,128)(2,1)S(1)}, u32[]{:S(2)}, u32[]{:S(2)}) collective-permute-start(bf16[32,16,128]{2,1,0:T(8,128)(2,1)S(1)} %collective-permute-done.11.refs_6_), channel_id=1, source_target_pairs={{0,4},{4,0},{8,12},{12,8},{16,20},{20,16},{24,28},{28,24},{1,5},{5... | collective-permute-start | bytes 393224 | tf_op jit(solution)/shard_map/ppermute | solution.py:129
  39.1 1.5 %collective-permute-start.14 = (bf16[32,16,128]{2,1,0:T(8,128)(2,1)S(1)}, bf16[32,16,128]{2,1,0:T(8,128)(2,1)S(1)}, u32[]{:S(2)}, u32[]{:S(2)}) collective-permute-start(bf16[32,16,128]{2,1,0:T(8,128)(2,1)S(1)} %collective-permute-done.10.refs_5_), channel_id=1, source_target_pairs={{0,4},{4,0},{8,12},{12,8},{16,20},{20,16},{24,28},{28,24},{1,5},{5... | collective-permute-start | bytes 393224 | tf_op jit(solution)/shard_map/ppermute | solution.py:129
  44.0 6.4 %collective-permute-start.17 = (bf16[32,16,128]{2,1,0:T(8,128)(2,1)S(1)}, bf16[32,16,128]{2,1,0:T(8,128)(2,1)S(1)}, u32[]{:S(2)}, u32[]{:S(2)}) collective-permute-start(bf16[32,16,128]{2,1,0:T(8,128)(2,1)S(1)} %get-tuple-element.18), channel_id=1, source_target_pairs={{0,1},{1,0},{2,3},{3,2},{4,5},{5,4},{6,7},{7,6},{8,9},{9,8},{10,11... | collective-permute-start | bytes 393224 | tf_op jit(solution)/shard_map/ppermute | solution.py:132
  45.4 6.5 %collective-permute-start.18 = (bf16[32,16,128]{2,1,0:T(8,128)(2,1)S(1)}, bf16[32,16,128]{2,1,0:T(8,128)(2,1)S(1)}, u32[]{:S(2)}, u32[]{:S(2)}) collective-permute-start(bf16[32,16,128]{2,1,0:T(8,128)(2,1)S(1)} %get-tuple-element.19), channel_id=1, source_target_pairs={{0,2},{1,3},{2,0},{3,1},{4,6},{5,7},{6,4},{7,5},{8,10},{9,11},{10,... | collective-permute-start | bytes 393224 | tf_op jit(solution)/shard_map/ppermute | solution.py:132
  46.1 7.6 %collective-permute-start.19 = (bf16[32,16,128]{2,1,0:T(8,128)(2,1)S(1)}, bf16[32,16,128]{2,1,0:T(8,128)(2,1)S(1)}, u32[]{:S(2)}, u32[]{:S(2)}) collective-permute-start(bf16[32,16,128]{2,1,0:T(8,128)(2,1)S(1)} %get-tuple-element.20), channel_id=1, source_target_pairs={{0,3},{1,2},{2,1},{3,0},{4,7},{5,6},{6,5},{7,4},{8,11},{9,10},{10,... | collective-permute-start | bytes 393224 | tf_op jit(solution)/shard_map/ppermute | solution.py:132

commit v4 on v3

v4 whole, which is shorter than its diff:
```python
import functools

import jax
import jax.numpy as jnp
from jax import lax
from jax.experimental import pallas as pl
from jax.experimental.pallas import tpu as pltpu
from jax.sharding import PartitionSpec as P

QC = 16
ITERS = 2
COPIES = 8
UNROLL = 64

HBM = pltpu.HBM
VMEM = pltpu.VMEM
SMEM = pltpu.SMEM


def div(value, size):
    if size & (size - 1) == 0:
        return lax.shift_right_logical(value, jnp.full_like(value, size.bit_length() - 1))
    return lax.div(value, jnp.full_like(value, size))


def fetch(nrow, ncol, blk, tiles_hbm, rows_hbm, cols_hbm, count, tiles, table, rows, cols, sem):
    nt = tiles.shape[0]
    part = nt // COPIES

    def copy(i):
        some = pl.ds(i * part, part)
        return pltpu.make_async_copy(tiles_hbm.at[some], tiles.at[some], sem.at[i])

    tables = [
        pltpu.make_async_copy(source, target, sem.at[COPIES + i])
        for i, (source, target) in enumerate(((rows_hbm, rows), (cols_hbm, cols)))
    ]
    for c in tables:
        c.start()
    for i in range(COPIES):
        copy(i).start()
    for c in tables:
        c.wait()
    row_pos = lax.axis_index("row")
    col = cols[...]
    owner = div(col, blk)
    far = div(owner, ncol) ^ row_pos
    slot = (far & 1) * (nrow // 2) + div(far, 2)
    table[pl.ds(0, 1), :] = slot * blk + col - owner * blk
    live = lax.broadcasted_iota(jnp.int32, (1, nt), 1) < count[0]
    table[pl.ds(1, 1), :] = jnp.where(live, rows[...] - row_pos * (blk * ncol), blk * ncol)
    for i in range(COPIES):
        copy(i).wait()


def spread(seeded, nrow, ncol, blk, *refs):
    tiles, table_in, refs = refs[0], refs[1], refs[2:]
    fields, refs = refs[:nrow], refs[nrow:]
    outs, refs = refs[:ncol], refs[ncol:]
    total, picks, table, sem = refs
    nt = tiles.shape[0]
    col_pos = lax.axis_index("col")
    load = pltpu.make_async_copy(table_in, table, sem)
    load.start()
    total[...] = jnp.zeros_like(total)
    if seeded:
        for i, f in enumerate(fields):
            for kind in range(2):
                picks[kind, pl.ds(i * blk, blk), :] = f[kind].astype(jnp.float32)
    else:
        for i, f in enumerate(fields):
            picks[pl.ds(i * blk, blk)] = f[...]
    query = lax.broadcasted_iota(jnp.int32, (QC, 128), 0).astype(jnp.float32)
    load.wait()

    def pick(t):
        place = table[0, t]
        if seeded:
            label = picks[0, pl.ds(place, 1), :]
            scale = picks[1, pl.ds(place, 1), :]
            return jnp.where(label == query, scale, 0.0).astype(jnp.bfloat16)
        return picks[place]

    def step(i, carry):
        terms = []
        for u in range(0, UNROLL, 2):
            t = i * UNROLL + u
            pair = lax.dot_general(
                jnp.concatenate([pick(t), pick(t + 1)], 0),
                tiles[pl.ds(t, 2)].reshape(256, 128),
                (((1,), (1,)), ((), ())),
                preferred_element_type=jnp.float32,
            )
            terms += [pair[:QC, :128], pair[QC:, 128:]]
        for u in range(UNROLL):
            total[table[1, i * UNROLL + u]] += terms[u]
        return carry

    lax.fori_loop(0, nt // UNROLL, step, 0)
    for k in range(ncol):
        part = total[pl.ds((col_pos ^ k) * blk, blk)]
        outs[k][...] = part.astype(outs[k].dtype)


def fetch_call(nrow, ncol, blk, tiles, rows, cols, count):
    nt = tiles.shape[0]
    return pl.pallas_call(
        functools.partial(fetch, nrow, ncol, blk),
        out_shape=[VMEM(tiles.shape, tiles.dtype), VMEM((2, nt), jnp.int32)],
        in_specs=[pl.BlockSpec(memory_space=HBM)] * 3 + [pl.BlockSpec(memory_space=SMEM)],
        out_specs=[pl.BlockSpec(memory_space=VMEM)] * 2,
        scratch_shapes=[VMEM((1, nt), jnp.int32)] * 2 + [pltpu.SemaphoreType.DMA((COPIES + 2,))],
        compiler_params=pltpu.CompilerParams(vmem_limit_bytes=16 << 20),
        cost_estimate=pl.CostEstimate(flops=0, bytes_accessed=tiles.size * 2, transcendentals=0),
    )(*(pltpu.with_memory_space_constraint(x, HBM) for x in (tiles, rows.reshape(1, nt), cols.reshape(1, nt))), count)


def spread_call(seeded, nrow, ncol, blk, tiles, table, fields):
    nt = tiles.shape[0]
    slots = nrow * blk
    shape = (blk, QC, 128)
    picks = pltpu.VMEM((2, slots, 128), jnp.float32) if seeded else pltpu.VMEM((slots, QC, 128), jnp.bfloat16)
    return pl.pallas_call(
        functools.partial(spread, seeded, nrow, ncol, blk),
        out_shape=[jax.ShapeDtypeStruct(shape, jnp.float32)]
        + [jax.ShapeDtypeStruct(shape, jnp.bfloat16)] * (ncol - 1),
        in_specs=[pl.BlockSpec(memory_space=VMEM)] * (2 + len(fields)),
        out_specs=[pl.BlockSpec(memory_space=VMEM)] * ncol,
        scratch_shapes=[
            pltpu.VMEM((blk * ncol + 1, QC, 128), jnp.float32),
            picks,
            pltpu.SMEM(table.shape, table.dtype),
            pltpu.SemaphoreType.DMA,
        ],
        compiler_params=pltpu.CompilerParams(vmem_limit_bytes=24 << 20),
        cost_estimate=pl.CostEstimate(
            flops=2 * nt * QC * 128 * 128, bytes_accessed=tiles.size * 2 + slots * QC * 256, transcendentals=0
        ),
    )(*(pltpu.with_memory_space_constraint(x, VMEM) for x in (tiles, table)), *fields)


def local(nrow, ncol, tiles, tile_rows, tile_cols, tile_count, degree, labels):
    blk = labels.shape[0]
    nz = nrow // 2

    def from_row(x, d):
        return lax.ppermute(x, "row", [(i, i ^ d) for i in range(nrow)])

    def from_col(x, k):
        return lax.ppermute(x, "col", [(i, i ^ k) for i in range(ncol)])

    scale = 1.0 / jnp.sqrt(degree.astype(jnp.float32))
    qidx = jnp.arange(QC, dtype=jnp.int32)
    prior = (labels[:, None, :] == qidx[None, :, None]).astype(jnp.float32)
    kind = lax.broadcasted_iota(jnp.int32, (2, 1, 1), 0)
    raw = jnp.where(kind == 0, labels[None], degree[None]).astype(jnp.float32)
    own = jnp.where(kind == 0, raw, 1.0 / jnp.sqrt(raw)).astype(jnp.bfloat16)
    tiles, table = fetch_call(nrow, ncol, blk, tiles, tile_rows, tile_cols, tile_count)
    for step in range(ITERS):
        if step > 0:
            own = (field * scale[:, None, :]).astype(jnp.bfloat16)
        near = [own] + [from_row(own, 2 * m) for m in range(1, nz)]
        if step == 0:
            near[-1], table = lax.optimization_barrier((near[-1], table))
        fields = near + [from_row(x, 1) for x in near]
        outs = spread_call(step == 0, nrow, ncol, blk, tiles, table, fields)
        summed = outs[0]
        for k in range(1, ncol):
            summed = summed + from_col(outs[k], k).astype(jnp.float32)
        field = 0.8 * scale[:, None, :] * summed + 0.2 * prior
    return field


def solution(mesh):
    nrow, ncol = mesh.shape["row"], mesh.shape["col"]
    return jax.shard_map(
        functools.partial(local, nrow, ncol),
        mesh=mesh,
        in_specs=(
            P(("row", "col"), None, None),
            P(("row", "col")),
            P(("row", "col")),
            P(("row", "col")),
            P(("row", "col"), None),
            P(("row", "col"), None),
        ),
        out_specs=P(("row", "col"), None, None),
        check_vma=False,
    )
```

time: 54.7 us -> 52.7 us (0.963)
  waiting for transfers between devices: 26.2 us -> 24.5 us
  other arithmetic: 2.43 us -> 1.73 us
    pallas_call x0 -> x1, Pallas kernels: none -> 2.27 us  [fetch_call(): pl.pallas_call(functools.partial(fetch, nrow, ncol, blk), out_shape=[VMEM...]
    pallas_call x2, Pallas kernels: 6.68 us -> 4.61 us  [spread_call(): pl.pallas_call(functools.partial(spread, seeded, nrow, ncol, blk), out_sh...]
    ppermute x14, waiting for transfers between devices: 13.8 us -> 11.9 us  [from_row(): return lax.ppermute(x, 'row', [(i, i ^ d) for i in range(nrow)])]
    convert_element_type x0 -> x1, other arithmetic: none -> 0.82 us  [local(): own = jnp.where(kind == 0, raw, 1.0 / jnp.sqrt(raw)).astype(jnp.bfloat16)]
    another operation x2 -> x0, other arithmetic: 0.8 us -> none  [local(): seeds = jnp.stack([labels.astype(jnp.bfloat16), scale.astype(jnp.bfloat16)])]
    mul x1, other arithmetic: 0.72 us -> 0.01 us  [local(): field = 0.8 * scale[:, None, :] * summed + 0.2 * prior]
  transfers between devices with their start and end apart: 20 -> 20, of which waited for: 12 -> 12; matrix products, arithmetic and copies ran while one was open for 0% -> 0% of each run, Pallas kernels for 0% -> 4%
where the time goes in v4:
time: 52.7 us; the launch traced here: 52.3 us
  waiting for transfers between devices  24.5 us (46%)
  starting transfers between devices  18.3 us (35%)
  Pallas kernels  6.88 us (13%)
  other arithmetic  1.73 us (3%)
  between operations  0.73 us (1%)
    ppermute x6, waiting for transfers between devices, from_col(): return lax.ppermute(x, 'col', [(i, i ^ k) for i in range(ncol)])  12.6 us
    ppermute x14, waiting for transfers between devices, from_row(): return lax.ppermute(x, 'row', [(i, i ^ d) for i in range(nrow)])  11.9 us
    ppermute x14, starting transfers between devices, from_row(): return lax.ppermute(x, 'row', [(i, i ^ d) for i in range(nrow)])  11.2 us
    ppermute x6, starting transfers between devices, from_col(): return lax.ppermute(x, 'col', [(i, i ^ k) for i in range(ncol)])  7.11 us
    pallas_call x2, Pallas kernels, spread_call(): pl.pallas_call(functools.partial(spread, seeded, nrow, ncol, blk), out_sh...  4.61 us
    pallas_call x1, Pallas kernels, fetch_call(): pl.pallas_call(functools.partial(fetch, nrow, ncol, blk), out_shape=[VMEM...  2.27 us
  transfers between devices with their start and end apart: 20, of which 12 were waited for; matrix products, arithmetic and copies ran while one was open for 0% of the time, Pallas kernels for 4%

profile of v4, /device:TPU:0, one launch (start us, length us, event | category | flops | bytes accessed | tf_op | source)
XLA Modules:
  0.0 52.3 jit_solution(5676678308433957981)
XLA Ops:
  0.0 0.8 %fusion.2.refs_2_ = bf16[2,32,128]{2,1,0:T(8,128)(2,1)S(1)} fusion(s32[32,128]{1,0:T(8,128)} %param.10, s32[32,128]{1,0:T(8,128)} %param.11, pred[2]{0:T(512)(128)(4,1)S(1)} %iota_compare_fusion.1), kind=kLoop, calls=%fused_computation.6 | loop fusion | flops 32768 | bytes 49154 | tf_op jit(solution)/shard_map/convert_element_type | solution.py:157
  0.8 5.1 %collective-permute-start = (bf16[2,32,128]{2,1,0:T(8,128)(2,1)S(1)}, bf16[2,32,128]{2,1,0:T(8,128)(2,1)S(1)}, u32[]{:S(2)}, u32[]{:S(2)}) collective-permute-start(bf16[2,32,128]{2,1,0:T(8,128)(2,1)S(1)} %fusion.2.refs_2_), channel_id=1, source_target_pairs={{0,24},{4,28},{8,16},{12,20},{16,8},{20,12},{24,0},{28,4},{1,25},{... | collective-permute-start | bytes 49160 | tf_op jit(solution)/shard_map/ppermute | solution.py:147
  5.9 0.0 collective-permute-start.2
  5.9 0.6 %collective-permute-start.1 = (bf16[2,32,128]{2,1,0:T(8,128)(2,1)S(1)}, bf16[2,32,128]{2,1,0:T(8,128)(2,1)S(1)}, u32[]{:S(2)}, u32[]{:S(2)}) collective-permute-start(bf16[2,32,128]{2,1,0:T(8,128)(2,1)S(1)} %fusion.2.refs_2_), channel_id=1, source_target_pairs={{0,8},{4,12},{8,0},{12,4},{16,24},{20,28},{24,16},{28,20},{1,9},{5... | collective-permute-start | bytes 49160 | tf_op jit(solution)/shard_map/ppermute | solution.py:147
  6.6 0.0 collective-permute-start.3
  7.2 0.0 copy-start.1
  7.3 0.0 copy-start
  7.3 2.3 %shard_map.64 = (bf16[128,128,128]{2,1,0:T(8,128)(2,1)S(1)}, s32[2,128]{1,0:T(2,128)S(1)}) custom-call(bf16[128,128,128]{2,1,0:T(8,128)(2,1)} %tiles_hbm.1, s32[1,128]{1,0:T(1,128)} %bitcast.2, s32[1,128]{1,0:T(1,128)} %bitcast.3, s32[1]{0:T(128)S(6)} %copy.7.count), custom_call_target="tpu_custom_call" | custom-call | bytes 4194304 | tf_op jit(solution)/shard_map/pallas_call | solution.py:107
  9.5 0.0 collective-permute-done.refs_5_
  9.6 1.0 %collective-permute-done.2.refs_4_ = bf16[2,32,128]{2,1,0:T(8,128)(2,1)S(1)} collective-permute-done((bf16[2,32,128]{2,1,0:T(8,128)(2,1)S(1)}, bf16[2,32,128]{2,1,0:T(8,128)(2,1)S(1)}, u32[]{:S(2)}, u32[]{:S(2)}) %collective-permute-start.2) | collective-permute-done | bytes 16416 | tf_op jit(solution)/shard_map/ppermute | solution.py:147
  10.6 0.0 collective-permute-start.5
  10.6 0.0 collective-permute-done.1.refs_3_
  10.6 0.5 collective-permute-start.4
  11.1 0.0 collective-permute-start.6
  11.1 0.0 collective-permute-done.3.refs_6_
  11.1 0.7 %collective-permute-done.5.refs_8_ = bf16[2,32,128]{2,1,0:T(8,128)(2,1)S(1)} collective-permute-done((bf16[2,32,128]{2,1,0:T(8,128)(2,1)S(1)}, bf16[2,32,128]{2,1,0:T(8,128)(2,1)S(1)}, u32[]{:S(2)}, u32[]{:S(2)}) %collective-permute-start.5) | collective-permute-done | bytes 16416 | tf_op jit(solution)/shard_map/ppermute | solution.py:147
  11.8 0.2 collective-permute-done.4.refs_7_
  11.9 0.3 collective-permute-done.6.refs_9_
  12.3 2.3 %shard_map.65 = (f32[32,16,128]{2,1,0:T(8,128)S(1)}, bf16[32,16,128]{2,1,0:T(8,128)(2,1)S(1)}, bf16[32,16,128]{2,1,0:T(8,128)(2,1)S(1)}, bf16[32,16,128]{2,1,0:T(8,128)(2,1)S(1)}) custom-call(bf16[128,128,128]{2,1,0:T(8,128)(2,1)S(1)} %get-tuple-element.17.refs_0_, s32[2,128]{1,0:T(2,128)S(1)} %get-tuple-element.19.refs_1_, ...), custom_call_target="tpu_custom_call" | custom-call | flops 67108864 | bytes 5242880 | tf_op jit(solution)/shard_map/pallas_call | solution.py:123
  14.6 1.5 %collective-permute-start.7 = (bf16[32,16,128]{2,1,0:T(8,128)(2,1)S(1)}, bf16[32,16,128]{2,1,0:T(8,128)(2,1)S(1)}, u32[]{:S(2)}, u32[]{:S(2)}) collective-permute-start(bf16[32,16,128]{2,1,0:T(8,128)(2,1)S(1)} %get-tuple-element.22), channel_id=1, source_target_pairs={{0,1},{1,0},{2,3},{3,2},{4,5},{5,4},{6,7},{7,6},{8,9},{9,8},{10,11... | collective-permute-start | bytes 393224 | tf_op jit(solution)/shard_map/ppermute | solution.py:150
  16.1 1.5 %collective-permute-start.8 = (bf16[32,16,128]{2,1,0:T(8,128)(2,1)S(1)}, bf16[32,16,128]{2,1,0:T(8,128)(2,1)S(1)}, u32[]{:S(2)}, u32[]{:S(2)}) collective-permute-start(bf16[32,16,128]{2,1,0:T(8,128)(2,1)S(1)} %get-tuple-element.23), channel_id=1, source_target_pairs={{0,2},{1,3},{2,0},{3,1},{4,6},{5,7},{6,4},{7,5},{8,10},{9,11},{10,... | collective-permute-start | bytes 393224 | tf_op jit(solution)/shard_map/ppermute | solution.py:150
  17.7 0.5 collective-permute-start.9
  18.1 0.0 copy-done.1
  18.2 2.4 %collective-permute-done.7 = bf16[32,16,128]{2,1,0:T(8,128)(2,1)S(1)} collective-permute-done((bf16[32,16,128]{2,1,0:T(8,128)(2,1)S(1)}, bf16[32,16,128]{2,1,0:T(8,128)(2,1)S(1)}, u32[]{:S(2)}, u32[]{:S(2)}) %collective-permute-start.7) | collective-permute-done | bytes 131104 | tf_op jit(solution)/shard_map/ppermute | solution.py:150
  20.5 3.7 %collective-permute-done.8 = bf16[32,16,128]{2,1,0:T(8,128)(2,1)S(1)} collective-permute-done((bf16[32,16,128]{2,1,0:T(8,128)(2,1)S(1)}, bf16[32,16,128]{2,1,0:T(8,128)(2,1)S(1)}, u32[]{:S(2)}, u32[]{:S(2)}) %collective-permute-start.8) | collective-permute-done | bytes 131104 | tf_op jit(solution)/shard_map/ppermute | solution.py:150
  24.2 0.0 collective-permute-done.9
  24.2 0.0 copy-done
  24.2 0.1 fusion.1.refs_2_
  24.3 3.2 %collective-permute-start.12 = (bf16[32,16,128]{2,1,0:T(8,128)(2,1)S(1)}, bf16[32,16,128]{2,1,0:T(8,128)(2,1)S(1)}, u32[]{:S(2)}, u32[]{:S(2)}) collective-permute-start(bf16[32,16,128]{2,1,0:T(8,128)(2,1)S(1)} %fusion.1.refs_2_), channel_id=1, source_target_pairs={{0,24},{4,28},{8,16},{12,20},{16,8},{20,12},{24,0},{28,4},{1,25},{... | collective-permute-start | bytes 393224 | tf_op jit(solution)/shard_map/ppermute | solution.py:147
  27.5 0.0 collective-permute-start.11
  27.5 1.2 %collective-permute-start.10 = (bf16[32,16,128]{2,1,0:T(8,128)(2,1)S(1)}, bf16[32,16,128]{2,1,0:T(8,128)(2,1)S(1)}, u32[]{:S(2)}, u32[]{:S(2)}) collective-permute-start(bf16[32,16,128]{2,1,0:T(8,128)(2,1)S(1)} %fusion.1.refs_2_), channel_id=1, source_target_pairs={{0,8},{4,12},{8,0},{12,4},{16,24},{20,28},{24,16},{28,20},{1,9},{5... | collective-permute-start | bytes 393224 | tf_op jit(solution)/shard_map/ppermute | solution.py:147
  28.8 0.0 collective-permute-start.13
  28.8 3.9 %collective-permute-done.12.refs_5_ = bf16[32,16,128]{2,1,0:T(8,128)(2,1)S(1)} collective-permute-done((bf16[32,16,128]{2,1,0:T(8,128)(2,1)S(1)}, bf16[32,16,128]{2,1,0:T(8,128)(2,1)S(1)}, u32[]{:S(2)}, u32[]{:S(2)}) %collective-permute-start.12) | collective-permute-done | bytes 131104 | tf_op jit(solution)/shard_map/ppermute | solution.py:147
  32.7 0.0 collective-permute-start.16
  32.7 4.8 %collective-permute-done.11.refs_4_ = bf16[32,16,128]{2,1,0:T(8,128)(2,1)S(1)} collective-permute-done((bf16[32,16,128]{2,1,0:T(8,128)(2,1)S(1)}, bf16[32,16,128]{2,1,0:T(8,128)(2,1)S(1)}, u32[]{:S(2)}, u32[]{:S(2)}) %collective-permute-start.11) | collective-permute-done | bytes 131104 | tf_op jit(solution)/shard_map/ppermute | solution.py:147
  37.5 0.0 collective-permute-start.15
  37.5 0.0 collective-permute-done.10.refs_3_
  37.5 0.5 collective-permute-start.14
  38.0 0.0 collective-permute-done.13.refs_6_
  38.0 0.0 collective-permute-done.16.refs_9_
  38.0 0.8 %collective-permute-done.15.refs_8_ = bf16[32,16,128]{2,1,0:T(8,128)(2,1)S(1)} collective-permute-done((bf16[32,16,128]{2,1,0:T(8,128)(2,1)S(1)}, bf16[32,16,128]{2,1,0:T(8,128)(2,1)S(1)}, u32[]{:S(2)}, u32[]{:S(2)}) %collective-permute-start.15) | collective-permute-done | bytes 131104 | tf_op jit(solution)/shard_map/ppermute | solution.py:147
  38.9 0.2 collective-permute-done.14.refs_7_
  39.0 2.3 %shard_map.66 = (f32[32,16,128]{2,1,0:T(8,128)S(1)}, bf16[32,16,128]{2,1,0:T(8,128)(2,1)S(1)}, bf16[32,16,128]{2,1,0:T(8,128)(2,1)S(1)}, bf16[32,16,128]{2,1,0:T(8,128)(2,1)S(1)}) custom-call(bf16[128,128,128]{2,1,0:T(8,128)(2,1)S(1)} %get-tuple-element.17.refs_0_, s32[2,128]{1,0:T(2,128)S(1)} %get-tuple-element.19.refs_1_, ...), custom_call_target="tpu_custom_call" | custom-call | flops 67108864 | bytes 5242880 | tf_op jit(solution)/shard_map/pallas_call | solution.py:123
  41.4 1.8 %collective-permute-start.17 = (bf16[32,16,128]{2,1,0:T(8,128)(2,1)S(1)}, bf16[32,16,128]{2,1,0:T(8,128)(2,1)S(1)}, u32[]{:S(2)}, u32[]{:S(2)}) collective-permute-start(bf16[32,16,128]{2,1,0:T(8,128)(2,1)S(1)} %get-tuple-element.26), channel_id=1, source_target_pairs={{0,1},{1,0},{2,3},{3,2},{4,5},{5,4},{6,7},{7,6},{8,9},{9,8},{10,11... | collective-permute-start | bytes 393224 | tf_op jit(solution)/shard_map/ppermute | solution.py:150
  43.2 0.5 collective-permute-start.18
  43.7 1.2 %collective-permute-start.19 = (bf16[32,16,128]{2,1,0:T(8,128)(2,1)S(1)}, bf16[32,16,128]{2,1,0:T(8,128)(2,1)S(1)}, u32[]{:S(2)}, u32[]{:S(2)}) collective-permute-start(bf16[32,16,128]{2,1,0:T(8,128)(2,1)S(1)} %get-tuple-element.28), channel_id=1, source_target_pairs={{0,3},{1,2},{2,1},{3,0},{4,7},{5,6},{6,5},{7,4},{8,11},{9,10},{10,... | collective-permute-start | bytes 393224 | tf_op jit(solution)/shard_map/ppermute | solution.py:150
  44.9 2.4 %collective-permute-done.17 = bf16[32,16,128]{2,1,0:T(8,128)(2,1)S(1)} collective-permute-done((bf16[32,16,128]{2,1,0:T(8,128)(2,1)S(1)}, bf16[32,16,128]{2,1,0:T(8,128)(2,1)S(1)}, u32[]{:S(2)}, u32[]{:S(2)}) %collective-permute-start.17) | collective-permute-done | bytes 131104 | tf_op jit(solution)/shard_map/ppermute | solution.py:150
  47.3 4.2 %collective-permute-done.18 = bf16[32,16,128]{2,1,0:T(8,128)(2,1)S(1)} collective-permute-done((bf16[32,16,128]{2,1,0:T(8,128)(2,1)S(1)}, bf16[32,16,128]{2,1,0:T(8,128)(2,1)S(1)}, u32[]{:S(2)}, u32[]{:S(2)}) %collective-permute-start.18) | collective-permute-done | bytes 131104 | tf_op jit(solution)/shard_map/ppermute | solution.py:150
  51.5 0.0 collective-permute-done.19
  51.5 0.8 %select_add_fusion = f32[32,16,128]{2,1,0:T(8,128)} fusion(bf16[32,16,128]{2,1,0:T(8,128)(2,1)S(1)} %collective-permute-done.19, bf16[32,16,128]{2,1,0:T(8,128)(2,1)S(1)} %collective-permute-done.18, f32[32,16,128]{2,1,0:T(8,128)S(1)} %get-tuple-element.25, bf16[32,16,128]{2,1,0:T(8,128)(2,1)S(1)} %collective-permute-done.17, s32[32,128]{1,0:T(8,128)S(1)} %copy-done, ...), kind=kLoop, calls=%fused_computation | loop fusion | flops 655360 | bytes 950272 | tf_op jit(solution)/shard_map/add | solution.py:170
  (2 shorter events, 0.0 us)
Async XLA Ops:
  0.8 8.7 %collective-permute-start = (bf16[2,32,128]{2,1,0:T(8,128)(2,1)S(1)}, bf16[2,32,128]{2,1,0:T(8,128)(2,1)S(1)}, u32[]{:S(2)}, u32[]{:S(2)}) collective-permute-start(bf16[2,32,128]{2,1,0:T(8,128)(2,1)S(1)} %fusion.2.refs_2_), channel_id=1, source_target_pairs={{0,24},{4,28},{8,16},{12,20},{16,8},{20,12},{24,0},{28,4},{1,25},{... | collective-permute-start | bytes 49160 | tf_op jit(solution)/shard_map/ppermute | solution.py:147
  5.9 4.6 %collective-permute-start.2 = (bf16[2,32,128]{2,1,0:T(8,128)(2,1)S(1)}, bf16[2,32,128]{2,1,0:T(8,128)(2,1)S(1)}, u32[]{:S(2)}, u32[]{:S(2)}) collective-permute-start(bf16[2,32,128]{2,1,0:T(8,128)(2,1)S(1)} %fusion.2.refs_2_), channel_id=1, source_target_pairs={{0,16},{4,20},{8,24},{12,28},{16,0},{20,4},{24,8},{28,12},{1,17},{... | collective-permute-start | bytes 49160 | tf_op jit(solution)/shard_map/ppermute | solution.py:147
  5.9 4.6 %collective-permute-start.1 = (bf16[2,32,128]{2,1,0:T(8,128)(2,1)S(1)}, bf16[2,32,128]{2,1,0:T(8,128)(2,1)S(1)}, u32[]{:S(2)}, u32[]{:S(2)}) collective-permute-start(bf16[2,32,128]{2,1,0:T(8,128)(2,1)S(1)} %fusion.2.refs_2_), channel_id=1, source_target_pairs={{0,8},{4,12},{8,0},{12,4},{16,24},{20,28},{24,16},{28,20},{1,9},{5... | collective-permute-start | bytes 49160 | tf_op jit(solution)/shard_map/ppermute | solution.py:147
  6.6 4.5 %collective-permute-start.3 = (bf16[2,32,128]{2,1,0:T(8,128)(2,1)S(1)}, bf16[2,32,128]{2,1,0:T(8,128)(2,1)S(1)}, u32[]{:S(2)}, u32[]{:S(2)}) collective-permute-start(bf16[2,32,128]{2,1,0:T(8,128)(2,1)S(1)} %fusion.2.refs_2_), channel_id=1, source_target_pairs={{0,4},{4,0},{8,12},{12,8},{16,20},{20,16},{24,28},{28,24},{1,5},{5... | collective-permute-start | bytes 49160 | tf_op jit(solution)/shard_map/ppermute | solution.py:147
  7.2 10.9 %copy-start.1 = (s32[32,128]{1,0:T(8,128)S(1)}, s32[32,128]{1,0:T(8,128)}, u32[]{:S(2)}) copy-start(s32[32,128]{1,0:T(8,128)} %param.10) | copy-start | bytes 49156
  7.3 17.0 %copy-start = (s32[32,128]{1,0:T(8,128)S(1)}, s32[32,128]{1,0:T(8,128)}, u32[]{:S(2)}) copy-start(s32[32,128]{1,0:T(8,128)} %param.11) | copy-start | bytes 49156
  10.6 1.2 %collective-permute-start.5 = (bf16[2,32,128]{2,1,0:T(8,128)(2,1)S(1)}, bf16[2,32,128]{2,1,0:T(8,128)(2,1)S(1)}, u32[]{:S(2)}, u32[]{:S(2)}) collective-permute-start(bf16[2,32,128]{2,1,0:T(8,128)(2,1)S(1)} %collective-permute-done.2.refs_4_), channel_id=1, source_target_pairs={{0,4},{4,0},{8,12},{12,8},{16,20},{20,16},{24,28},{28,24},{1,5},{5... | collective-permute-start | bytes 49160 | tf_op jit(solution)/shard_map/ppermute | solution.py:147
  10.6 1.3 %collective-permute-start.4 = (bf16[2,32,128]{2,1,0:T(8,128)(2,1)S(1)}, bf16[2,32,128]{2,1,0:T(8,128)(2,1)S(1)}, u32[]{:S(2)}, u32[]{:S(2)}) collective-permute-start(bf16[2,32,128]{2,1,0:T(8,128)(2,1)S(1)} %collective-permute-done.1.refs_3_), channel_id=1, source_target_pairs={{0,4},{4,0},{8,12},{12,8},{16,20},{20,16},{24,28},{28,24},{1,5},{5... | collective-permute-start | bytes 49160 | tf_op jit(solution)/shard_map/ppermute | solution.py:147
  11.1 1.2 %collective-permute-start.6 = (bf16[2,32,128]{2,1,0:T(8,128)(2,1)S(1)}, bf16[2,32,128]{2,1,0:T(8,128)(2,1)S(1)}, u32[]{:S(2)}, u32[]{:S(2)}) collective-permute-start(bf16[2,32,128]{2,1,0:T(8,128)(2,1)S(1)} %collective-permute-done.refs_5_), channel_id=1, source_target_pairs={{0,4},{4,0},{8,12},{12,8},{16,20},{20,16},{24,28},{28,24},{1,5},{5... | collective-permute-start | bytes 49160 | tf_op jit(solution)/shard_map/ppermute | solution.py:147
  14.6 6.0 %collective-permute-start.7 = (bf16[32,16,128]{2,1,0:T(8,128)(2,1)S(1)}, bf16[32,16,128]{2,1,0:T(8,128)(2,1)S(1)}, u32[]{:S(2)}, u32[]{:S(2)}) collective-permute-start(bf16[32,16,128]{2,1,0:T(8,128)(2,1)S(1)} %get-tuple-element.22), channel_id=1, source_target_pairs={{0,1},{1,0},{2,3},{3,2},{4,5},{5,4},{6,7},{7,6},{8,9},{9,8},{10,11... | collective-permute-start | bytes 393224 | tf_op jit(solution)/shard_map/ppermute | solution.py:150
  16.1 8.1 %collective-permute-start.8 = (bf16[32,16,128]{2,1,0:T(8,128)(2,1)S(1)}, bf16[32,16,128]{2,1,0:T(8,128)(2,1)S(1)}, u32[]{:S(2)}, u32[]{:S(2)}) collective-permute-start(bf16[32,16,128]{2,1,0:T(8,128)(2,1)S(1)} %get-tuple-element.23), channel_id=1, source_target_pairs={{0,2},{1,3},{2,0},{3,1},{4,6},{5,7},{6,4},{7,5},{8,10},{9,11},{10,... | collective-permute-start | bytes 393224 | tf_op jit(solution)/shard_map/ppermute | solution.py:150
  17.7 6.6 %collective-permute-start.9 = (bf16[32,16,128]{2,1,0:T(8,128)(2,1)S(1)}, bf16[32,16,128]{2,1,0:T(8,128)(2,1)S(1)}, u32[]{:S(2)}, u32[]{:S(2)}) collective-permute-start(bf16[32,16,128]{2,1,0:T(8,128)(2,1)S(1)} %get-tuple-element.24), channel_id=1, source_target_pairs={{0,3},{1,2},{2,1},{3,0},{4,7},{5,6},{6,5},{7,4},{8,11},{9,10},{10,... | collective-permute-start | bytes 393224 | tf_op jit(solution)/shard_map/ppermute | solution.py:150
  24.3 8.3 %collective-permute-start.12 = (bf16[32,16,128]{2,1,0:T(8,128)(2,1)S(1)}, bf16[32,16,128]{2,1,0:T(8,128)(2,1)S(1)}, u32[]{:S(2)}, u32[]{:S(2)}) collective-permute-start(bf16[32,16,128]{2,1,0:T(8,128)(2,1)S(1)} %fusion.1.refs_2_), channel_id=1, source_target_pairs={{0,24},{4,28},{8,16},{12,20},{16,8},{20,12},{24,0},{28,4},{1,25},{... | collective-permute-start | bytes 393224 | tf_op jit(solution)/shard_map/ppermute | solution.py:147
  27.5 10.0 %collective-permute-start.11 = (bf16[32,16,128]{2,1,0:T(8,128)(2,1)S(1)}, bf16[32,16,128]{2,1,0:T(8,128)(2,1)S(1)}, u32[]{:S(2)}, u32[]{:S(2)}) collective-permute-start(bf16[32,16,128]{2,1,0:T(8,128)(2,1)S(1)} %fusion.1.refs_2_), channel_id=1, source_target_pairs={{0,16},{4,20},{8,24},{12,28},{16,0},{20,4},{24,8},{28,12},{1,17},{... | collective-permute-start | bytes 393224 | tf_op jit(solution)/shard_map/ppermute | solution.py:147
  27.5 10.0 %collective-permute-start.10 = (bf16[32,16,128]{2,1,0:T(8,128)(2,1)S(1)}, bf16[32,16,128]{2,1,0:T(8,128)(2,1)S(1)}, u32[]{:S(2)}, u32[]{:S(2)}) collective-permute-start(bf16[32,16,128]{2,1,0:T(8,128)(2,1)S(1)} %fusion.1.refs_2_), channel_id=1, source_target_pairs={{0,8},{4,12},{8,0},{12,4},{16,24},{20,28},{24,16},{28,20},{1,9},{5... | collective-permute-start | bytes 393224 | tf_op jit(solution)/shard_map/ppermute | solution.py:147
  28.8 9.2 %collective-permute-start.13 = (bf16[32,16,128]{2,1,0:T(8,128)(2,1)S(1)}, bf16[32,16,128]{2,1,0:T(8,128)(2,1)S(1)}, u32[]{:S(2)}, u32[]{:S(2)}) collective-permute-start(bf16[32,16,128]{2,1,0:T(8,128)(2,1)S(1)} %fusion.1.refs_2_), channel_id=1, source_target_pairs={{0,4},{4,0},{8,12},{12,8},{16,20},{20,16},{24,28},{28,24},{1,5},{5... | collective-permute-start | bytes 393224 | tf_op jit(solution)/shard_map/ppermute | solution.py:147
  32.7 5.4 %collective-permute-start.16 = (bf16[32,16,128]{2,1,0:T(8,128)(2,1)S(1)}, bf16[32,16,128]{2,1,0:T(8,128)(2,1)S(1)}, u32[]{:S(2)}, u32[]{:S(2)}) collective-permute-start(bf16[32,16,128]{2,1,0:T(8,128)(2,1)S(1)} %collective-permute-done.12.refs_5_), channel_id=1, source_target_pairs={{0,4},{4,0},{8,12},{12,8},{16,20},{20,16},{24,28},{28,24},{1,5},{5... | collective-permute-start | bytes 393224 | tf_op jit(solution)/shard_map/ppermute | solution.py:147
  37.5 1.3 %collective-permute-start.15 = (bf16[32,16,128]{2,1,0:T(8,128)(2,1)S(1)}, bf16[32,16,128]{2,1,0:T(8,128)(2,1)S(1)}, u32[]{:S(2)}, u32[]{:S(2)}) collective-permute-start(bf16[32,16,128]{2,1,0:T(8,128)(2,1)S(1)} %collective-permute-done.11.refs_4_), channel_id=1, source_target_pairs={{0,4},{4,0},{8,12},{12,8},{16,20},{20,16},{24,28},{28,24},{1,5},{5... | collective-permute-start | bytes 393224 | tf_op jit(solution)/shard_map/ppermute | solution.py:147
  37.5 1.5 %collective-permute-start.14 = (bf16[32,16,128]{2,1,0:T(8,128)(2,1)S(1)}, bf16[32,16,128]{2,1,0:T(8,128)(2,1)S(1)}, u32[]{:S(2)}, u32[]{:S(2)}) collective-permute-start(bf16[32,16,128]{2,1,0:T(8,128)(2,1)S(1)} %collective-permute-done.10.refs_3_), channel_id=1, source_target_pairs={{0,4},{4,0},{8,12},{12,8},{16,20},{20,16},{24,28},{28,24},{1,5},{5... | collective-permute-start | bytes 393224 | tf_op jit(solution)/shard_map/ppermute | solution.py:147
  41.4 5.9 %collective-permute-start.17 = (bf16[32,16,128]{2,1,0:T(8,128)(2,1)S(1)}, bf16[32,16,128]{2,1,0:T(8,128)(2,1)S(1)}, u32[]{:S(2)}, u32[]{:S(2)}) collective-permute-start(bf16[32,16,128]{2,1,0:T(8,128)(2,1)S(1)} %get-tuple-element.26), channel_id=1, source_target_pairs={{0,1},{1,0},{2,3},{3,2},{4,5},{5,4},{6,7},{7,6},{8,9},{9,8},{10,11... | collective-permute-start | bytes 393224 | tf_op jit(solution)/shard_map/ppermute | solution.py:150
  43.2 8.3 %collective-permute-start.18 = (bf16[32,16,128]{2,1,0:T(8,128)(2,1)S(1)}, bf16[32,16,128]{2,1,0:T(8,128)(2,1)S(1)}, u32[]{:S(2)}, u32[]{:S(2)}) collective-permute-start(bf16[32,16,128]{2,1,0:T(8,128)(2,1)S(1)} %get-tuple-element.27), channel_id=1, source_target_pairs={{0,2},{1,3},{2,0},{3,1},{4,6},{5,7},{6,4},{7,5},{8,10},{9,11},{10,... | collective-permute-start | bytes 393224 | tf_op jit(solution)/shard_map/ppermute | solution.py:150
  43.7 7.8 %collective-permute-start.19 = (bf16[32,16,128]{2,1,0:T(8,128)(2,1)S(1)}, bf16[32,16,128]{2,1,0:T(8,128)(2,1)S(1)}, u32[]{:S(2)}, u32[]{:S(2)}) collective-permute-start(bf16[32,16,128]{2,1,0:T(8,128)(2,1)S(1)} %get-tuple-element.28), channel_id=1, source_target_pairs={{0,3},{1,2},{2,1},{3,0},{4,7},{5,6},{6,5},{7,4},{8,11},{9,10},{10,... | collective-permute-start | bytes 393224 | tf_op jit(solution)/shard_map/ppermute | solution.py:150

commit v5 on v4

--- a/solution.py
+++ b/solution.py
@@ -23,7 +23,7 @@
     return lax.div(value, jnp.full_like(value, size))
 
 
-def fetch(nrow, ncol, blk, tiles_hbm, rows_hbm, cols_hbm, count, tiles, table, rows, cols, sem):
+def fetch(nrow, ncol, blk, tiles_hbm, rows_hbm, cols_hbm, count, tiles, table_out, rows, cols, table, sem):
     nt = tiles.shape[0]
     part = nt // COPIES
 
@@ -49,29 +49,32 @@
     table[pl.ds(0, 1), :] = slot * blk + col - owner * blk
     live = lax.broadcasted_iota(jnp.int32, (1, nt), 1) < count[0]
     table[pl.ds(1, 1), :] = jnp.where(live, rows[...] - row_pos * (blk * ncol), blk * ncol)
+    out = pltpu.make_async_copy(table, table_out, sem.at[COPIES + 2])
+    out.start()
     for i in range(COPIES):
         copy(i).wait()
+    out.wait()
 
 
 def spread(seeded, nrow, ncol, blk, *refs):
-    tiles, table_in, refs = refs[0], refs[1], refs[2:]
-    fields, refs = refs[:nrow], refs[nrow:]
+    tiles, table, refs = refs[0], refs[1], refs[2:]
+    nfields = nrow // 2 if seeded else nrow
+    fields, refs = refs[:nfields], refs[nfields:]
     outs, refs = refs[:ncol], refs[ncol:]
-    total, picks, table, sem = refs
+    total, picks = refs
     nt = tiles.shape[0]
     col_pos = lax.axis_index("col")
-    load = pltpu.make_async_copy(table_in, table, sem)
-    load.start()
     total[...] = jnp.zeros_like(total)
     if seeded:
         for i, f in enumerate(fields):
-            for kind in range(2):
-                picks[kind, pl.ds(i * blk, blk), :] = f[kind].astype(jnp.float32)
+            for half in range(2):
+                for kind in range(2):
+                    place = (half * len(fields) + i) * blk
+                    picks[kind, pl.ds(place, blk), :] = f[half, kind].astype(jnp.float32)
     else:
         for i, f in enumerate(fields):
             picks[pl.ds(i * blk, blk)] = f[...]
     query = lax.broadcasted_iota(jnp.int32, (QC, 128), 0).astype(jnp.float32)
-    load.wait()
 
     def pick(t):
         place = table[0, t]
@@ -106,10 +109,10 @@
     nt = tiles.shape[0]
     return pl.pallas_call(
         functools.partial(fetch, nrow, ncol, blk),
-        out_shape=[VMEM(tiles.shape, tiles.dtype), VMEM((2, nt), jnp.int32)],
+        out_shape=[VMEM(tiles.shape, tiles.dtype), SMEM((2, nt), jnp.int32)],
         in_specs=[pl.BlockSpec(memory_space=HBM)] * 3 + [pl.BlockSpec(memory_space=SMEM)],
-        out_specs=[pl.BlockSpec(memory_space=VMEM)] * 2,
-        scratch_shapes=[VMEM((1, nt), jnp.int32)] * 2 + [pltpu.SemaphoreType.DMA((COPIES + 2,))],
+        out_specs=[pl.BlockSpec(memory_space=VMEM), pl.BlockSpec(memory_space=SMEM)],
+        scratch_shapes=[VMEM((1, nt), jnp.int32)] * 2 + [VMEM((2, nt), jnp.int32), pltpu.SemaphoreType.DMA((COPIES + 3,))],
         compiler_params=pltpu.CompilerParams(vmem_limit_bytes=16 << 20),
         cost_estimate=pl.CostEstimate(flops=0, bytes_accessed=tiles.size * 2, transcendentals=0),
     )(*(pltpu.with_memory_space_constraint(x, HBM) for x in (tiles, rows.reshape(1, nt), cols.reshape(1, nt))), count)
@@ -124,19 +127,18 @@
         functools.partial(spread, seeded, nrow, ncol, blk),
         out_shape=[jax.ShapeDtypeStruct(shape, jnp.float32)]
         + [jax.ShapeDtypeStruct(shape, jnp.bfloat16)] * (ncol - 1),
-        in_specs=[pl.BlockSpec(memory_space=VMEM)] * (2 + len(fields)),
+        in_specs=[pl.BlockSpec(memory_space=VMEM), pl.BlockSpec(memory_space=SMEM)]
+        + [pl.BlockSpec(memory_space=VMEM)] * len(fields),
         out_specs=[pl.BlockSpec(memory_space=VMEM)] * ncol,
         scratch_shapes=[
             pltpu.VMEM((blk * ncol + 1, QC, 128), jnp.float32),
             picks,
-            pltpu.SMEM(table.shape, table.dtype),
-            pltpu.SemaphoreType.DMA,
         ],
         compiler_params=pltpu.CompilerParams(vmem_limit_bytes=24 << 20),
         cost_estimate=pl.CostEstimate(
             flops=2 * nt * QC * 128 * 128, bytes_accessed=tiles.size * 2 + slots * QC * 256, transcendentals=0
         ),
-    )(*(pltpu.with_memory_space_constraint(x, VMEM) for x in (tiles, table)), *fields)
+    )(pltpu.with_memory_space_constraint(tiles, VMEM), pltpu.with_memory_space_constraint(table, SMEM), *fields)
 
 
 def local(nrow, ncol, tiles, tile_rows, tile_cols, tile_count, degree, labels):
@@ -159,10 +161,13 @@
     for step in range(ITERS):
         if step > 0:
             own = (field * scale[:, None, :]).astype(jnp.bfloat16)
-        near = [own] + [from_row(own, 2 * m) for m in range(1, nz)]
         if step == 0:
-            near[-1], table = lax.optimization_barrier((near[-1], table))
-        fields = near + [from_row(x, 1) for x in near]
+            own = lax.optimization_barrier(own)
+            both = jnp.stack([own, from_row(own, 1)])
+            fields = [both] + [from_row(both, 2 * m) for m in range(1, nz)]
+        else:
+            near = [own] + [from_row(own, 2 * m) for m in range(1, nz)]
+            fields = near + [from_row(x, 1) for x in near]
         outs = spread_call(step == 0, nrow, ncol, blk, tiles, table, fields)
         summed = outs[0]
         for k in range(1, ncol):

time: 52.7 us -> 49.3 us (0.935)
  waiting for transfers between devices: 24.5 us -> 22.1 us
  Pallas kernels: 6.88 us -> 6.08 us
    ppermute x6, waiting for transfers between devices: 12.6 us -> 11.2 us  [from_col(): return lax.ppermute(x, 'col', [(i, i ^ k) for i in range(ncol)])]
    ppermute x14 -> x11, waiting for transfers between devices: 11.9 us -> 10.9 us  [from_row(): return lax.ppermute(x, 'row', [(i, i ^ d) for i in range(nrow)])]
    pallas_call x2, Pallas kernels: 4.61 us -> 3.79 us  [spread_call(): pl.pallas_call(functools.partial(spread, seeded, nrow, ncol, blk), out_sh...]
    ppermute x14 -> x11, starting transfers between devices: 11.2 us -> 11.1 us  [from_row(): return lax.ppermute(x, 'row', [(i, i ^ d) for i in range(nrow)])]
  transfers between devices with their start and end apart: 20 -> 17, of which waited for: 12 -> 10; matrix products, arithmetic and copies ran while one was open for 0% -> 0% of each run, Pallas kernels for 4% -> 5%
where the time goes in v5:
time: 49.3 us; the launch traced here: 48.8 us
  waiting for transfers between devices  22.1 us (45%)
  starting transfers between devices  18.2 us (37%)
  Pallas kernels  6.08 us (12%)
  other arithmetic  1.74 us (4%)
  between operations  0.73 us (1%)
    ppermute x6, waiting for transfers between devices, from_col(): return lax.ppermute(x, 'col', [(i, i ^ k) for i in range(ncol)])  11.2 us
    ppermute x11, starting transfers between devices, from_row(): return lax.ppermute(x, 'row', [(i, i ^ d) for i in range(nrow)])  11.1 us
    ppermute x11, waiting for transfers between devices, from_row(): return lax.ppermute(x, 'row', [(i, i ^ d) for i in range(nrow)])  10.9 us
    ppermute x6, starting transfers between devices, from_col(): return lax.ppermute(x, 'col', [(i, i ^ k) for i in range(ncol)])  7.11 us
    pallas_call x2, Pallas kernels, spread_call(): pl.pallas_call(functools.partial(spread, seeded, nrow, ncol, blk), out_sh...  3.79 us
    pallas_call x1, Pallas kernels, fetch_call(): pl.pallas_call(functools.partial(fetch, nrow, ncol, blk), out_shape=[VMEM...  2.29 us
  transfers between devices with their start and end apart: 17, of which 10 were waited for; matrix products, arithmetic and copies ran while one was open for 0% of the time, Pallas kernels for 5%

profile of v5, /device:TPU:0, one launch (start us, length us, event | category | flops | bytes accessed | tf_op | source)
XLA Modules:
  0.0 48.8 jit_solution(6776072649300349754)
XLA Ops:
  0.0 0.8 %fusion.2 = bf16[2,32,128]{2,1,0:T(8,128)(2,1)S(1)} fusion(s32[32,128]{1,0:T(8,128)} %param.10, s32[32,128]{1,0:T(8,128)} %param.11, pred[2]{0:T(512)(128)(4,1)S(1)} %iota_compare_fusion.1), kind=kLoop, calls=%fused_computation.6 | loop fusion | flops 32768 | bytes 49154 | tf_op jit(solution)/shard_map/convert_element_type | solution.py:159
  0.8 0.5 %collective-permute-start = (bf16[2,32,128]{2,1,0:T(8,128)(2,1)S(1)}, bf16[2,32,128]{2,1,0:T(8,128)(2,1)S(1)}, u32[]{:S(2)}, u32[]{:S(2)}) collective-permute-start(bf16[2,32,128]{2,1,0:T(8,128)(2,1)S(1)} %fusion.2), channel_id=1, source_target_pairs={{0,4},{4,0},{8,12},{12,8},{16,20},{20,16},{24,28},{28,24},{1,5},{5... | collective-permute-start | bytes 49160 | tf_op jit(solution)/shard_map/ppermute | solution.py:149
  1.3 0.8 %collective-permute-done = bf16[2,32,128]{2,1,0:T(8,128)(2,1)S(1)} collective-permute-done((bf16[2,32,128]{2,1,0:T(8,128)(2,1)S(1)}, bf16[2,32,128]{2,1,0:T(8,128)(2,1)S(1)}, u32[]{:S(2)}, u32[]{:S(2)}) %collective-permute-start) | collective-permute-done | bytes 16416 | tf_op jit(solution)/shard_map/ppermute | solution.py:149
  2.2 4.9 %collective-permute-start.3 = (bf16[2,2,32,128]{3,2,1,0:T(8,128)(2,1)S(1)}, bf16[2,2,32,128]{3,2,1,0:T(8,128)(2,1)S(1)}, u32[]{:S(2)}, u32[]{:S(2)}) collective-permute-start(bf16[2,2,32,128]{3,2,1,0:T(8,128)(2,1)S(1)} %pad_maximum_fusion.refs_2_), channel_id=1, source_target_pairs={{0,24},{4,28},{8,16},{12,20},{16,8},{20,12},{24,0},{28,4},{1,25},{... | collective-permute-start | bytes 98312 | tf_op jit(solution)/shard_map/ppermute | solution.py:149
  7.1 0.0 collective-permute-start.2
  7.1 0.6 %collective-permute-start.1 = (bf16[2,2,32,128]{3,2,1,0:T(8,128)(2,1)S(1)}, bf16[2,2,32,128]{3,2,1,0:T(8,128)(2,1)S(1)}, u32[]{:S(2)}, u32[]{:S(2)}) collective-permute-start(bf16[2,2,32,128]{3,2,1,0:T(8,128)(2,1)S(1)} %pad_maximum_fusion.refs_2_), channel_id=1, source_target_pairs={{0,8},{4,12},{8,0},{12,4},{16,24},{20,28},{24,16},{28,20},{1,9},{5... | collective-permute-start | bytes 98312 | tf_op jit(solution)/shard_map/ppermute | solution.py:149
  8.4 0.0 copy-start.1
  8.4 0.0 copy-start
  8.4 2.3 %shard_map.64 = (bf16[128,128,128]{2,1,0:T(8,128)(2,1)S(1)}, s32[2,128]{1,0:T(2,128)S(4)}) custom-call(bf16[128,128,128]{2,1,0:T(8,128)(2,1)} %tiles_hbm.1, s32[1,128]{1,0:T(1,128)} %bitcast.6, s32[1,128]{1,0:T(1,128)} %bitcast.7, s32[1]{0:T(128)S(6)} %copy.7.count), custom_call_target="tpu_custom_call" | custom-call | bytes 4194304 | tf_op jit(solution)/shard_map/pallas_call | solution.py:110
  10.7 0.0 collective-permute-done.3.refs_5_
  10.8 1.2 %collective-permute-done.2.refs_4_ = bf16[2,2,32,128]{3,2,1,0:T(8,128)(2,1)S(1)} collective-permute-done((bf16[2,2,32,128]{3,2,1,0:T(8,128)(2,1)S(1)}, bf16[2,2,32,128]{3,2,1,0:T(8,128)(2,1)S(1)}, u32[]{:S(2)}, u32[]{:S(2)}) %collective-permute-start.2) | collective-permute-done | bytes 32800 | tf_op jit(solution)/shard_map/ppermute | solution.py:149
  11.9 0.0 collective-permute-done.1.refs_3_
  11.9 1.9 %shard_map.65 = (f32[32,16,128]{2,1,0:T(8,128)S(1)}, bf16[32,16,128]{2,1,0:T(8,128)(2,1)S(1)}, bf16[32,16,128]{2,1,0:T(8,128)(2,1)S(1)}, bf16[32,16,128]{2,1,0:T(8,128)(2,1)S(1)}) custom-call(bf16[128,128,128]{2,1,0:T(8,128)(2,1)S(1)} %get-tuple-element.15.refs_0_, s32[2,128]{1,0:T(2,128)S(4)} %get-tuple-element.16.refs_1_, ...), custom_call_target="tpu_custom_call" | custom-call | flops 67108864 | bytes 5242880 | tf_op jit(solution)/shard_map/pallas_call | solution.py:126
  13.8 1.5 %collective-permute-start.4 = (bf16[32,16,128]{2,1,0:T(8,128)(2,1)S(1)}, bf16[32,16,128]{2,1,0:T(8,128)(2,1)S(1)}, u32[]{:S(2)}, u32[]{:S(2)}) collective-permute-start(bf16[32,16,128]{2,1,0:T(8,128)(2,1)S(1)} %get-tuple-element.18), channel_id=1, source_target_pairs={{0,1},{1,0},{2,3},{3,2},{4,5},{5,4},{6,7},{7,6},{8,9},{9,8},{10,11... | collective-permute-start | bytes 393224 | tf_op jit(solution)/shard_map/ppermute | solution.py:152
  15.4 1.5 %collective-permute-start.5 = (bf16[32,16,128]{2,1,0:T(8,128)(2,1)S(1)}, bf16[32,16,128]{2,1,0:T(8,128)(2,1)S(1)}, u32[]{:S(2)}, u32[]{:S(2)}) collective-permute-start(bf16[32,16,128]{2,1,0:T(8,128)(2,1)S(1)} %get-tuple-element.19), channel_id=1, source_target_pairs={{0,2},{1,3},{2,0},{3,1},{4,6},{5,7},{6,4},{7,5},{8,10},{9,11},{10,... | collective-permute-start | bytes 393224 | tf_op jit(solution)/shard_map/ppermute | solution.py:152
  16.9 0.5 %collective-permute-start.6 = (bf16[32,16,128]{2,1,0:T(8,128)(2,1)S(1)}, bf16[32,16,128]{2,1,0:T(8,128)(2,1)S(1)}, u32[]{:S(2)}, u32[]{:S(2)}) collective-permute-start(bf16[32,16,128]{2,1,0:T(8,128)(2,1)S(1)} %get-tuple-element.20), channel_id=1, source_target_pairs={{0,3},{1,2},{2,1},{3,0},{4,7},{5,6},{6,5},{7,4},{8,11},{9,10},{10,... | collective-permute-start | bytes 393224 | tf_op jit(solution)/shard_map/ppermute | solution.py:152
  17.4 0.0 copy-done.1
  17.4 2.4 %collective-permute-done.4 = bf16[32,16,128]{2,1,0:T(8,128)(2,1)S(1)} collective-permute-done((bf16[32,16,128]{2,1,0:T(8,128)(2,1)S(1)}, bf16[32,16,128]{2,1,0:T(8,128)(2,1)S(1)}, u32[]{:S(2)}, u32[]{:S(2)}) %collective-permute-start.4) | collective-permute-done | bytes 131104 | tf_op jit(solution)/shard_map/ppermute | solution.py:152
  19.8 3.3 %collective-permute-done.5 = bf16[32,16,128]{2,1,0:T(8,128)(2,1)S(1)} collective-permute-done((bf16[32,16,128]{2,1,0:T(8,128)(2,1)S(1)}, bf16[32,16,128]{2,1,0:T(8,128)(2,1)S(1)}, u32[]{:S(2)}, u32[]{:S(2)}) %collective-permute-start.5) | collective-permute-done | bytes 131104 | tf_op jit(solution)/shard_map/ppermute | solution.py:152
  23.1 0.0 collective-permute-done.6
  23.1 0.0 copy-done
  23.1 0.1 fusion.1.refs_2_
  23.2 2.7 %collective-permute-start.9 = (bf16[32,16,128]{2,1,0:T(8,128)(2,1)S(1)}, bf16[32,16,128]{2,1,0:T(8,128)(2,1)S(1)}, u32[]{:S(2)}, u32[]{:S(2)}) collective-permute-start(bf16[32,16,128]{2,1,0:T(8,128)(2,1)S(1)} %fusion.1.refs_2_), channel_id=1, source_target_pairs={{0,24},{4,28},{8,16},{12,20},{16,8},{20,12},{24,0},{28,4},{1,25},{... | collective-permute-start | bytes 393224 | tf_op jit(solution)/shard_map/ppermute | solution.py:149
  25.9 0.0 collective-permute-start.8
  25.9 1.8 %collective-permute-start.7 = (bf16[32,16,128]{2,1,0:T(8,128)(2,1)S(1)}, bf16[32,16,128]{2,1,0:T(8,128)(2,1)S(1)}, u32[]{:S(2)}, u32[]{:S(2)}) collective-permute-start(bf16[32,16,128]{2,1,0:T(8,128)(2,1)S(1)} %fusion.1.refs_2_), channel_id=1, source_target_pairs={{0,8},{4,12},{8,0},{12,4},{16,24},{20,28},{24,16},{28,20},{1,9},{5... | collective-permute-start | bytes 393224 | tf_op jit(solution)/shard_map/ppermute | solution.py:149
  27.7 0.0 collective-permute-start.10
  27.7 3.6 %collective-permute-done.9.refs_5_ = bf16[32,16,128]{2,1,0:T(8,128)(2,1)S(1)} collective-permute-done((bf16[32,16,128]{2,1,0:T(8,128)(2,1)S(1)}, bf16[32,16,128]{2,1,0:T(8,128)(2,1)S(1)}, u32[]{:S(2)}, u32[]{:S(2)}) %collective-permute-start.9) | collective-permute-done | bytes 131104 | tf_op jit(solution)/shard_map/ppermute | solution.py:149
  31.3 0.0 collective-permute-start.13
  31.3 4.2 %collective-permute-done.8.refs_4_ = bf16[32,16,128]{2,1,0:T(8,128)(2,1)S(1)} collective-permute-done((bf16[32,16,128]{2,1,0:T(8,128)(2,1)S(1)}, bf16[32,16,128]{2,1,0:T(8,128)(2,1)S(1)}, u32[]{:S(2)}, u32[]{:S(2)}) %collective-permute-start.8) | collective-permute-done | bytes 131104 | tf_op jit(solution)/shard_map/ppermute | solution.py:149
  35.5 0.0 collective-permute-start.12
  35.5 0.0 collective-permute-done.7.refs_3_
  35.5 0.5 %collective-permute-start.11 = (bf16[32,16,128]{2,1,0:T(8,128)(2,1)S(1)}, bf16[32,16,128]{2,1,0:T(8,128)(2,1)S(1)}, u32[]{:S(2)}, u32[]{:S(2)}) collective-permute-start(bf16[32,16,128]{2,1,0:T(8,128)(2,1)S(1)} %collective-permute-done.7.refs_3_), channel_id=1, source_target_pairs={{0,4},{4,0},{8,12},{12,8},{16,20},{20,16},{24,28},{28,24},{1,5},{5... | collective-permute-start | bytes 393224 | tf_op jit(solution)/shard_map/ppermute | solution.py:149
  36.0 0.0 collective-permute-done.10.refs_6_
  36.0 0.0 collective-permute-done.13.refs_9_
  36.0 0.8 %collective-permute-done.12.refs_8_ = bf16[32,16,128]{2,1,0:T(8,128)(2,1)S(1)} collective-permute-done((bf16[32,16,128]{2,1,0:T(8,128)(2,1)S(1)}, bf16[32,16,128]{2,1,0:T(8,128)(2,1)S(1)}, u32[]{:S(2)}, u32[]{:S(2)}) %collective-permute-start.12) | collective-permute-done | bytes 131104 | tf_op jit(solution)/shard_map/ppermute | solution.py:149
  36.8 0.2 collective-permute-done.11.refs_7_
  37.0 1.9 %shard_map.66 = (f32[32,16,128]{2,1,0:T(8,128)S(1)}, bf16[32,16,128]{2,1,0:T(8,128)(2,1)S(1)}, bf16[32,16,128]{2,1,0:T(8,128)(2,1)S(1)}, bf16[32,16,128]{2,1,0:T(8,128)(2,1)S(1)}) custom-call(bf16[128,128,128]{2,1,0:T(8,128)(2,1)S(1)} %get-tuple-element.15.refs_0_, s32[2,128]{1,0:T(2,128)S(4)} %get-tuple-element.16.refs_1_, ...), custom_call_target="tpu_custom_call" | custom-call | flops 67108864 | bytes 5242880 | tf_op jit(solution)/shard_map/pallas_call | solution.py:126
  38.9 0.8 %collective-permute-start.14 = (bf16[32,16,128]{2,1,0:T(8,128)(2,1)S(1)}, bf16[32,16,128]{2,1,0:T(8,128)(2,1)S(1)}, u32[]{:S(2)}, u32[]{:S(2)}) collective-permute-start(bf16[32,16,128]{2,1,0:T(8,128)(2,1)S(1)} %get-tuple-element.22), channel_id=1, source_target_pairs={{0,1},{1,0},{2,3},{3,2},{4,5},{5,4},{6,7},{7,6},{8,9},{9,8},{10,11... | collective-permute-start | bytes 393224 | tf_op jit(solution)/shard_map/ppermute | solution.py:152
  39.8 0.7 %collective-permute-start.15 = (bf16[32,16,128]{2,1,0:T(8,128)(2,1)S(1)}, bf16[32,16,128]{2,1,0:T(8,128)(2,1)S(1)}, u32[]{:S(2)}, u32[]{:S(2)}) collective-permute-start(bf16[32,16,128]{2,1,0:T(8,128)(2,1)S(1)} %get-tuple-element.23), channel_id=1, source_target_pairs={{0,2},{1,3},{2,0},{3,1},{4,6},{5,7},{6,4},{7,5},{8,10},{9,11},{10,... | collective-permute-start | bytes 393224 | tf_op jit(solution)/shard_map/ppermute | solution.py:152
  40.5 2.0 %collective-permute-start.16 = (bf16[32,16,128]{2,1,0:T(8,128)(2,1)S(1)}, bf16[32,16,128]{2,1,0:T(8,128)(2,1)S(1)}, u32[]{:S(2)}, u32[]{:S(2)}) collective-permute-start(bf16[32,16,128]{2,1,0:T(8,128)(2,1)S(1)} %get-tuple-element.24), channel_id=1, source_target_pairs={{0,3},{1,2},{2,1},{3,0},{4,7},{5,6},{6,5},{7,4},{8,11},{9,10},{10,... | collective-permute-start | bytes 393224 | tf_op jit(solution)/shard_map/ppermute | solution.py:152
  42.5 2.8 %collective-permute-done.14 = bf16[32,16,128]{2,1,0:T(8,128)(2,1)S(1)} collective-permute-done((bf16[32,16,128]{2,1,0:T(8,128)(2,1)S(1)}, bf16[32,16,128]{2,1,0:T(8,128)(2,1)S(1)}, u32[]{:S(2)}, u32[]{:S(2)}) %collective-permute-start.14) | collective-permute-done | bytes 131104 | tf_op jit(solution)/shard_map/ppermute | solution.py:152
  45.3 2.7 %collective-permute-done.15 = bf16[32,16,128]{2,1,0:T(8,128)(2,1)S(1)} collective-permute-done((bf16[32,16,128]{2,1,0:T(8,128)(2,1)S(1)}, bf16[32,16,128]{2,1,0:T(8,128)(2,1)S(1)}, u32[]{:S(2)}, u32[]{:S(2)}) %collective-permute-start.15) | collective-permute-done | bytes 131104 | tf_op jit(solution)/shard_map/ppermute | solution.py:152
  48.0 0.0 collective-permute-done.16
  48.0 0.8 %select_add_fusion = f32[32,16,128]{2,1,0:T(8,128)} fusion(bf16[32,16,128]{2,1,0:T(8,128)(2,1)S(1)} %collective-permute-done.16, bf16[32,16,128]{2,1,0:T(8,128)(2,1)S(1)} %collective-permute-done.15, f32[32,16,128]{2,1,0:T(8,128)S(1)} %get-tuple-element.21, bf16[32,16,128]{2,1,0:T(8,128)(2,1)S(1)} %collective-permute-done.14, s32[32,128]{1,0:T(8,128)S(1)} %copy-done, ...), kind=kLoop, calls=%fused_computation | loop fusion | flops 655360 | bytes 950272 | tf_op jit(solution)/shard_map/add | solution.py:175
  (3 shorter events, 0.0 us)
Async XLA Ops:
  0.8 1.4 %collective-permute-start = (bf16[2,32,128]{2,1,0:T(8,128)(2,1)S(1)}, bf16[2,32,128]{2,1,0:T(8,128)(2,1)S(1)}, u32[]{:S(2)}, u32[]{:S(2)}) collective-permute-start(bf16[2,32,128]{2,1,0:T(8,128)(2,1)S(1)} %fusion.2), channel_id=1, source_target_pairs={{0,4},{4,0},{8,12},{12,8},{16,20},{20,16},{24,28},{28,24},{1,5},{5... | collective-permute-start | bytes 49160 | tf_op jit(solution)/shard_map/ppermute | solution.py:149
  2.2 8.6 %collective-permute-start.3 = (bf16[2,2,32,128]{3,2,1,0:T(8,128)(2,1)S(1)}, bf16[2,2,32,128]{3,2,1,0:T(8,128)(2,1)S(1)}, u32[]{:S(2)}, u32[]{:S(2)}) collective-permute-start(bf16[2,2,32,128]{3,2,1,0:T(8,128)(2,1)S(1)} %pad_maximum_fusion.refs_2_), channel_id=1, source_target_pairs={{0,24},{4,28},{8,16},{12,20},{16,8},{20,12},{24,0},{28,4},{1,25},{... | collective-permute-start | bytes 98312 | tf_op jit(solution)/shard_map/ppermute | solution.py:149
  7.1 4.8 %collective-permute-start.2 = (bf16[2,2,32,128]{3,2,1,0:T(8,128)(2,1)S(1)}, bf16[2,2,32,128]{3,2,1,0:T(8,128)(2,1)S(1)}, u32[]{:S(2)}, u32[]{:S(2)}) collective-permute-start(bf16[2,2,32,128]{3,2,1,0:T(8,128)(2,1)S(1)} %pad_maximum_fusion.refs_2_), channel_id=1, source_target_pairs={{0,16},{4,20},{8,24},{12,28},{16,0},{20,4},{24,8},{28,12},{1,17},{... | collective-permute-start | bytes 98312 | tf_op jit(solution)/shard_map/ppermute | solution.py:149
  7.1 4.8 %collective-permute-start.1 = (bf16[2,2,32,128]{3,2,1,0:T(8,128)(2,1)S(1)}, bf16[2,2,32,128]{3,2,1,0:T(8,128)(2,1)S(1)}, u32[]{:S(2)}, u32[]{:S(2)}) collective-permute-start(bf16[2,2,32,128]{3,2,1,0:T(8,128)(2,1)S(1)} %pad_maximum_fusion.refs_2_), channel_id=1, source_target_pairs={{0,8},{4,12},{8,0},{12,4},{16,24},{20,28},{24,16},{28,20},{1,9},{5... | collective-permute-start | bytes 98312 | tf_op jit(solution)/shard_map/ppermute | solution.py:149
  8.4 9.0 %copy-start.1 = (s32[32,128]{1,0:T(8,128)S(1)}, s32[32,128]{1,0:T(8,128)}, u32[]{:S(2)}) copy-start(s32[32,128]{1,0:T(8,128)} %param.10) | copy-start | bytes 49156
  8.4 14.7 %copy-start = (s32[32,128]{1,0:T(8,128)S(1)}, s32[32,128]{1,0:T(8,128)}, u32[]{:S(2)}) copy-start(s32[32,128]{1,0:T(8,128)} %param.11) | copy-start | bytes 49156
  13.8 6.0 %collective-permute-start.4 = (bf16[32,16,128]{2,1,0:T(8,128)(2,1)S(1)}, bf16[32,16,128]{2,1,0:T(8,128)(2,1)S(1)}, u32[]{:S(2)}, u32[]{:S(2)}) collective-permute-start(bf16[32,16,128]{2,1,0:T(8,128)(2,1)S(1)} %get-tuple-element.18), channel_id=1, source_target_pairs={{0,1},{1,0},{2,3},{3,2},{4,5},{5,4},{6,7},{7,6},{8,9},{9,8},{10,11... | collective-permute-start | bytes 393224 | tf_op jit(solution)/shard_map/ppermute | solution.py:152
  15.4 7.7 %collective-permute-start.5 = (bf16[32,16,128]{2,1,0:T(8,128)(2,1)S(1)}, bf16[32,16,128]{2,1,0:T(8,128)(2,1)S(1)}, u32[]{:S(2)}, u32[]{:S(2)}) collective-permute-start(bf16[32,16,128]{2,1,0:T(8,128)(2,1)S(1)} %get-tuple-element.19), channel_id=1, source_target_pairs={{0,2},{1,3},{2,0},{3,1},{4,6},{5,7},{6,4},{7,5},{8,10},{9,11},{10,... | collective-permute-start | bytes 393224 | tf_op jit(solution)/shard_map/ppermute | solution.py:152
  16.9 6.3 %collective-permute-start.6 = (bf16[32,16,128]{2,1,0:T(8,128)(2,1)S(1)}, bf16[32,16,128]{2,1,0:T(8,128)(2,1)S(1)}, u32[]{:S(2)}, u32[]{:S(2)}) collective-permute-start(bf16[32,16,128]{2,1,0:T(8,128)(2,1)S(1)} %get-tuple-element.20), channel_id=1, source_target_pairs={{0,3},{1,2},{2,1},{3,0},{4,7},{5,6},{6,5},{7,4},{8,11},{9,10},{10,... | collective-permute-start | bytes 393224 | tf_op jit(solution)/shard_map/ppermute | solution.py:152
  23.2 8.1 %collective-permute-start.9 = (bf16[32,16,128]{2,1,0:T(8,128)(2,1)S(1)}, bf16[32,16,128]{2,1,0:T(8,128)(2,1)S(1)}, u32[]{:S(2)}, u32[]{:S(2)}) collective-permute-start(bf16[32,16,128]{2,1,0:T(8,128)(2,1)S(1)} %fusion.1.refs_2_), channel_id=1, source_target_pairs={{0,24},{4,28},{8,16},{12,20},{16,8},{20,12},{24,0},{28,4},{1,25},{... | collective-permute-start | bytes 393224 | tf_op jit(solution)/shard_map/ppermute | solution.py:149
  25.9 9.6 %collective-permute-start.8 = (bf16[32,16,128]{2,1,0:T(8,128)(2,1)S(1)}, bf16[32,16,128]{2,1,0:T(8,128)(2,1)S(1)}, u32[]{:S(2)}, u32[]{:S(2)}) collective-permute-start(bf16[32,16,128]{2,1,0:T(8,128)(2,1)S(1)} %fusion.1.refs_2_), channel_id=1, source_target_pairs={{0,16},{4,20},{8,24},{12,28},{16,0},{20,4},{24,8},{28,12},{1,17},{... | collective-permute-start | bytes 393224 | tf_op jit(solution)/shard_map/ppermute | solution.py:149
  25.9 9.6 %collective-permute-start.7 = (bf16[32,16,128]{2,1,0:T(8,128)(2,1)S(1)}, bf16[32,16,128]{2,1,0:T(8,128)(2,1)S(1)}, u32[]{:S(2)}, u32[]{:S(2)}) collective-permute-start(bf16[32,16,128]{2,1,0:T(8,128)(2,1)S(1)} %fusion.1.refs_2_), channel_id=1, source_target_pairs={{0,8},{4,12},{8,0},{12,4},{16,24},{20,28},{24,16},{28,20},{1,9},{5... | collective-permute-start | bytes 393224 | tf_op jit(solution)/shard_map/ppermute | solution.py:149
  27.7 8.3 %collective-permute-start.10 = (bf16[32,16,128]{2,1,0:T(8,128)(2,1)S(1)}, bf16[32,16,128]{2,1,0:T(8,128)(2,1)S(1)}, u32[]{:S(2)}, u32[]{:S(2)}) collective-permute-start(bf16[32,16,128]{2,1,0:T(8,128)(2,1)S(1)} %fusion.1.refs_2_), channel_id=1, source_target_pairs={{0,4},{4,0},{8,12},{12,8},{16,20},{20,16},{24,28},{28,24},{1,5},{5... | collective-permute-start | bytes 393224 | tf_op jit(solution)/shard_map/ppermute | solution.py:149
  31.3 4.7 %collective-permute-start.13 = (bf16[32,16,128]{2,1,0:T(8,128)(2,1)S(1)}, bf16[32,16,128]{2,1,0:T(8,128)(2,1)S(1)}, u32[]{:S(2)}, u32[]{:S(2)}) collective-permute-start(bf16[32,16,128]{2,1,0:T(8,128)(2,1)S(1)} %collective-permute-done.9.refs_5_), channel_id=1, source_target_pairs={{0,4},{4,0},{8,12},{12,8},{16,20},{20,16},{24,28},{28,24},{1,5},{5... | collective-permute-start | bytes 393224 | tf_op jit(solution)/shard_map/ppermute | solution.py:149
  35.5 1.3 %collective-permute-start.12 = (bf16[32,16,128]{2,1,0:T(8,128)(2,1)S(1)}, bf16[32,16,128]{2,1,0:T(8,128)(2,1)S(1)}, u32[]{:S(2)}, u32[]{:S(2)}) collective-permute-start(bf16[32,16,128]{2,1,0:T(8,128)(2,1)S(1)} %collective-permute-done.8.refs_4_), channel_id=1, source_target_pairs={{0,4},{4,0},{8,12},{12,8},{16,20},{20,16},{24,28},{28,24},{1,5},{5... | collective-permute-start | bytes 393224 | tf_op jit(solution)/shard_map/ppermute | solution.py:149
  35.5 1.5 %collective-permute-start.11 = (bf16[32,16,128]{2,1,0:T(8,128)(2,1)S(1)}, bf16[32,16,128]{2,1,0:T(8,128)(2,1)S(1)}, u32[]{:S(2)}, u32[]{:S(2)}) collective-permute-start(bf16[32,16,128]{2,1,0:T(8,128)(2,1)S(1)} %collective-permute-done.7.refs_3_), channel_id=1, source_target_pairs={{0,4},{4,0},{8,12},{12,8},{16,20},{20,16},{24,28},{28,24},{1,5},{5... | collective-permute-start | bytes 393224 | tf_op jit(solution)/shard_map/ppermute | solution.py:149
  38.9 6.4 %collective-permute-start.14 = (bf16[32,16,128]{2,1,0:T(8,128)(2,1)S(1)}, bf16[32,16,128]{2,1,0:T(8,128)(2,1)S(1)}, u32[]{:S(2)}, u32[]{:S(2)}) collective-permute-start(bf16[32,16,128]{2,1,0:T(8,128)(2,1)S(1)} %get-tuple-element.22), channel_id=1, source_target_pairs={{0,1},{1,0},{2,3},{3,2},{4,5},{5,4},{6,7},{7,6},{8,9},{9,8},{10,11... | collective-permute-start | bytes 393224 | tf_op jit(solution)/shard_map/ppermute | solution.py:152
  39.8 8.3 %collective-permute-start.15 = (bf16[32,16,128]{2,1,0:T(8,128)(2,1)S(1)}, bf16[32,16,128]{2,1,0:T(8,128)(2,1)S(1)}, u32[]{:S(2)}, u32[]{:S(2)}) collective-permute-start(bf16[32,16,128]{2,1,0:T(8,128)(2,1)S(1)} %get-tuple-element.23), channel_id=1, source_target_pairs={{0,2},{1,3},{2,0},{3,1},{4,6},{5,7},{6,4},{7,5},{8,10},{9,11},{10,... | collective-permute-start | bytes 393224 | tf_op jit(solution)/shard_map/ppermute | solution.py:152
  40.5 7.5 %collective-permute-start.16 = (bf16[32,16,128]{2,1,0:T(8,128)(2,1)S(1)}, bf16[32,16,128]{2,1,0:T(8,128)(2,1)S(1)}, u32[]{:S(2)}, u32[]{:S(2)}) collective-permute-start(bf16[32,16,128]{2,1,0:T(8,128)(2,1)S(1)} %get-tuple-element.24), channel_id=1, source_target_pairs={{0,3},{1,2},{2,1},{3,0},{4,7},{5,6},{6,5},{7,4},{8,11},{9,10},{10,... | collective-permute-start | bytes 393224 | tf_op jit(solution)/shard_map/ppermute | solution.py:152

commit v6 on v5

v6 whole, which is shorter than its diff:
```python
import functools

import jax
import jax.numpy as jnp
from jax import lax
from jax.experimental import pallas as pl
from jax.experimental.pallas import tpu as pltpu
from jax.sharding import PartitionSpec as P

QC = 16
ITERS = 2
COPIES = 8
UNROLL = 32

HBM = pltpu.HBM
VMEM = pltpu.VMEM
SMEM = pltpu.SMEM


def div(value, size):
    if size & (size - 1) == 0:
        return lax.shift_right_logical(value, jnp.full_like(value, size.bit_length() - 1))
    return lax.div(value, jnp.full_like(value, size))


def parts_of(ncol):
    far = max(1, ncol // 4)
    return [(ncol - far, ncol), (1, ncol - far), (0, 1)]


def fetch(nrow, ncol, blk, tiles_hbm, rows_hbm, cols_hbm, count, tiles, table_out, rows, cols, table, sem):
    nt = tiles.shape[0]
    part = nt // COPIES

    def copy(i):
        some = pl.ds(i * part, part)
        return pltpu.make_async_copy(tiles_hbm.at[some], tiles.at[some], sem.at[i])

    tables = [
        pltpu.make_async_copy(source, target, sem.at[COPIES + i])
        for i, (source, target) in enumerate(((rows_hbm, rows), (cols_hbm, cols)))
    ]
    for c in tables:
        c.start()
    for i in range(COPIES):
        copy(i).start()
    for c in tables:
        c.wait()
    row_pos, col_pos = lax.axis_index("row"), lax.axis_index("col")
    col = cols[...]
    owner = div(col, blk)
    far = div(owner, ncol) ^ row_pos
    slot = (far & 1) * (nrow // 2) + div(far, 2)
    place = slot * blk + col - owner * blk
    row = rows[...] - row_pos * (blk * ncol)
    target = div(row, blk)
    slice_ = target ^ col_pos
    row = row - target * blk + slice_ * blk
    parts = parts_of(ncol)
    key = sum((slice_ < low).astype(jnp.int32) for low, _ in parts[:-1])
    lane = lax.broadcasted_iota(jnp.int32, (1, nt), 1)
    key = jnp.where(lane < count[0], key, len(parts)).astype(jnp.float32)
    across = lax.broadcasted_iota(jnp.int32, (nt, nt), 1).astype(jnp.float32)
    down = lax.broadcasted_iota(jnp.int32, (nt, nt), 0).astype(jnp.float32)
    same = across == down

    def stand(x):
        return jnp.sum(jnp.where(same, jnp.broadcast_to(x.astype(jnp.float32), (nt, nt)), 0.0), 1, keepdims=True)

    key_down = stand(key)
    ahead = (key < key_down) | ((key == key_down) & (across < down))
    rank = jnp.sum(jnp.where(ahead, 1.0, 0.0), 1, keepdims=True)
    chosen = rank == across

    def pull(x):
        return jnp.sum(jnp.where(chosen, x, 0.0), 0, keepdims=True).astype(jnp.int32)

    table[...] = jnp.zeros_like(table)
    table[pl.ds(0, 1), pl.ds(0, nt)] = pull(stand(place))
    table[pl.ds(1, 1), pl.ds(0, nt)] = pull(stand(row))
    table[pl.ds(2, 1), pl.ds(0, nt)] = pull(down)
    table[pl.ds(3, 1), pl.ds(0, nt)] = jnp.sum(
        jnp.where(key_down < across, 1.0, 0.0), 0, keepdims=True
    ).astype(jnp.int32)
    out = pltpu.make_async_copy(table, table_out, sem.at[COPIES + 2])
    out.start()
    for i in range(COPIES):
        copy(i).wait()
    out.wait()


def spread(seeded, first, index, part, nrow, ncol, blk, *refs):
    low, high = part
    tiles, table, refs = refs[0], refs[1], refs[2:]
    if first:
        nfields = nrow // 2 if seeded else nrow
        fields, refs = refs[:nfields], refs[nfields:]
    else:
        picks, refs = refs[0], refs[1:]
    outs, refs = refs[: high - low], refs[high - low :]
    if first:
        picks, refs = refs[0], refs[1:]
    (total,) = refs
    total[...] = jnp.zeros_like(total)
    if first and seeded:
        for i, f in enumerate(fields):
            for half in range(2):
                for kind in range(2):
                    place = (half * len(fields) + i) * blk
                    picks[kind, pl.ds(place, blk), :] = f[half, kind].astype(jnp.float32)
    elif first:
        for i, f in enumerate(fields):
            picks[pl.ds(i * blk, blk)] = f[...]
    query = lax.broadcasted_iota(jnp.int32, (QC, 128), 0).astype(jnp.float32)
    begin, end = table[3, index], table[3, index + 1]

    def pick(t):
        place = table[0, t]
        if seeded:
            label = picks[0, pl.ds(place, 1), :]
            scale = picks[1, pl.ds(place, 1), :]
            return jnp.where(label == query, scale, 0.0).astype(jnp.bfloat16)
        return picks[place]

    def step(i, carry):
        base = begin + i * UNROLL
        terms = []
        for u in range(0, UNROLL, 2):
            t = base + u
            pair = lax.dot_general(
                jnp.concatenate([pick(t), pick(t + 1)], 0),
                jnp.concatenate([tiles[table[2, t]], tiles[table[2, t + 1]]], 0),
                (((1,), (1,)), ((), ())),
                preferred_element_type=jnp.float32,
            )
            terms += [pair[:QC, :128], pair[QC:, 128:]]
        for u in range(UNROLL):
            t = base + u
            total[jnp.where(t < end, table[1, t] - low * blk, (high - low) * blk)] += terms[u]
        return carry

    lax.fori_loop(0, lax.div(end - begin + (UNROLL - 1), UNROLL), step, 0)
    for k in range(high - low):
        outs[k][...] = total[pl.ds(k * blk, blk)].astype(outs[k].dtype)


def fetch_call(nrow, ncol, blk, tiles, rows, cols, count):
    nt = tiles.shape[0]
    wide = (4, nt + 128)
    return pl.pallas_call(
        functools.partial(fetch, nrow, ncol, blk),
        out_shape=[VMEM(tiles.shape, tiles.dtype), SMEM(wide, jnp.int32)],
        in_specs=[pl.BlockSpec(memory_space=HBM)] * 3 + [pl.BlockSpec(memory_space=SMEM)],
        out_specs=[pl.BlockSpec(memory_space=VMEM), pl.BlockSpec(memory_space=SMEM)],
        scratch_shapes=[VMEM((1, nt), jnp.int32)] * 2
        + [VMEM(wide, jnp.int32), pltpu.SemaphoreType.DMA((COPIES + 3,))],
        compiler_params=pltpu.CompilerParams(vmem_limit_bytes=16 << 20),
        cost_estimate=pl.CostEstimate(flops=0, bytes_accessed=tiles.size * 2, transcendentals=0),
    )(*(pltpu.with_memory_space_constraint(x, HBM) for x in (tiles, rows.reshape(1, nt), cols.reshape(1, nt))), count)


def spread_calls(seeded, nrow, ncol, blk, tiles, table, fields):
    nt = tiles.shape[0]
    slots = nrow * blk
    shape = (blk, QC, 128)
    picks = VMEM((2, slots, 128), jnp.float32) if seeded else VMEM((slots, QC, 128), jnp.bfloat16)
    slices = [None] * ncol
    arrays = fields
    for index, (low, high) in enumerate(parts_of(ncol)):
        first = index == 0
        share = max(1, (high - low) * nt // ncol)
        results = pl.pallas_call(
            functools.partial(spread, seeded, first, index, (low, high), nrow, ncol, blk),
            out_shape=[
                jax.ShapeDtypeStruct(shape, jnp.float32 if k == 0 else jnp.bfloat16) for k in range(low, high)
            ]
            + [picks] * first,
            in_specs=[pl.BlockSpec(memory_space=VMEM), pl.BlockSpec(memory_space=SMEM)]
            + [pl.BlockSpec(memory_space=VMEM)] * len(arrays),
            out_specs=[pl.BlockSpec(memory_space=VMEM)] * (high - low + first),
            scratch_shapes=[VMEM(((high - low) * blk + 1, QC, 128), jnp.float32)],
            compiler_params=pltpu.CompilerParams(vmem_limit_bytes=24 << 20),
            cost_estimate=pl.CostEstimate(
                flops=2 * share * QC * 128 * 128, bytes_accessed=share * 128 * 256, transcendentals=0
            ),
        )(
            pltpu.with_memory_space_constraint(tiles, VMEM),
            pltpu.with_memory_space_constraint(table, SMEM),
            *arrays,
        )
        slices[low:high] = results[: high - low]
        if first:
            arrays = [pltpu.with_memory_space_constraint(results[-1], VMEM)]
    return slices


def local(nrow, ncol, tiles, tile_rows, tile_cols, tile_count, degree, labels):
    blk = labels.shape[0]
    nz = nrow // 2

    def from_row(x, d):
        return lax.ppermute(x, "row", [(i, i ^ d) for i in range(nrow)])

    def from_col(x, k):
        return lax.ppermute(x, "col", [(i, i ^ k) for i in range(ncol)])

    scale = 1.0 / jnp.sqrt(degree.astype(jnp.float32))
    qidx = jnp.arange(QC, dtype=jnp.int32)
    prior = (labels[:, None, :] == qidx[None, :, None]).astype(jnp.float32)
    kind = lax.broadcasted_iota(jnp.int32, (2, 1, 1), 0)
    raw = jnp.where(kind == 0, labels[None], degree[None]).astype(jnp.float32)
    own = jnp.where(kind == 0, raw, 1.0 / jnp.sqrt(raw)).astype(jnp.bfloat16)
    tiles, table = fetch_call(nrow, ncol, blk, tiles, tile_rows, tile_cols, tile_count)
    for step in range(ITERS):
        if step > 0:
            own = (field * scale[:, None, :]).astype(jnp.bfloat16)
        if step == 0:
            own = lax.optimization_barrier(own)
            both = jnp.stack([own, from_row(own, 1)])
            fields = [both] + [from_row(both, 2 * m) for m in range(1, nz)]
        else:
            near = [own] + [from_row(own, 2 * m) for m in range(1, nz)]
            fields = near + [from_row(x, 1) for x in near]
        outs = spread_calls(step == 0, nrow, ncol, blk, tiles, table, fields)
        summed = outs[0]
        for k in range(1, ncol):
            summed = summed + from_col(outs[k], k).astype(jnp.float32)
        field = 0.8 * scale[:, None, :] * summed + 0.2 * prior
    return field


def solution(mesh):
    nrow, ncol = mesh.shape["row"], mesh.shape["col"]
    return jax.shard_map(
        functools.partial(local, nrow, ncol),
        mesh=mesh,
        in_specs=(
            P(("row", "col"), None, None),
            P(("row", "col")),
            P(("row", "col")),
            P(("row", "col")),
            P(("row", "col"), None),
            P(("row", "col"), None),
        ),
        out_specs=P(("row", "col"), None, None),
        check_vma=False,
    )
```

time: 49.3 us -> 47.3 us (0.959)
  waiting for transfers between devices: 22.1 us -> 20 us
    ppermute x6, waiting for transfers between devices: 11.2 us -> 8.41 us  [from_col(): return lax.ppermute(x, 'col', [(i, i ^ k) for i in range(ncol)])]
    ppermute x11, waiting for transfers between devices: 10.9 us -> 11.6 us  [from_row(): return lax.ppermute(x, 'row', [(i, i ^ d) for i in range(nrow)])]
    pallas_call x2 -> x6, Pallas kernels: 3.79 us -> 3.9 us  [spread_calls(): pl.pallas_call(functools.partial(spread, seeded, first, index, (low, high...]
  transfers between devices with their start and end apart: 17 -> 17, of which waited for: 10 -> 12; matrix products, arithmetic and copies ran while one was open for 0% -> 0% of each run, Pallas kernels for 5% -> 11%
where the time goes in v6:
time: 47.3 us; the launch traced here: 47 us
  waiting for transfers between devices  20 us (42%)
  starting transfers between devices  18.3 us (39%)
  Pallas kernels  6.18 us (13%)
  other arithmetic  1.73 us (4%)
  between operations  0.75 us (2%)
    ppermute x11, waiting for transfers between devices, from_row(): return lax.ppermute(x, 'row', [(i, i ^ d) for i in range(nrow)])  11.6 us
    ppermute x11, starting transfers between devices, from_row(): return lax.ppermute(x, 'row', [(i, i ^ d) for i in range(nrow)])  11.1 us
    ppermute x6, waiting for transfers between devices, from_col(): return lax.ppermute(x, 'col', [(i, i ^ k) for i in range(ncol)])  8.41 us
    ppermute x6, starting transfers between devices, from_col(): return lax.ppermute(x, 'col', [(i, i ^ k) for i in range(ncol)])  7.26 us
    pallas_call x6, Pallas kernels, spread_calls(): pl.pallas_call(functools.partial(spread, seeded, first, index, (low, high...  3.9 us
    pallas_call x1, Pallas kernels, fetch_call(): pl.pallas_call(functools.partial(fetch, nrow, ncol, blk), out_shape=[VMEM...  2.28 us
  transfers between devices with their start and end apart: 17, of which 12 were waited for; matrix products, arithmetic and copies ran while one was open for 0% of the time, Pallas kernels for 11%

profile of v6, /device:TPU:0, one launch (start us, length us, event | category | flops | bytes accessed | tf_op | source)
XLA Modules:
  0.0 47.0 jit_solution(14091851714661603764)
XLA Ops:
  0.0 0.8 %fusion.2 = bf16[2,32,128]{2,1,0:T(8,128)(2,1)S(1)} fusion(s32[32,128]{1,0:T(8,128)} %param.10, s32[32,128]{1,0:T(8,128)} %param.11, pred[2]{0:T(512)(128)(4,1)S(1)} %iota_compare_fusion.1), kind=kLoop, calls=%fused_computation.6 | loop fusion | flops 32768 | bytes 49154 | tf_op jit(solution)/shard_map/convert_element_type | solution.py:212
  0.8 0.5 %collective-permute-start = (bf16[2,32,128]{2,1,0:T(8,128)(2,1)S(1)}, bf16[2,32,128]{2,1,0:T(8,128)(2,1)S(1)}, u32[]{:S(2)}, u32[]{:S(2)}) collective-permute-start(bf16[2,32,128]{2,1,0:T(8,128)(2,1)S(1)} %fusion.2), channel_id=1, source_target_pairs={{0,4},{4,0},{8,12},{12,8},{16,20},{20,16},{24,28},{28,24},{1,5},{5... | collective-permute-start | bytes 49160 | tf_op jit(solution)/shard_map/ppermute | solution.py:202
  1.3 0.8 %collective-permute-done = bf16[2,32,128]{2,1,0:T(8,128)(2,1)S(1)} collective-permute-done((bf16[2,32,128]{2,1,0:T(8,128)(2,1)S(1)}, bf16[2,32,128]{2,1,0:T(8,128)(2,1)S(1)}, u32[]{:S(2)}, u32[]{:S(2)}) %collective-permute-start) | collective-permute-done | bytes 16416 | tf_op jit(solution)/shard_map/ppermute | solution.py:202
  2.2 4.9 %collective-permute-start.3 = (bf16[2,2,32,128]{3,2,1,0:T(8,128)(2,1)S(1)}, bf16[2,2,32,128]{3,2,1,0:T(8,128)(2,1)S(1)}, u32[]{:S(2)}, u32[]{:S(2)}) collective-permute-start(bf16[2,2,32,128]{3,2,1,0:T(8,128)(2,1)S(1)} %pad_maximum_fusion.refs_2_), channel_id=1, source_target_pairs={{0,24},{4,28},{8,16},{12,20},{16,8},{20,12},{24,0},{28,4},{1,25},{... | collective-permute-start | bytes 98312 | tf_op jit(solution)/shard_map/ppermute | solution.py:202
  7.1 0.0 collective-permute-start.2
  7.1 0.6 %collective-permute-start.1 = (bf16[2,2,32,128]{3,2,1,0:T(8,128)(2,1)S(1)}, bf16[2,2,32,128]{3,2,1,0:T(8,128)(2,1)S(1)}, u32[]{:S(2)}, u32[]{:S(2)}) collective-permute-start(bf16[2,2,32,128]{3,2,1,0:T(8,128)(2,1)S(1)} %pad_maximum_fusion.refs_2_), channel_id=1, source_target_pairs={{0,8},{4,12},{8,0},{12,4},{16,24},{20,28},{24,16},{28,20},{1,9},{5... | collective-permute-start | bytes 98312 | tf_op jit(solution)/shard_map/ppermute | solution.py:202
  8.4 2.3 %shard_map.64 = (bf16[128,128,128]{2,1,0:T(8,128)(2,1)S(1)}, s32[4,256]{1,0:T(4,128)S(4)}) custom-call(bf16[128,128,128]{2,1,0:T(8,128)(2,1)} %tiles_hbm.1, s32[1,128]{1,0:T(1,128)} %bitcast.6, s32[1,128]{1,0:T(1,128)} %bitcast.7, s32[1]{0:T(128)S(6)} %copy.7.count), custom_call_target="tpu_custom_call" | custom-call | bytes 4194304 | tf_op jit(solution)/shard_map/pallas_call | solution.py:150
  10.7 0.0 collective-permute-done.3.refs_5_
  10.7 1.2 %collective-permute-done.2.refs_4_ = bf16[2,2,32,128]{3,2,1,0:T(8,128)(2,1)S(1)} collective-permute-done((bf16[2,2,32,128]{3,2,1,0:T(8,128)(2,1)S(1)}, bf16[2,2,32,128]{3,2,1,0:T(8,128)(2,1)S(1)}, u32[]{:S(2)}, u32[]{:S(2)}) %collective-permute-start.2) | collective-permute-done | bytes 32800 | tf_op jit(solution)/shard_map/ppermute | solution.py:202
  11.9 0.0 collective-permute-done.1.refs_3_
  11.9 0.0 copy-start.1
  12.0 0.5 %shard_map.65 = (bf16[32,16,128]{2,1,0:T(8,128)(2,1)S(1)}, f32[2,256,128]{2,1,0:T(8,128)S(1)}) custom-call(bf16[128,128,128]{2,1,0:T(8,128)(2,1)S(1)} %get-tuple-element.15.refs_0_, s32[4,256]{1,0:T(4,128)S(4)} %get-tuple-element.16.refs_1_, bf16[2,2,32,128]{3,2,1,0:T(8,128)(2,1)S(1)} %pad_maximum_fusion.refs_2_, ...), custom_call_target="tpu_custom_call" | custom-call | flops 16777216 | bytes 1048576 | tf_op jit(solution)/shard_map/pallas_call | solution.py:172
  12.4 2.5 %collective-permute-start.6 = (bf16[32,16,128]{2,1,0:T(8,128)(2,1)S(1)}, bf16[32,16,128]{2,1,0:T(8,128)(2,1)S(1)}, u32[]{:S(2)}, u32[]{:S(2)}) collective-permute-start(bf16[32,16,128]{2,1,0:T(8,128)(2,1)S(1)} %get-tuple-element.20), channel_id=1, source_target_pairs={{0,3},{1,2},{2,1},{3,0},{4,7},{5,6},{6,5},{7,4},{8,11},{9,10},{10,... | collective-permute-start | bytes 393224 | tf_op jit(solution)/shard_map/ppermute | solution.py:205
  15.0 0.0 copy-start
  15.0 0.9 %shard_map.67 = (bf16[32,16,128]{2,1,0:T(8,128)(2,1)S(1)}, bf16[32,16,128]{2,1,0:T(8,128)(2,1)S(1)}) custom-call(bf16[128,128,128]{2,1,0:T(8,128)(2,1)S(1)} %get-tuple-element.15.refs_0_, s32[4,256]{1,0:T(4,128)S(4)} %get-tuple-element.16.refs_1_, f32[2,256,128]{2,1,0:T(8,128)S(1)} %get-tuple-element.17.refs_2_), custom_call_target="tpu_custom_call" | custom-call | flops 33554432 | bytes 2097152 | tf_op jit(solution)/shard_map/pallas_call | solution.py:172
  15.9 0.6 %collective-permute-start.4 = (bf16[32,16,128]{2,1,0:T(8,128)(2,1)S(1)}, bf16[32,16,128]{2,1,0:T(8,128)(2,1)S(1)}, u32[]{:S(2)}, u32[]{:S(2)}) collective-permute-start(bf16[32,16,128]{2,1,0:T(8,128)(2,1)S(1)} %get-tuple-element.18), channel_id=1, source_target_pairs={{0,1},{1,0},{2,3},{3,2},{4,5},{5,4},{6,7},{7,6},{8,9},{9,8},{10,11... | collective-permute-start | bytes 393224 | tf_op jit(solution)/shard_map/ppermute | solution.py:205
  16.5 0.5 %collective-permute-start.5 = (bf16[32,16,128]{2,1,0:T(8,128)(2,1)S(1)}, bf16[32,16,128]{2,1,0:T(8,128)(2,1)S(1)}, u32[]{:S(2)}, u32[]{:S(2)}) collective-permute-start(bf16[32,16,128]{2,1,0:T(8,128)(2,1)S(1)} %get-tuple-element.19), channel_id=1, source_target_pairs={{0,2},{1,3},{2,0},{3,1},{4,6},{5,7},{6,4},{7,5},{8,10},{9,11},{10,... | collective-permute-start | bytes 393224 | tf_op jit(solution)/shard_map/ppermute | solution.py:205
  17.0 0.0 copy-done.1
  17.0 0.5 %shard_map.66 = f32[32,16,128]{2,1,0:T(8,128)S(1)} custom-call(bf16[128,128,128]{2,1,0:T(8,128)(2,1)S(1)} %get-tuple-element.15.refs_0_, s32[4,256]{1,0:T(4,128)S(4)} %get-tuple-element.16.refs_1_, f32[2,256,128]{2,1,0:T(8,128)S(1)} %get-tuple-element.17.refs_2_), custom_call_target="tpu_custom_call" | custom-call | flops 16777216 | bytes 1048576 | tf_op jit(solution)/shard_map/pallas_call | solution.py:172
  17.5 2.3 %collective-permute-done.6 = bf16[32,16,128]{2,1,0:T(8,128)(2,1)S(1)} collective-permute-done((bf16[32,16,128]{2,1,0:T(8,128)(2,1)S(1)}, bf16[32,16,128]{2,1,0:T(8,128)(2,1)S(1)}, u32[]{:S(2)}, u32[]{:S(2)}) %collective-permute-start.6) | collective-permute-done | bytes 131104 | tf_op jit(solution)/shard_map/ppermute | solution.py:205
  19.8 1.4 %collective-permute-done.4 = bf16[32,16,128]{2,1,0:T(8,128)(2,1)S(1)} collective-permute-done((bf16[32,16,128]{2,1,0:T(8,128)(2,1)S(1)}, bf16[32,16,128]{2,1,0:T(8,128)(2,1)S(1)}, u32[]{:S(2)}, u32[]{:S(2)}) %collective-permute-start.4) | collective-permute-done | bytes 131104 | tf_op jit(solution)/shard_map/ppermute | solution.py:205
  21.2 0.4 collective-permute-done.5
  21.5 0.0 copy-done
  21.5 0.1 fusion.1.refs_2_
  21.6 2.8 %collective-permute-start.9 = (bf16[32,16,128]{2,1,0:T(8,128)(2,1)S(1)}, bf16[32,16,128]{2,1,0:T(8,128)(2,1)S(1)}, u32[]{:S(2)}, u32[]{:S(2)}) collective-permute-start(bf16[32,16,128]{2,1,0:T(8,128)(2,1)S(1)} %fusion.1.refs_2_), channel_id=1, source_target_pairs={{0,24},{4,28},{8,16},{12,20},{16,8},{20,12},{24,0},{28,4},{1,25},{... | collective-permute-start | bytes 393224 | tf_op jit(solution)/shard_map/ppermute | solution.py:202
  24.4 0.0 collective-permute-start.8
  24.4 1.6 %collective-permute-start.7 = (bf16[32,16,128]{2,1,0:T(8,128)(2,1)S(1)}, bf16[32,16,128]{2,1,0:T(8,128)(2,1)S(1)}, u32[]{:S(2)}, u32[]{:S(2)}) collective-permute-start(bf16[32,16,128]{2,1,0:T(8,128)(2,1)S(1)} %fusion.1.refs_2_), channel_id=1, source_target_pairs={{0,8},{4,12},{8,0},{12,4},{16,24},{20,28},{24,16},{28,20},{1,9},{5... | collective-permute-start | bytes 393224 | tf_op jit(solution)/shard_map/ppermute | solution.py:202
  26.1 0.0 collective-permute-start.10
  26.1 3.9 %collective-permute-done.9.refs_5_ = bf16[32,16,128]{2,1,0:T(8,128)(2,1)S(1)} collective-permute-done((bf16[32,16,128]{2,1,0:T(8,128)(2,1)S(1)}, bf16[32,16,128]{2,1,0:T(8,128)(2,1)S(1)}, u32[]{:S(2)}, u32[]{:S(2)}) %collective-permute-start.9) | collective-permute-done | bytes 131104 | tf_op jit(solution)/shard_map/ppermute | solution.py:202
  30.0 0.0 collective-permute-start.13
  30.0 4.7 %collective-permute-done.8.refs_4_ = bf16[32,16,128]{2,1,0:T(8,128)(2,1)S(1)} collective-permute-done((bf16[32,16,128]{2,1,0:T(8,128)(2,1)S(1)}, bf16[32,16,128]{2,1,0:T(8,128)(2,1)S(1)}, u32[]{:S(2)}, u32[]{:S(2)}) %collective-permute-start.8) | collective-permute-done | bytes 131104 | tf_op jit(solution)/shard_map/ppermute | solution.py:202
  34.6 0.0 collective-permute-start.12
  34.6 0.0 collective-permute-done.7.refs_3_
  34.6 0.5 %collective-permute-start.11 = (bf16[32,16,128]{2,1,0:T(8,128)(2,1)S(1)}, bf16[32,16,128]{2,1,0:T(8,128)(2,1)S(1)}, u32[]{:S(2)}, u32[]{:S(2)}) collective-permute-start(bf16[32,16,128]{2,1,0:T(8,128)(2,1)S(1)} %collective-permute-done.7.refs_3_), channel_id=1, source_target_pairs={{0,4},{4,0},{8,12},{12,8},{16,20},{20,16},{24,28},{28,24},{1,5},{5... | collective-permute-start | bytes 393224 | tf_op jit(solution)/shard_map/ppermute | solution.py:202
  35.2 0.0 collective-permute-done.10.refs_6_
  35.2 0.0 collective-permute-done.13.refs_9_
  35.2 0.8 %collective-permute-done.12.refs_8_ = bf16[32,16,128]{2,1,0:T(8,128)(2,1)S(1)} collective-permute-done((bf16[32,16,128]{2,1,0:T(8,128)(2,1)S(1)}, bf16[32,16,128]{2,1,0:T(8,128)(2,1)S(1)}, u32[]{:S(2)}, u32[]{:S(2)}) %collective-permute-start.12) | collective-permute-done | bytes 131104 | tf_op jit(solution)/shard_map/ppermute | solution.py:202
  36.0 0.2 collective-permute-done.11.refs_7_
  36.2 0.5 %shard_map.68 = (bf16[32,16,128]{2,1,0:T(8,128)(2,1)S(1)}, bf16[256,16,128]{2,1,0:T(8,128)(2,1)S(1)}) custom-call(bf16[128,128,128]{2,1,0:T(8,128)(2,1)S(1)} %get-tuple-element.15.refs_0_, s32[4,256]{1,0:T(4,128)S(4)} %get-tuple-element.16.refs_1_, bf16[32,16,128]{2,1,0:T(8,128)(2,1)S(1)} %fusion.1.refs_2_, ...), custom_call_target="tpu_custom_call" | custom-call | flops 16777216 | bytes 1048576 | tf_op jit(solution)/shard_map/pallas_call | solution.py:172
  36.7 2.1 %collective-permute-start.16 = (bf16[32,16,128]{2,1,0:T(8,128)(2,1)S(1)}, bf16[32,16,128]{2,1,0:T(8,128)(2,1)S(1)}, u32[]{:S(2)}, u32[]{:S(2)}) collective-permute-start(bf16[32,16,128]{2,1,0:T(8,128)(2,1)S(1)} %get-tuple-element.24), channel_id=1, source_target_pairs={{0,3},{1,2},{2,1},{3,0},{4,7},{5,6},{6,5},{7,4},{8,11},{9,10},{10,... | collective-permute-start | bytes 393224 | tf_op jit(solution)/shard_map/ppermute | solution.py:205
  38.9 0.9 %shard_map.70 = (bf16[32,16,128]{2,1,0:T(8,128)(2,1)S(1)}, bf16[32,16,128]{2,1,0:T(8,128)(2,1)S(1)}) custom-call(bf16[128,128,128]{2,1,0:T(8,128)(2,1)S(1)} %get-tuple-element.15.refs_0_, s32[4,256]{1,0:T(4,128)S(4)} %get-tuple-element.16.refs_1_, bf16[256,16,128]{2,1,0:T(8,128)(2,1)S(1)} %get-tuple-element.21.refs_2_), custom_call_target="tpu_custom_call" | custom-call | flops 33554432 | bytes 2097152 | tf_op jit(solution)/shard_map/pallas_call | solution.py:172
  39.8 0.6 %collective-permute-start.14 = (bf16[32,16,128]{2,1,0:T(8,128)(2,1)S(1)}, bf16[32,16,128]{2,1,0:T(8,128)(2,1)S(1)}, u32[]{:S(2)}, u32[]{:S(2)}) collective-permute-start(bf16[32,16,128]{2,1,0:T(8,128)(2,1)S(1)} %get-tuple-element.22), channel_id=1, source_target_pairs={{0,1},{1,0},{2,3},{3,2},{4,5},{5,4},{6,7},{7,6},{8,9},{9,8},{10,11... | collective-permute-start | bytes 393224 | tf_op jit(solution)/shard_map/ppermute | solution.py:205
  40.4 0.9 %collective-permute-start.15 = (bf16[32,16,128]{2,1,0:T(8,128)(2,1)S(1)}, bf16[32,16,128]{2,1,0:T(8,128)(2,1)S(1)}, u32[]{:S(2)}, u32[]{:S(2)}) collective-permute-start(bf16[32,16,128]{2,1,0:T(8,128)(2,1)S(1)} %get-tuple-element.23), channel_id=1, source_target_pairs={{0,2},{1,3},{2,0},{3,1},{4,6},{5,7},{6,4},{7,5},{8,10},{9,11},{10,... | collective-permute-start | bytes 393224 | tf_op jit(solution)/shard_map/ppermute | solution.py:205
  41.3 0.5 %shard_map.69 = f32[32,16,128]{2,1,0:T(8,128)S(1)} custom-call(bf16[128,128,128]{2,1,0:T(8,128)(2,1)S(1)} %get-tuple-element.15.refs_0_, s32[4,256]{1,0:T(4,128)S(4)} %get-tuple-element.16.refs_1_, bf16[256,16,128]{2,1,0:T(8,128)(2,1)S(1)} %get-tuple-element.21.refs_2_), custom_call_target="tpu_custom_call" | custom-call | flops 16777216 | bytes 1048576 | tf_op jit(solution)/shard_map/pallas_call | solution.py:172
  41.8 2.2 %collective-permute-done.16 = bf16[32,16,128]{2,1,0:T(8,128)(2,1)S(1)} collective-permute-done((bf16[32,16,128]{2,1,0:T(8,128)(2,1)S(1)}, bf16[32,16,128]{2,1,0:T(8,128)(2,1)S(1)}, u32[]{:S(2)}, u32[]{:S(2)}) %collective-permute-start.16) | collective-permute-done | bytes 131104 | tf_op jit(solution)/shard_map/ppermute | solution.py:205
  44.0 1.9 %collective-permute-done.14 = bf16[32,16,128]{2,1,0:T(8,128)(2,1)S(1)} collective-permute-done((bf16[32,16,128]{2,1,0:T(8,128)(2,1)S(1)}, bf16[32,16,128]{2,1,0:T(8,128)(2,1)S(1)}, u32[]{:S(2)}, u32[]{:S(2)}) %collective-permute-start.14) | collective-permute-done | bytes 131104 | tf_op jit(solution)/shard_map/ppermute | solution.py:205
  45.9 0.3 collective-permute-done.15
  46.2 0.8 %select_add_fusion = f32[32,16,128]{2,1,0:T(8,128)} fusion(bf16[32,16,128]{2,1,0:T(8,128)(2,1)S(1)} %collective-permute-done.16, bf16[32,16,128]{2,1,0:T(8,128)(2,1)S(1)} %collective-permute-done.15, f32[32,16,128]{2,1,0:T(8,128)S(1)} %shard_map.69, bf16[32,16,128]{2,1,0:T(8,128)(2,1)S(1)} %collective-permute-done.14, s32[32,128]{1,0:T(8,128)S(1)} %copy-done, ...), kind=kLoop, calls=%fused_computation | loop fusion | flops 655360 | bytes 950272 | tf_op jit(solution)/shard_map/add | solution.py:228
  (3 shorter events, 0.0 us)
Async XLA Ops:
  0.8 1.4 %collective-permute-start = (bf16[2,32,128]{2,1,0:T(8,128)(2,1)S(1)}, bf16[2,32,128]{2,1,0:T(8,128)(2,1)S(1)}, u32[]{:S(2)}, u32[]{:S(2)}) collective-permute-start(bf16[2,32,128]{2,1,0:T(8,128)(2,1)S(1)} %fusion.2), channel_id=1, source_target_pairs={{0,4},{4,0},{8,12},{12,8},{16,20},{20,16},{24,28},{28,24},{1,5},{5... | collective-permute-start | bytes 49160 | tf_op jit(solution)/shard_map/ppermute | solution.py:202
  2.2 8.5 %collective-permute-start.3 = (bf16[2,2,32,128]{3,2,1,0:T(8,128)(2,1)S(1)}, bf16[2,2,32,128]{3,2,1,0:T(8,128)(2,1)S(1)}, u32[]{:S(2)}, u32[]{:S(2)}) collective-permute-start(bf16[2,2,32,128]{3,2,1,0:T(8,128)(2,1)S(1)} %pad_maximum_fusion.refs_2_), channel_id=1, source_target_pairs={{0,24},{4,28},{8,16},{12,20},{16,8},{20,12},{24,0},{28,4},{1,25},{... | collective-permute-start | bytes 98312 | tf_op jit(solution)/shard_map/ppermute | solution.py:202
  7.1 4.8 %collective-permute-start.2 = (bf16[2,2,32,128]{3,2,1,0:T(8,128)(2,1)S(1)}, bf16[2,2,32,128]{3,2,1,0:T(8,128)(2,1)S(1)}, u32[]{:S(2)}, u32[]{:S(2)}) collective-permute-start(bf16[2,2,32,128]{3,2,1,0:T(8,128)(2,1)S(1)} %pad_maximum_fusion.refs_2_), channel_id=1, source_target_pairs={{0,16},{4,20},{8,24},{12,28},{16,0},{20,4},{24,8},{28,12},{1,17},{... | collective-permute-start | bytes 98312 | tf_op jit(solution)/shard_map/ppermute | solution.py:202
  7.1 4.8 %collective-permute-start.1 = (bf16[2,2,32,128]{3,2,1,0:T(8,128)(2,1)S(1)}, bf16[2,2,32,128]{3,2,1,0:T(8,128)(2,1)S(1)}, u32[]{:S(2)}, u32[]{:S(2)}) collective-permute-start(bf16[2,2,32,128]{3,2,1,0:T(8,128)(2,1)S(1)} %pad_maximum_fusion.refs_2_), channel_id=1, source_target_pairs={{0,8},{4,12},{8,0},{12,4},{16,24},{20,28},{24,16},{28,20},{1,9},{5... | collective-permute-start | bytes 98312 | tf_op jit(solution)/shard_map/ppermute | solution.py:202
  11.9 5.1 %copy-start.1 = (s32[32,128]{1,0:T(8,128)S(1)}, s32[32,128]{1,0:T(8,128)}, u32[]{:S(2)}) copy-start(s32[32,128]{1,0:T(8,128)} %param.10) | copy-start | bytes 49156
  12.4 7.4 %collective-permute-start.6 = (bf16[32,16,128]{2,1,0:T(8,128)(2,1)S(1)}, bf16[32,16,128]{2,1,0:T(8,128)(2,1)S(1)}, u32[]{:S(2)}, u32[]{:S(2)}) collective-permute-start(bf16[32,16,128]{2,1,0:T(8,128)(2,1)S(1)} %get-tuple-element.20), channel_id=1, source_target_pairs={{0,3},{1,2},{2,1},{3,0},{4,7},{5,6},{6,5},{7,4},{8,11},{9,10},{10,... | collective-permute-start | bytes 393224 | tf_op jit(solution)/shard_map/ppermute | solution.py:205
  15.0 6.6 %copy-start = (s32[32,128]{1,0:T(8,128)S(1)}, s32[32,128]{1,0:T(8,128)}, u32[]{:S(2)}) copy-start(s32[32,128]{1,0:T(8,128)} %param.11) | copy-start | bytes 49156
  15.9 5.3 %collective-permute-start.4 = (bf16[32,16,128]{2,1,0:T(8,128)(2,1)S(1)}, bf16[32,16,128]{2,1,0:T(8,128)(2,1)S(1)}, u32[]{:S(2)}, u32[]{:S(2)}) collective-permute-start(bf16[32,16,128]{2,1,0:T(8,128)(2,1)S(1)} %get-tuple-element.18), channel_id=1, source_target_pairs={{0,1},{1,0},{2,3},{3,2},{4,5},{5,4},{6,7},{7,6},{8,9},{9,8},{10,11... | collective-permute-start | bytes 393224 | tf_op jit(solution)/shard_map/ppermute | solution.py:205
  16.5 5.0 %collective-permute-start.5 = (bf16[32,16,128]{2,1,0:T(8,128)(2,1)S(1)}, bf16[32,16,128]{2,1,0:T(8,128)(2,1)S(1)}, u32[]{:S(2)}, u32[]{:S(2)}) collective-permute-start(bf16[32,16,128]{2,1,0:T(8,128)(2,1)S(1)} %get-tuple-element.19), channel_id=1, source_target_pairs={{0,2},{1,3},{2,0},{3,1},{4,6},{5,7},{6,4},{7,5},{8,10},{9,11},{10,... | collective-permute-start | bytes 393224 | tf_op jit(solution)/shard_map/ppermute | solution.py:205
  21.6 8.3 %collective-permute-start.9 = (bf16[32,16,128]{2,1,0:T(8,128)(2,1)S(1)}, bf16[32,16,128]{2,1,0:T(8,128)(2,1)S(1)}, u32[]{:S(2)}, u32[]{:S(2)}) collective-permute-start(bf16[32,16,128]{2,1,0:T(8,128)(2,1)S(1)} %fusion.1.refs_2_), channel_id=1, source_target_pairs={{0,24},{4,28},{8,16},{12,20},{16,8},{20,12},{24,0},{28,4},{1,25},{... | collective-permute-start | bytes 393224 | tf_op jit(solution)/shard_map/ppermute | solution.py:202
  24.4 10.2 %collective-permute-start.8 = (bf16[32,16,128]{2,1,0:T(8,128)(2,1)S(1)}, bf16[32,16,128]{2,1,0:T(8,128)(2,1)S(1)}, u32[]{:S(2)}, u32[]{:S(2)}) collective-permute-start(bf16[32,16,128]{2,1,0:T(8,128)(2,1)S(1)} %fusion.1.refs_2_), channel_id=1, source_target_pairs={{0,16},{4,20},{8,24},{12,28},{16,0},{20,4},{24,8},{28,12},{1,17},{... | collective-permute-start | bytes 393224 | tf_op jit(solution)/shard_map/ppermute | solution.py:202
  24.4 10.2 %collective-permute-start.7 = (bf16[32,16,128]{2,1,0:T(8,128)(2,1)S(1)}, bf16[32,16,128]{2,1,0:T(8,128)(2,1)S(1)}, u32[]{:S(2)}, u32[]{:S(2)}) collective-permute-start(bf16[32,16,128]{2,1,0:T(8,128)(2,1)S(1)} %fusion.1.refs_2_), channel_id=1, source_target_pairs={{0,8},{4,12},{8,0},{12,4},{16,24},{20,28},{24,16},{28,20},{1,9},{5... | collective-permute-start | bytes 393224 | tf_op jit(solution)/shard_map/ppermute | solution.py:202
  26.1 9.1 %collective-permute-start.10 = (bf16[32,16,128]{2,1,0:T(8,128)(2,1)S(1)}, bf16[32,16,128]{2,1,0:T(8,128)(2,1)S(1)}, u32[]{:S(2)}, u32[]{:S(2)}) collective-permute-start(bf16[32,16,128]{2,1,0:T(8,128)(2,1)S(1)} %fusion.1.refs_2_), channel_id=1, source_target_pairs={{0,4},{4,0},{8,12},{12,8},{16,20},{20,16},{24,28},{28,24},{1,5},{5... | collective-permute-start | bytes 393224 | tf_op jit(solution)/shard_map/ppermute | solution.py:202
  30.0 5.2 %collective-permute-start.13 = (bf16[32,16,128]{2,1,0:T(8,128)(2,1)S(1)}, bf16[32,16,128]{2,1,0:T(8,128)(2,1)S(1)}, u32[]{:S(2)}, u32[]{:S(2)}) collective-permute-start(bf16[32,16,128]{2,1,0:T(8,128)(2,1)S(1)} %collective-permute-done.9.refs_5_), channel_id=1, source_target_pairs={{0,4},{4,0},{8,12},{12,8},{16,20},{20,16},{24,28},{28,24},{1,5},{5... | collective-permute-start | bytes 393224 | tf_op jit(solution)/shard_map/ppermute | solution.py:202
  34.6 1.3 %collective-permute-start.12 = (bf16[32,16,128]{2,1,0:T(8,128)(2,1)S(1)}, bf16[32,16,128]{2,1,0:T(8,128)(2,1)S(1)}, u32[]{:S(2)}, u32[]{:S(2)}) collective-permute-start(bf16[32,16,128]{2,1,0:T(8,128)(2,1)S(1)} %collective-permute-done.8.refs_4_), channel_id=1, source_target_pairs={{0,4},{4,0},{8,12},{12,8},{16,20},{20,16},{24,28},{28,24},{1,5},{5... | collective-permute-start | bytes 393224 | tf_op jit(solution)/shard_map/ppermute | solution.py:202
  34.6 1.5 %collective-permute-start.11 = (bf16[32,16,128]{2,1,0:T(8,128)(2,1)S(1)}, bf16[32,16,128]{2,1,0:T(8,128)(2,1)S(1)}, u32[]{:S(2)}, u32[]{:S(2)}) collective-permute-start(bf16[32,16,128]{2,1,0:T(8,128)(2,1)S(1)} %collective-permute-done.7.refs_3_), channel_id=1, source_target_pairs={{0,4},{4,0},{8,12},{12,8},{16,20},{20,16},{24,28},{28,24},{1,5},{5... | collective-permute-start | bytes 393224 | tf_op jit(solution)/shard_map/ppermute | solution.py:202
  36.7 7.3 %collective-permute-start.16 = (bf16[32,16,128]{2,1,0:T(8,128)(2,1)S(1)}, bf16[32,16,128]{2,1,0:T(8,128)(2,1)S(1)}, u32[]{:S(2)}, u32[]{:S(2)}) collective-permute-start(bf16[32,16,128]{2,1,0:T(8,128)(2,1)S(1)} %get-tuple-element.24), channel_id=1, source_target_pairs={{0,3},{1,2},{2,1},{3,0},{4,7},{5,6},{6,5},{7,4},{8,11},{9,10},{10,... | collective-permute-start | bytes 393224 | tf_op jit(solution)/shard_map/ppermute | solution.py:205
  39.8 6.1 %collective-permute-start.14 = (bf16[32,16,128]{2,1,0:T(8,128)(2,1)S(1)}, bf16[32,16,128]{2,1,0:T(8,128)(2,1)S(1)}, u32[]{:S(2)}, u32[]{:S(2)}) collective-permute-start(bf16[32,16,128]{2,1,0:T(8,128)(2,1)S(1)} %get-tuple-element.22), channel_id=1, source_target_pairs={{0,1},{1,0},{2,3},{3,2},{4,5},{5,4},{6,7},{7,6},{8,9},{9,8},{10,11... | collective-permute-start | bytes 393224 | tf_op jit(solution)/shard_map/ppermute | solution.py:205
  40.4 5.8 %collective-permute-start.15 = (bf16[32,16,128]{2,1,0:T(8,128)(2,1)S(1)}, bf16[32,16,128]{2,1,0:T(8,128)(2,1)S(1)}, u32[]{:S(2)}, u32[]{:S(2)}) collective-permute-start(bf16[32,16,128]{2,1,0:T(8,128)(2,1)S(1)} %get-tuple-element.23), channel_id=1, source_target_pairs={{0,2},{1,3},{2,0},{3,1},{4,6},{5,7},{6,4},{7,5},{8,10},{9,11},{10,... | collective-permute-start | bytes 393224 | tf_op jit(solution)/shard_map/ppermute | solution.py:205

commit v7 on v6

--- a/solution.py
+++ b/solution.py
@@ -109,8 +109,10 @@
                     place = (half * len(fields) + i) * blk
                     picks[kind, pl.ds(place, blk), :] = f[half, kind].astype(jnp.float32)
     elif first:
+        near = slots_of(nrow, lax.axis_index("row"))
         for i, f in enumerate(fields):
-            picks[pl.ds(i * blk, blk)] = f[...]
+            slot = near[i % (nrow // 2)] + i // (nrow // 2) * (nrow // 2)
+            picks[pl.ds(slot * blk, blk)] = f[...]
     query = lax.broadcasted_iota(jnp.int32, (QC, 128), 0).astype(jnp.float32)
     begin, end = table[3, index], table[3, index + 1]
 
@@ -194,6 +196,29 @@
     return slices
 
 
+def gather_far(own, nrow):
+    nz = nrow // 2
+    if nz != 4:
+        return [lax.ppermute(own, "row", [(i, i ^ (2 * m)) for i in range(nrow)]) for m in range(1, nz)], lax.ppermute(own, "row", [(i, i ^ 1) for i in range(nrow)])
+    ring = [(0, 2), (2, 3), (3, 1), (1, 0)]
+    ahead = [(2 * a + k, 2 * b + k) for a, b in ring for k in range(2)]
+    back = [(b, a) for a, b in ahead]
+    one = lax.ppermute(own, "row", ahead)
+    partner = lax.ppermute(own, "row", [(i, i ^ 1) for i in range(nrow)])
+    later, partner = lax.optimization_barrier((own, partner))
+    other = lax.ppermute(later, "row", back)
+    return [one, other, lax.ppermute(one, "row", ahead)], partner
+
+
+def slots_of(nrow, row_pos):
+    nz = nrow // 2
+    if nz != 4:
+        return list(range(nz))
+    z = div(row_pos, 2)
+    inner = (z ^ div(z, 2)) & 1
+    return [0, 1 + inner, 2 - inner, 3]
+
+
 def local(nrow, ncol, tiles, tile_rows, tile_cols, tile_count, degree, labels):
     blk = labels.shape[0]
     nz = nrow // 2
@@ -219,8 +244,8 @@
             both = jnp.stack([own, from_row(own, 1)])
             fields = [both] + [from_row(both, 2 * m) for m in range(1, nz)]
         else:
-            near = [own] + [from_row(own, 2 * m) for m in range(1, nz)]
-            fields = near + [from_row(x, 1) for x in near]
+            far, partner = gather_far(own, nrow)
+            fields = [own] + far + [partner] + [from_row(x, 1) for x in far]
         outs = spread_calls(step == 0, nrow, ncol, blk, tiles, table, fields)
         summed = outs[0]
         for k in range(1, ncol):

time: 47.3 us -> 46.8 us (0.989)
  waiting for transfers between devices: 20 us -> 19 us
  starting transfers between devices: 18.3 us -> 18.8 us
    ppermute x11 -> x7, waiting for transfers between devices: 11.6 us -> 3.4 us  [from_row(): return lax.ppermute(x, 'row', [(i, i ^ d) for i in range(nrow)])]
    ppermute x0 -> x4, waiting for transfers between devices: none -> 7.5 us  [the longest x1 3.84 us: gather_far(): one = lax.ppermute(own, 'row', ahead)]
    ppermute x0 -> x4, starting transfers between devices: none -> 5.43 us  [the longest x1 3.28 us: gather_far(): return ([one, other, lax.ppermute(one, 'row', ahead)], partner)]
    ppermute x11 -> x7, starting transfers between devices: 11.1 us -> 6.11 us  [from_row(): return lax.ppermute(x, 'row', [(i, i ^ d) for i in range(nrow)])]
where the time goes in v7:
time: 46.8 us; the launch traced here: 46.5 us
  waiting for transfers between devices  19 us (41%)
  starting transfers between devices  18.8 us (40%)
  Pallas kernels  6.18 us (13%)
  other arithmetic  1.73 us (4%)
  between operations  0.75 us (2%)
    ppermute x6, waiting for transfers between devices, from_col(): return lax.ppermute(x, 'col', [(i, i ^ k) for i in range(ncol)])  8.12 us
    ppermute x6, starting transfers between devices, from_col(): return lax.ppermute(x, 'col', [(i, i ^ k) for i in range(ncol)])  7.25 us
    ppermute x7, starting transfers between devices, from_row(): return lax.ppermute(x, 'row', [(i, i ^ d) for i in range(nrow)])  6.11 us
    pallas_call x6, Pallas kernels, spread_calls(): pl.pallas_call(functools.partial(spread, seeded, first, index, (low, high...  3.9 us
    ppermute x1, waiting for transfers between devices, gather_far(): one = lax.ppermute(own, 'row', ahead)  3.84 us
    ppermute x7, waiting for transfers between devices, from_row(): return lax.ppermute(x, 'row', [(i, i ^ d) for i in range(nrow)])  3.4 us
    ppermute x1, starting transfers between devices, gather_far(): return ([one, other, lax.ppermute(one, 'row', ahead)], partner)  3.28 us
    ppermute x1, waiting for transfers between devices, gather_far(): return ([one, other, lax.ppermute(one, 'row', ahead)], partner)  2.7 us
  transfers between devices with their start and end apart: 17, of which 12 were waited for; matrix products, arithmetic and copies ran while one was open for 0% of the time, Pallas kernels for 11%

profile of v7, /device:TPU:0, one launch (start us, length us, event | category | flops | bytes accessed | tf_op | source)
XLA Modules:
  0.0 46.5 jit_solution(14774622318567241379)
XLA Ops:
  0.0 0.8 %fusion.2 = bf16[2,32,128]{2,1,0:T(8,128)(2,1)S(1)} fusion(s32[32,128]{1,0:T(8,128)} %param.10, s32[32,128]{1,0:T(8,128)} %param.11, pred[2]{0:T(512)(128)(4,1)S(1)} %iota_compare_fusion.1), kind=kLoop, calls=%fused_computation.6 | loop fusion | flops 32768 | bytes 49154 | tf_op jit(solution)/shard_map/convert_element_type | solution.py:237
  0.8 0.5 %collective-permute-start = (bf16[2,32,128]{2,1,0:T(8,128)(2,1)S(1)}, bf16[2,32,128]{2,1,0:T(8,128)(2,1)S(1)}, u32[]{:S(2)}, u32[]{:S(2)}) collective-permute-start(bf16[2,32,128]{2,1,0:T(8,128)(2,1)S(1)} %fusion.2), channel_id=1, source_target_pairs={{0,4},{4,0},{8,12},{12,8},{16,20},{20,16},{24,28},{28,24},{1,5},{5... | collective-permute-start | bytes 49160 | tf_op jit(solution)/shard_map/ppermute | solution.py:227
  1.3 0.8 %collective-permute-done = bf16[2,32,128]{2,1,0:T(8,128)(2,1)S(1)} collective-permute-done((bf16[2,32,128]{2,1,0:T(8,128)(2,1)S(1)}, bf16[2,32,128]{2,1,0:T(8,128)(2,1)S(1)}, u32[]{:S(2)}, u32[]{:S(2)}) %collective-permute-start) | collective-permute-done | bytes 16416 | tf_op jit(solution)/shard_map/ppermute | solution.py:227
  2.2 4.9 %collective-permute-start.3 = (bf16[2,2,32,128]{3,2,1,0:T(8,128)(2,1)S(1)}, bf16[2,2,32,128]{3,2,1,0:T(8,128)(2,1)S(1)}, u32[]{:S(2)}, u32[]{:S(2)}) collective-permute-start(bf16[2,2,32,128]{3,2,1,0:T(8,128)(2,1)S(1)} %pad_maximum_fusion.refs_2_), channel_id=1, source_target_pairs={{0,24},{4,28},{8,16},{12,20},{16,8},{20,12},{24,0},{28,4},{1,25},{... | collective-permute-start | bytes 98312 | tf_op jit(solution)/shard_map/ppermute | solution.py:227
  7.1 0.0 collective-permute-start.2
  7.1 0.6 %collective-permute-start.1 = (bf16[2,2,32,128]{3,2,1,0:T(8,128)(2,1)S(1)}, bf16[2,2,32,128]{3,2,1,0:T(8,128)(2,1)S(1)}, u32[]{:S(2)}, u32[]{:S(2)}) collective-permute-start(bf16[2,2,32,128]{3,2,1,0:T(8,128)(2,1)S(1)} %pad_maximum_fusion.refs_2_), channel_id=1, source_target_pairs={{0,8},{4,12},{8,0},{12,4},{16,24},{20,28},{24,16},{28,20},{1,9},{5... | collective-permute-start | bytes 98312 | tf_op jit(solution)/shard_map/ppermute | solution.py:227
  8.4 2.3 %shard_map.64 = (bf16[128,128,128]{2,1,0:T(8,128)(2,1)S(1)}, s32[4,256]{1,0:T(4,128)S(4)}) custom-call(bf16[128,128,128]{2,1,0:T(8,128)(2,1)} %tiles_hbm.1, s32[1,128]{1,0:T(1,128)} %bitcast.6, s32[1,128]{1,0:T(1,128)} %bitcast.7, s32[1]{0:T(128)S(6)} %copy.7.count), custom_call_target="tpu_custom_call" | custom-call | bytes 4194304 | tf_op jit(solution)/shard_map/pallas_call | solution.py:152
  10.7 0.0 collective-permute-done.3.refs_5_
  10.7 1.2 %collective-permute-done.2.refs_4_ = bf16[2,2,32,128]{3,2,1,0:T(8,128)(2,1)S(1)} collective-permute-done((bf16[2,2,32,128]{3,2,1,0:T(8,128)(2,1)S(1)}, bf16[2,2,32,128]{3,2,1,0:T(8,128)(2,1)S(1)}, u32[]{:S(2)}, u32[]{:S(2)}) %collective-permute-start.2) | collective-permute-done | bytes 32800 | tf_op jit(solution)/shard_map/ppermute | solution.py:227
  11.9 0.0 collective-permute-done.1.refs_3_
  11.9 0.0 copy-start.1
  12.0 0.5 %shard_map.65 = (bf16[32,16,128]{2,1,0:T(8,128)(2,1)S(1)}, f32[2,256,128]{2,1,0:T(8,128)S(1)}) custom-call(bf16[128,128,128]{2,1,0:T(8,128)(2,1)S(1)} %get-tuple-element.17.refs_0_, s32[4,256]{1,0:T(4,128)S(4)} %get-tuple-element.18.refs_1_, bf16[2,2,32,128]{3,2,1,0:T(8,128)(2,1)S(1)} %pad_maximum_fusion.refs_2_, ...), custom_call_target="tpu_custom_call" | custom-call | flops 16777216 | bytes 1048576 | tf_op jit(solution)/shard_map/pallas_call | solution.py:174
  12.4 2.5 %collective-permute-start.6 = (bf16[32,16,128]{2,1,0:T(8,128)(2,1)S(1)}, bf16[32,16,128]{2,1,0:T(8,128)(2,1)S(1)}, u32[]{:S(2)}, u32[]{:S(2)}) collective-permute-start(bf16[32,16,128]{2,1,0:T(8,128)(2,1)S(1)} %get-tuple-element.22), channel_id=1, source_target_pairs={{0,3},{1,2},{2,1},{3,0},{4,7},{5,6},{6,5},{7,4},{8,11},{9,10},{10,... | collective-permute-start | bytes 393224 | tf_op jit(solution)/shard_map/ppermute | solution.py:230
  15.0 0.0 copy-start
  15.0 0.9 %shard_map.67 = (bf16[32,16,128]{2,1,0:T(8,128)(2,1)S(1)}, bf16[32,16,128]{2,1,0:T(8,128)(2,1)S(1)}) custom-call(bf16[128,128,128]{2,1,0:T(8,128)(2,1)S(1)} %get-tuple-element.17.refs_0_, s32[4,256]{1,0:T(4,128)S(4)} %get-tuple-element.18.refs_1_, f32[2,256,128]{2,1,0:T(8,128)S(1)} %get-tuple-element.19.refs_2_), custom_call_target="tpu_custom_call" | custom-call | flops 33554432 | bytes 2097152 | tf_op jit(solution)/shard_map/pallas_call | solution.py:174
  15.9 0.2 collective-permute-start.4
  16.1 0.9 %collective-permute-start.5 = (bf16[32,16,128]{2,1,0:T(8,128)(2,1)S(1)}, bf16[32,16,128]{2,1,0:T(8,128)(2,1)S(1)}, u32[]{:S(2)}, u32[]{:S(2)}) collective-permute-start(bf16[32,16,128]{2,1,0:T(8,128)(2,1)S(1)} %get-tuple-element.21), channel_id=1, source_target_pairs={{0,2},{1,3},{2,0},{3,1},{4,6},{5,7},{6,4},{7,5},{8,10},{9,11},{10,... | collective-permute-start | bytes 393224 | tf_op jit(solution)/shard_map/ppermute | solution.py:230
  17.0 0.0 copy-done.1
  17.0 0.5 %shard_map.66 = f32[32,16,128]{2,1,0:T(8,128)S(1)} custom-call(bf16[128,128,128]{2,1,0:T(8,128)(2,1)S(1)} %get-tuple-element.17.refs_0_, s32[4,256]{1,0:T(4,128)S(4)} %get-tuple-element.18.refs_1_, f32[2,256,128]{2,1,0:T(8,128)S(1)} %get-tuple-element.19.refs_2_), custom_call_target="tpu_custom_call" | custom-call | flops 16777216 | bytes 1048576 | tf_op jit(solution)/shard_map/pallas_call | solution.py:174
  17.5 2.0 %collective-permute-done.6 = bf16[32,16,128]{2,1,0:T(8,128)(2,1)S(1)} collective-permute-done((bf16[32,16,128]{2,1,0:T(8,128)(2,1)S(1)}, bf16[32,16,128]{2,1,0:T(8,128)(2,1)S(1)}, u32[]{:S(2)}, u32[]{:S(2)}) %collective-permute-start.6) | collective-permute-done | bytes 131104 | tf_op jit(solution)/shard_map/ppermute | solution.py:230
  19.5 1.6 %collective-permute-done.4 = bf16[32,16,128]{2,1,0:T(8,128)(2,1)S(1)} collective-permute-done((bf16[32,16,128]{2,1,0:T(8,128)(2,1)S(1)}, bf16[32,16,128]{2,1,0:T(8,128)(2,1)S(1)}, u32[]{:S(2)}, u32[]{:S(2)}) %collective-permute-start.4) | collective-permute-done | bytes 131104 | tf_op jit(solution)/shard_map/ppermute | solution.py:230
  21.2 0.2 collective-permute-done.5
  21.4 0.0 copy-done
  21.4 0.1 fusion.1.refs_2_
  21.5 0.1 collective-permute-start.8
  21.6 2.0 %collective-permute-start.7 = (bf16[32,16,128]{2,1,0:T(8,128)(2,1)S(1)}, bf16[32,16,128]{2,1,0:T(8,128)(2,1)S(1)}, u32[]{:S(2)}, u32[]{:S(2)}) collective-permute-start(bf16[32,16,128]{2,1,0:T(8,128)(2,1)S(1)} %fusion.1.refs_2_), channel_id=1, source_target_pairs={{0,16},{4,20},{16,24},{20,28},{24,8},{28,12},{8,0},{12,4},{1,17},{... | collective-permute-start | bytes 393224 | tf_op jit(solution)/shard_map/ppermute | solution.py:206
  23.6 0.0 collective-permute-done.8.refs_6_
  23.6 0.1 collective-permute-start.9
  23.7 3.8 %collective-permute-done.7.refs_3_ = bf16[32,16,128]{2,1,0:T(8,128)(2,1)S(1)} collective-permute-done((bf16[32,16,128]{2,1,0:T(8,128)(2,1)S(1)}, bf16[32,16,128]{2,1,0:T(8,128)(2,1)S(1)}, u32[]{:S(2)}, u32[]{:S(2)}) %collective-permute-start.7) | collective-permute-done | bytes 131104 | tf_op jit(solution)/shard_map/ppermute | solution.py:206
  27.5 3.3 %collective-permute-start.10 = (bf16[32,16,128]{2,1,0:T(8,128)(2,1)S(1)}, bf16[32,16,128]{2,1,0:T(8,128)(2,1)S(1)}, u32[]{:S(2)}, u32[]{:S(2)}) collective-permute-start(bf16[32,16,128]{2,1,0:T(8,128)(2,1)S(1)} %collective-permute-done.7.refs_3_), channel_id=1, source_target_pairs={{0,16},{4,20},{16,24},{20,28},{24,8},{28,12},{8,0},{12,4},{1,17},{... | collective-permute-start | bytes 393224 | tf_op jit(solution)/shard_map/ppermute | solution.py:210
  30.8 0.0 collective-permute-start.11
  30.8 1.0 %collective-permute-done.9.refs_4_ = bf16[32,16,128]{2,1,0:T(8,128)(2,1)S(1)} collective-permute-done((bf16[32,16,128]{2,1,0:T(8,128)(2,1)S(1)}, bf16[32,16,128]{2,1,0:T(8,128)(2,1)S(1)}, u32[]{:S(2)}, u32[]{:S(2)}) %collective-permute-start.9) | collective-permute-done | bytes 131104 | tf_op jit(solution)/shard_map/ppermute | solution.py:209
  31.8 0.0 collective-permute-start.12
  31.8 2.7 %collective-permute-done.10.refs_5_ = bf16[32,16,128]{2,1,0:T(8,128)(2,1)S(1)} collective-permute-done((bf16[32,16,128]{2,1,0:T(8,128)(2,1)S(1)}, bf16[32,16,128]{2,1,0:T(8,128)(2,1)S(1)}, u32[]{:S(2)}, u32[]{:S(2)}) %collective-permute-start.10) | collective-permute-done | bytes 131104 | tf_op jit(solution)/shard_map/ppermute | solution.py:210
  34.5 0.0 collective-permute-start.13
  34.5 0.0 collective-permute-done.11.refs_7_
  34.5 0.0 collective-permute-done.12.refs_8_
  34.5 1.3 %collective-permute-done.13.refs_9_ = bf16[32,16,128]{2,1,0:T(8,128)(2,1)S(1)} collective-permute-done((bf16[32,16,128]{2,1,0:T(8,128)(2,1)S(1)}, bf16[32,16,128]{2,1,0:T(8,128)(2,1)S(1)}, u32[]{:S(2)}, u32[]{:S(2)}) %collective-permute-start.13) | collective-permute-done | bytes 131104 | tf_op jit(solution)/shard_map/ppermute | solution.py:227
  35.8 0.6 %shard_map.68 = (bf16[32,16,128]{2,1,0:T(8,128)(2,1)S(1)}, bf16[256,16,128]{2,1,0:T(8,128)(2,1)S(1)}) custom-call(bf16[128,128,128]{2,1,0:T(8,128)(2,1)S(1)} %get-tuple-element.17.refs_0_, s32[4,256]{1,0:T(4,128)S(4)} %get-tuple-element.18.refs_1_, bf16[32,16,128]{2,1,0:T(8,128)(2,1)S(1)} %fusion.1.refs_2_, ...), custom_call_target="tpu_custom_call" | custom-call | flops 16777216 | bytes 1048576 | tf_op jit(solution)/shard_map/pallas_call | solution.py:174
  36.4 1.7 %collective-permute-start.16 = (bf16[32,16,128]{2,1,0:T(8,128)(2,1)S(1)}, bf16[32,16,128]{2,1,0:T(8,128)(2,1)S(1)}, u32[]{:S(2)}, u32[]{:S(2)}) collective-permute-start(bf16[32,16,128]{2,1,0:T(8,128)(2,1)S(1)} %get-tuple-element.28), channel_id=1, source_target_pairs={{0,3},{1,2},{2,1},{3,0},{4,7},{5,6},{6,5},{7,4},{8,11},{9,10},{10,... | collective-permute-start | bytes 393224 | tf_op jit(solution)/shard_map/ppermute | solution.py:230
  38.0 0.9 %shard_map.70 = (bf16[32,16,128]{2,1,0:T(8,128)(2,1)S(1)}, bf16[32,16,128]{2,1,0:T(8,128)(2,1)S(1)}) custom-call(bf16[128,128,128]{2,1,0:T(8,128)(2,1)S(1)} %get-tuple-element.17.refs_0_, s32[4,256]{1,0:T(4,128)S(4)} %get-tuple-element.18.refs_1_, bf16[256,16,128]{2,1,0:T(8,128)(2,1)S(1)} %get-tuple-element.25.refs_2_), custom_call_target="tpu_custom_call" | custom-call | flops 33554432 | bytes 2097152 | tf_op jit(solution)/shard_map/pallas_call | solution.py:174
  39.0 0.1 collective-permute-start.14
  39.1 1.8 %collective-permute-start.15 = (bf16[32,16,128]{2,1,0:T(8,128)(2,1)S(1)}, bf16[32,16,128]{2,1,0:T(8,128)(2,1)S(1)}, u32[]{:S(2)}, u32[]{:S(2)}) collective-permute-start(bf16[32,16,128]{2,1,0:T(8,128)(2,1)S(1)} %get-tuple-element.27), channel_id=1, source_target_pairs={{0,2},{1,3},{2,0},{3,1},{4,6},{5,7},{6,4},{7,5},{8,10},{9,11},{10,... | collective-permute-start | bytes 393224 | tf_op jit(solution)/shard_map/ppermute | solution.py:230
  40.9 0.5 %shard_map.69 = f32[32,16,128]{2,1,0:T(8,128)S(1)} custom-call(bf16[128,128,128]{2,1,0:T(8,128)(2,1)S(1)} %get-tuple-element.17.refs_0_, s32[4,256]{1,0:T(4,128)S(4)} %get-tuple-element.18.refs_1_, bf16[256,16,128]{2,1,0:T(8,128)(2,1)S(1)} %get-tuple-element.25.refs_2_), custom_call_target="tpu_custom_call" | custom-call | flops 16777216 | bytes 1048576 | tf_op jit(solution)/shard_map/pallas_call | solution.py:174
  41.4 2.2 %collective-permute-done.16 = bf16[32,16,128]{2,1,0:T(8,128)(2,1)S(1)} collective-permute-done((bf16[32,16,128]{2,1,0:T(8,128)(2,1)S(1)}, bf16[32,16,128]{2,1,0:T(8,128)(2,1)S(1)}, u32[]{:S(2)}, u32[]{:S(2)}) %collective-permute-start.16) | collective-permute-done | bytes 131104 | tf_op jit(solution)/shard_map/ppermute | solution.py:230
  43.7 1.2 %collective-permute-done.14 = bf16[32,16,128]{2,1,0:T(8,128)(2,1)S(1)} collective-permute-done((bf16[32,16,128]{2,1,0:T(8,128)(2,1)S(1)}, bf16[32,16,128]{2,1,0:T(8,128)(2,1)S(1)}, u32[]{:S(2)}, u32[]{:S(2)}) %collective-permute-start.14) | collective-permute-done | bytes 131104 | tf_op jit(solution)/shard_map/ppermute | solution.py:230
  44.9 0.8 %collective-permute-done.15 = bf16[32,16,128]{2,1,0:T(8,128)(2,1)S(1)} collective-permute-done((bf16[32,16,128]{2,1,0:T(8,128)(2,1)S(1)}, bf16[32,16,128]{2,1,0:T(8,128)(2,1)S(1)}, u32[]{:S(2)}, u32[]{:S(2)}) %collective-permute-start.15) | collective-permute-done | bytes 131104 | tf_op jit(solution)/shard_map/ppermute | solution.py:230
  45.7 0.8 %select_add_fusion = f32[32,16,128]{2,1,0:T(8,128)} fusion(bf16[32,16,128]{2,1,0:T(8,128)(2,1)S(1)} %collective-permute-done.16, bf16[32,16,128]{2,1,0:T(8,128)(2,1)S(1)} %collective-permute-done.15, f32[32,16,128]{2,1,0:T(8,128)S(1)} %shard_map.69, bf16[32,16,128]{2,1,0:T(8,128)(2,1)S(1)} %collective-permute-done.14, s32[32,128]{1,0:T(8,128)S(1)} %copy-done, ...), kind=kLoop, calls=%fused_computation | loop fusion | flops 655360 | bytes 950272 | tf_op jit(solution)/shard_map/add | solution.py:253
  (3 shorter events, 0.0 us)
Async XLA Ops:
  0.8 1.4 %collective-permute-start = (bf16[2,32,128]{2,1,0:T(8,128)(2,1)S(1)}, bf16[2,32,128]{2,1,0:T(8,128)(2,1)S(1)}, u32[]{:S(2)}, u32[]{:S(2)}) collective-permute-start(bf16[2,32,128]{2,1,0:T(8,128)(2,1)S(1)} %fusion.2), channel_id=1, source_target_pairs={{0,4},{4,0},{8,12},{12,8},{16,20},{20,16},{24,28},{28,24},{1,5},{5... | collective-permute-start | bytes 49160 | tf_op jit(solution)/shard_map/ppermute | solution.py:227
  2.2 8.5 %collective-permute-start.3 = (bf16[2,2,32,128]{3,2,1,0:T(8,128)(2,1)S(1)}, bf16[2,2,32,128]{3,2,1,0:T(8,128)(2,1)S(1)}, u32[]{:S(2)}, u32[]{:S(2)}) collective-permute-start(bf16[2,2,32,128]{3,2,1,0:T(8,128)(2,1)S(1)} %pad_maximum_fusion.refs_2_), channel_id=1, source_target_pairs={{0,24},{4,28},{8,16},{12,20},{16,8},{20,12},{24,0},{28,4},{1,25},{... | collective-permute-start | bytes 98312 | tf_op jit(solution)/shard_map/ppermute | solution.py:227
  7.1 4.8 %collective-permute-start.2 = (bf16[2,2,32,128]{3,2,1,0:T(8,128)(2,1)S(1)}, bf16[2,2,32,128]{3,2,1,0:T(8,128)(2,1)S(1)}, u32[]{:S(2)}, u32[]{:S(2)}) collective-permute-start(bf16[2,2,32,128]{3,2,1,0:T(8,128)(2,1)S(1)} %pad_maximum_fusion.refs_2_), channel_id=1, source_target_pairs={{0,16},{4,20},{8,24},{12,28},{16,0},{20,4},{24,8},{28,12},{1,17},{... | collective-permute-start | bytes 98312 | tf_op jit(solution)/shard_map/ppermute | solution.py:227
  7.1 4.8 %collective-permute-start.1 = (bf16[2,2,32,128]{3,2,1,0:T(8,128)(2,1)S(1)}, bf16[2,2,32,128]{3,2,1,0:T(8,128)(2,1)S(1)}, u32[]{:S(2)}, u32[]{:S(2)}) collective-permute-start(bf16[2,2,32,128]{3,2,1,0:T(8,128)(2,1)S(1)} %pad_maximum_fusion.refs_2_), channel_id=1, source_target_pairs={{0,8},{4,12},{8,0},{12,4},{16,24},{20,28},{24,16},{28,20},{1,9},{5... | collective-permute-start | bytes 98312 | tf_op jit(solution)/shard_map/ppermute | solution.py:227
  11.9 5.1 %copy-start.1 = (s32[32,128]{1,0:T(8,128)S(1)}, s32[32,128]{1,0:T(8,128)}, u32[]{:S(2)}) copy-start(s32[32,128]{1,0:T(8,128)} %param.10) | copy-start | bytes 49156
  12.4 7.1 %collective-permute-start.6 = (bf16[32,16,128]{2,1,0:T(8,128)(2,1)S(1)}, bf16[32,16,128]{2,1,0:T(8,128)(2,1)S(1)}, u32[]{:S(2)}, u32[]{:S(2)}) collective-permute-start(bf16[32,16,128]{2,1,0:T(8,128)(2,1)S(1)} %get-tuple-element.22), channel_id=1, source_target_pairs={{0,3},{1,2},{2,1},{3,0},{4,7},{5,6},{6,5},{7,4},{8,11},{9,10},{10,... | collective-permute-start | bytes 393224 | tf_op jit(solution)/shard_map/ppermute | solution.py:230
  15.0 6.4 %copy-start = (s32[32,128]{1,0:T(8,128)S(1)}, s32[32,128]{1,0:T(8,128)}, u32[]{:S(2)}) copy-start(s32[32,128]{1,0:T(8,128)} %param.11) | copy-start | bytes 49156
  15.9 5.3 %collective-permute-start.4 = (bf16[32,16,128]{2,1,0:T(8,128)(2,1)S(1)}, bf16[32,16,128]{2,1,0:T(8,128)(2,1)S(1)}, u32[]{:S(2)}, u32[]{:S(2)}) collective-permute-start(bf16[32,16,128]{2,1,0:T(8,128)(2,1)S(1)} %get-tuple-element.20), channel_id=1, source_target_pairs={{0,1},{1,0},{2,3},{3,2},{4,5},{5,4},{6,7},{7,6},{8,9},{9,8},{10,11... | collective-permute-start | bytes 393224 | tf_op jit(solution)/shard_map/ppermute | solution.py:230
  16.1 5.3 %collective-permute-start.5 = (bf16[32,16,128]{2,1,0:T(8,128)(2,1)S(1)}, bf16[32,16,128]{2,1,0:T(8,128)(2,1)S(1)}, u32[]{:S(2)}, u32[]{:S(2)}) collective-permute-start(bf16[32,16,128]{2,1,0:T(8,128)(2,1)S(1)} %get-tuple-element.21), channel_id=1, source_target_pairs={{0,2},{1,3},{2,0},{3,1},{4,6},{5,7},{6,4},{7,5},{8,10},{9,11},{10,... | collective-permute-start | bytes 393224 | tf_op jit(solution)/shard_map/ppermute | solution.py:230
  21.5 2.1 %collective-permute-start.8 = (bf16[32,16,128]{2,1,0:T(8,128)(2,1)S(1)}, bf16[32,16,128]{2,1,0:T(8,128)(2,1)S(1)}, u32[]{:S(2)}, u32[]{:S(2)}) collective-permute-start(bf16[32,16,128]{2,1,0:T(8,128)(2,1)S(1)} %fusion.1.refs_2_), channel_id=1, source_target_pairs={{0,4},{4,0},{8,12},{12,8},{16,20},{20,16},{24,28},{28,24},{1,5},{5... | collective-permute-start | bytes 393224 | tf_op jit(solution)/shard_map/ppermute | solution.py:207
  21.6 5.9 %collective-permute-start.7 = (bf16[32,16,128]{2,1,0:T(8,128)(2,1)S(1)}, bf16[32,16,128]{2,1,0:T(8,128)(2,1)S(1)}, u32[]{:S(2)}, u32[]{:S(2)}) collective-permute-start(bf16[32,16,128]{2,1,0:T(8,128)(2,1)S(1)} %fusion.1.refs_2_), channel_id=1, source_target_pairs={{0,16},{4,20},{16,24},{20,28},{24,8},{28,12},{8,0},{12,4},{1,17},{... | collective-permute-start | bytes 393224 | tf_op jit(solution)/shard_map/ppermute | solution.py:206
  23.6 8.2 %collective-permute-start.9 = (bf16[32,16,128]{2,1,0:T(8,128)(2,1)S(1)}, bf16[32,16,128]{2,1,0:T(8,128)(2,1)S(1)}, u32[]{:S(2)}, u32[]{:S(2)}) collective-permute-start(bf16[32,16,128]{2,1,0:T(8,128)(2,1)S(1)} %fusion.1.refs_2_), channel_id=1, source_target_pairs={{16,0},{20,4},{24,16},{28,20},{8,24},{12,28},{0,8},{4,12},{17,1},{... | collective-permute-start | bytes 393224 | tf_op jit(solution)/shard_map/ppermute | solution.py:209
  27.5 6.9 %collective-permute-start.10 = (bf16[32,16,128]{2,1,0:T(8,128)(2,1)S(1)}, bf16[32,16,128]{2,1,0:T(8,128)(2,1)S(1)}, u32[]{:S(2)}, u32[]{:S(2)}) collective-permute-start(bf16[32,16,128]{2,1,0:T(8,128)(2,1)S(1)} %collective-permute-done.7.refs_3_), channel_id=1, source_target_pairs={{0,16},{4,20},{16,24},{20,28},{24,8},{28,12},{8,0},{12,4},{1,17},{... | collective-permute-start | bytes 393224 | tf_op jit(solution)/shard_map/ppermute | solution.py:210
  30.8 3.7 %collective-permute-start.11 = (bf16[32,16,128]{2,1,0:T(8,128)(2,1)S(1)}, bf16[32,16,128]{2,1,0:T(8,128)(2,1)S(1)}, u32[]{:S(2)}, u32[]{:S(2)}) collective-permute-start(bf16[32,16,128]{2,1,0:T(8,128)(2,1)S(1)} %collective-permute-done.7.refs_3_), channel_id=1, source_target_pairs={{0,4},{4,0},{8,12},{12,8},{16,20},{20,16},{24,28},{28,24},{1,5},{5... | collective-permute-start | bytes 393224 | tf_op jit(solution)/shard_map/ppermute | solution.py:227
  31.8 2.7 %collective-permute-start.12 = (bf16[32,16,128]{2,1,0:T(8,128)(2,1)S(1)}, bf16[32,16,128]{2,1,0:T(8,128)(2,1)S(1)}, u32[]{:S(2)}, u32[]{:S(2)}) collective-permute-start(bf16[32,16,128]{2,1,0:T(8,128)(2,1)S(1)} %collective-permute-done.9.refs_4_), channel_id=1, source_target_pairs={{0,4},{4,0},{8,12},{12,8},{16,20},{20,16},{24,28},{28,24},{1,5},{5... | collective-permute-start | bytes 393224 | tf_op jit(solution)/shard_map/ppermute | solution.py:227
  34.5 1.3 %collective-permute-start.13 = (bf16[32,16,128]{2,1,0:T(8,128)(2,1)S(1)}, bf16[32,16,128]{2,1,0:T(8,128)(2,1)S(1)}, u32[]{:S(2)}, u32[]{:S(2)}) collective-permute-start(bf16[32,16,128]{2,1,0:T(8,128)(2,1)S(1)} %collective-permute-done.10.refs_5_), channel_id=1, source_target_pairs={{0,4},{4,0},{8,12},{12,8},{16,20},{20,16},{24,28},{28,24},{1,5},{5... | collective-permute-start | bytes 393224 | tf_op jit(solution)/shard_map/ppermute | solution.py:227
  36.4 7.3 %collective-permute-start.16 = (bf16[32,16,128]{2,1,0:T(8,128)(2,1)S(1)}, bf16[32,16,128]{2,1,0:T(8,128)(2,1)S(1)}, u32[]{:S(2)}, u32[]{:S(2)}) collective-permute-start(bf16[32,16,128]{2,1,0:T(8,128)(2,1)S(1)} %get-tuple-element.28), channel_id=1, source_target_pairs={{0,3},{1,2},{2,1},{3,0},{4,7},{5,6},{6,5},{7,4},{8,11},{9,10},{10,... | collective-permute-start | bytes 393224 | tf_op jit(solution)/shard_map/ppermute | solution.py:230
  39.0 5.9 %collective-permute-start.14 = (bf16[32,16,128]{2,1,0:T(8,128)(2,1)S(1)}, bf16[32,16,128]{2,1,0:T(8,128)(2,1)S(1)}, u32[]{:S(2)}, u32[]{:S(2)}) collective-permute-start(bf16[32,16,128]{2,1,0:T(8,128)(2,1)S(1)} %get-tuple-element.26), channel_id=1, source_target_pairs={{0,1},{1,0},{2,3},{3,2},{4,5},{5,4},{6,7},{7,6},{8,9},{9,8},{10,11... | collective-permute-start | bytes 393224 | tf_op jit(solution)/shard_map/ppermute | solution.py:230
  39.1 6.6 %collective-permute-start.15 = (bf16[32,16,128]{2,1,0:T(8,128)(2,1)S(1)}, bf16[32,16,128]{2,1,0:T(8,128)(2,1)S(1)}, u32[]{:S(2)}, u32[]{:S(2)}) collective-permute-start(bf16[32,16,128]{2,1,0:T(8,128)(2,1)S(1)} %get-tuple-element.27), channel_id=1, source_target_pairs={{0,2},{1,3},{2,0},{3,1},{4,6},{5,7},{6,4},{7,5},{8,10},{9,11},{10,... | collective-permute-start | bytes 393224 | tf_op jit(solution)/shard_map/ppermute | solution.py:230

commit v8 on v7

--- a/solution.py
+++ b/solution.py
@@ -59,7 +59,7 @@
     parts = parts_of(ncol)
     key = sum((slice_ < low).astype(jnp.int32) for low, _ in parts[:-1])
     lane = lax.broadcasted_iota(jnp.int32, (1, nt), 1)
-    key = jnp.where(lane < count[0], key, len(parts)).astype(jnp.float32)
+    key = jnp.where(lane < count[...], key, len(parts)).astype(jnp.float32)
     across = lax.broadcasted_iota(jnp.int32, (nt, nt), 1).astype(jnp.float32)
     down = lax.broadcasted_iota(jnp.int32, (nt, nt), 0).astype(jnp.float32)
     same = across == down
@@ -152,7 +152,7 @@
     return pl.pallas_call(
         functools.partial(fetch, nrow, ncol, blk),
         out_shape=[VMEM(tiles.shape, tiles.dtype), SMEM(wide, jnp.int32)],
-        in_specs=[pl.BlockSpec(memory_space=HBM)] * 3 + [pl.BlockSpec(memory_space=SMEM)],
+        in_specs=[pl.BlockSpec(memory_space=HBM)] * 3 + [pl.BlockSpec(memory_space=VMEM)],
         out_specs=[pl.BlockSpec(memory_space=VMEM), pl.BlockSpec(memory_space=SMEM)],
         scratch_shapes=[VMEM((1, nt), jnp.int32)] * 2
         + [VMEM(wide, jnp.int32), pltpu.SemaphoreType.DMA((COPIES + 3,))],
@@ -198,13 +198,15 @@
 
 def gather_far(own, nrow):
     nz = nrow // 2
+    across = [(i, i ^ 1) for i in range(nrow)]
     if nz != 4:
-        return [lax.ppermute(own, "row", [(i, i ^ (2 * m)) for i in range(nrow)]) for m in range(1, nz)], lax.ppermute(own, "row", [(i, i ^ 1) for i in range(nrow)])
+        far = [lax.ppermute(own, "row", [(i, i ^ (2 * m)) for i in range(nrow)]) for m in range(1, nz)]
+        return far, lax.ppermute(own, "row", across)
     ring = [(0, 2), (2, 3), (3, 1), (1, 0)]
     ahead = [(2 * a + k, 2 * b + k) for a, b in ring for k in range(2)]
     back = [(b, a) for a, b in ahead]
     one = lax.ppermute(own, "row", ahead)
-    partner = lax.ppermute(own, "row", [(i, i ^ 1) for i in range(nrow)])
+    partner = lax.ppermute(own, "row", across)
     later, partner = lax.optimization_barrier((own, partner))
     other = lax.ppermute(later, "row", back)
     return [one, other, lax.ppermute(one, "row", ahead)], partner
@@ -235,13 +237,14 @@
     kind = lax.broadcasted_iota(jnp.int32, (2, 1, 1), 0)
     raw = jnp.where(kind == 0, labels[None], degree[None]).astype(jnp.float32)
     own = jnp.where(kind == 0, raw, 1.0 / jnp.sqrt(raw)).astype(jnp.bfloat16)
-    tiles, table = fetch_call(nrow, ncol, blk, tiles, tile_rows, tile_cols, tile_count)
+    own = lax.optimization_barrier(own)
+    other, count = lax.optimization_barrier((from_row(own, 1), jnp.broadcast_to(tile_count, (1, tiles.shape[0]))))
+    both = jnp.stack([own, other])
+    tiles, table = fetch_call(nrow, ncol, blk, tiles, tile_rows, tile_cols, count)
     for step in range(ITERS):
         if step > 0:
             own = (field * scale[:, None, :]).astype(jnp.bfloat16)
         if step == 0:
-            own = lax.optimization_barrier(own)
-            both = jnp.stack([own, from_row(own, 1)])
             fields = [both] + [from_row(both, 2 * m) for m in range(1, nz)]
         else:
             far, partner = gather_far(own, nrow)

time: 46.8 us -> 46.2 us (0.987)
  starting transfers between devices: 18.8 us -> 21.2 us
  waiting for transfers between devices: 19 us -> 16.7 us
  Pallas kernels: 6.18 us -> 5.34 us
    ppermute x6, starting transfers between devices: 7.25 us -> 8.99 us  [from_col(): return lax.ppermute(x, 'col', [(i, i ^ k) for i in range(ncol)])]
    ppermute x1, waiting for transfers between devices: 0.96 us -> 0.01 us  [gather_far(): other = lax.ppermute(later, 'row', back)]
    pallas_call x6, Pallas kernels: 3.9 us -> 3.06 us  [spread_calls(): pl.pallas_call(functools.partial(spread, seeded, first, index, (low, high...]
    ppermute x6, waiting for transfers between devices: 8.12 us -> 7.32 us  [from_col(): return lax.ppermute(x, 'col', [(i, i ^ k) for i in range(ncol)])]
    ppermute x1, waiting for transfers between devices: 2.7 us -> 2.12 us  [gather_far(): return ([one, other, lax.ppermute(one, 'row', ahead)], partner)]
    ppermute x7, starting transfers between devices: 6.11 us -> 6.67 us  [from_row(): return lax.ppermute(x, 'row', [(i, i ^ d) for i in range(nrow)])]
  transfers between devices with their start and end apart: 17 -> 17, of which waited for: 12 -> 11; matrix products, arithmetic and copies ran while one was open for 0% -> 0% of each run, Pallas kernels for 11% -> 9%
where the time goes in v8:
time: 46.2 us; the launch traced here: 45.7 us
  starting transfers between devices  21.2 us (46%)
  waiting for transfers between devices  16.7 us (36%)
  Pallas kernels  5.34 us (12%)
  other arithmetic  1.73 us (4%)
  between operations  0.76 us (2%)
    ppermute x6, starting transfers between devices, from_col(): return lax.ppermute(x, 'col', [(i, i ^ k) for i in range(ncol)])  8.99 us
    ppermute x6, waiting for transfers between devices, from_col(): return lax.ppermute(x, 'col', [(i, i ^ k) for i in range(ncol)])  7.32 us
    ppermute x7, starting transfers between devices, from_row(): return lax.ppermute(x, 'row', [(i, i ^ d) for i in range(nrow)])  6.67 us
    ppermute x1, waiting for transfers between devices, gather_far(): one = lax.ppermute(own, 'row', ahead)  3.85 us
    ppermute x7, waiting for transfers between devices, from_row(): return lax.ppermute(x, 'row', [(i, i ^ d) for i in range(nrow)])  3.41 us
    ppermute x1, starting transfers between devices, gather_far(): return ([one, other, lax.ppermute(one, 'row', ahead)], partner)  3.38 us
    pallas_call x6, Pallas kernels, spread_calls(): pl.pallas_call(functools.partial(spread, seeded, first, index, (low, high...  3.06 us
    pallas_call x1, Pallas kernels, fetch_call(): pl.pallas_call(functools.partial(fetch, nrow, ncol, blk), out_shape=[VMEM...  2.28 us
  transfers between devices with their start and end apart: 17, of which 11 were waited for; matrix products, arithmetic and copies ran while one was open for 0% of the time, Pallas kernels for 9%

profile of v8, /device:TPU:0, one launch (start us, length us, event | category | flops | bytes accessed | tf_op | source)
XLA Modules:
  0.0 45.7 jit_solution(6314027152324251245)
XLA Ops:
  0.0 0.8 %fusion.2 = bf16[2,32,128]{2,1,0:T(8,128)(2,1)S(1)} fusion(s32[32,128]{1,0:T(8,128)} %param.10, s32[32,128]{1,0:T(8,128)} %param.11, pred[2]{0:T(512)(128)(4,1)S(1)} %iota_compare_fusion.1), kind=kLoop, calls=%fused_computation.6 | loop fusion | flops 32768 | bytes 49154 | tf_op jit(solution)/shard_map/convert_element_type | solution.py:239
  0.8 0.5 %collective-permute-start = (bf16[2,32,128]{2,1,0:T(8,128)(2,1)S(1)}, bf16[2,32,128]{2,1,0:T(8,128)(2,1)S(1)}, u32[]{:S(2)}, u32[]{:S(2)}) collective-permute-start(bf16[2,32,128]{2,1,0:T(8,128)(2,1)S(1)} %fusion.2), channel_id=1, source_target_pairs={{0,4},{4,0},{8,12},{12,8},{16,20},{20,16},{24,28},{28,24},{1,5},{5... | collective-permute-start | bytes 49160 | tf_op jit(solution)/shard_map/ppermute | solution.py:229
  2.0 0.2 collective-permute-done
  2.2 5.0 %collective-permute-start.3 = (bf16[2,2,32,128]{3,2,1,0:T(8,128)(2,1)S(1)}, bf16[2,2,32,128]{3,2,1,0:T(8,128)(2,1)S(1)}, u32[]{:S(2)}, u32[]{:S(2)}) collective-permute-start(bf16[2,2,32,128]{3,2,1,0:T(8,128)(2,1)S(1)} %pad_maximum_fusion.refs_2_), channel_id=1, source_target_pairs={{0,24},{4,28},{8,16},{12,20},{16,8},{20,12},{24,0},{28,4},{1,25},{... | collective-permute-start | bytes 98312 | tf_op jit(solution)/shard_map/ppermute | solution.py:229
  7.2 0.0 collective-permute-start.2
  7.2 0.6 %collective-permute-start.1 = (bf16[2,2,32,128]{3,2,1,0:T(8,128)(2,1)S(1)}, bf16[2,2,32,128]{3,2,1,0:T(8,128)(2,1)S(1)}, u32[]{:S(2)}, u32[]{:S(2)}) collective-permute-start(bf16[2,2,32,128]{3,2,1,0:T(8,128)(2,1)S(1)} %pad_maximum_fusion.refs_2_), channel_id=1, source_target_pairs={{0,8},{4,12},{8,0},{12,4},{16,24},{20,28},{24,16},{28,20},{1,9},{5... | collective-permute-start | bytes 98312 | tf_op jit(solution)/shard_map/ppermute | solution.py:229
  7.8 2.3 %shard_map.67 = (bf16[128,128,128]{2,1,0:T(8,128)(2,1)S(1)}, s32[4,256]{1,0:T(4,128)S(4)}) custom-call(bf16[128,128,128]{2,1,0:T(8,128)(2,1)} %tiles_hbm.1, s32[1,128]{1,0:T(1,128)} %bitcast.8, s32[1,128]{1,0:T(1,128)} %bitcast.9, s32[1,128]{1,0:T(1,128)S(1)} %broadcast_in_dim.47.count), custom_call_target="tpu_custom_call" | custom-call | bytes 4194304 | tf_op jit(solution)/shard_map/pallas_call | solution.py:152
  10.1 0.0 collective-permute-done.3.refs_5_
  10.1 1.9 %collective-permute-done.2.refs_4_ = bf16[2,2,32,128]{3,2,1,0:T(8,128)(2,1)S(1)} collective-permute-done((bf16[2,2,32,128]{3,2,1,0:T(8,128)(2,1)S(1)}, bf16[2,2,32,128]{3,2,1,0:T(8,128)(2,1)S(1)}, u32[]{:S(2)}, u32[]{:S(2)}) %collective-permute-start.2) | collective-permute-done | bytes 32800 | tf_op jit(solution)/shard_map/ppermute | solution.py:229
  12.0 0.0 collective-permute-done.1.refs_3_
  12.0 0.0 copy-start.1
  12.0 0.5 %shard_map.68 = (bf16[32,16,128]{2,1,0:T(8,128)(2,1)S(1)}, f32[2,256,128]{2,1,0:T(8,128)S(1)}) custom-call(bf16[128,128,128]{2,1,0:T(8,128)(2,1)S(1)} %get-tuple-element.20.refs_0_, s32[4,256]{1,0:T(4,128)S(4)} %get-tuple-element.21.refs_1_, bf16[2,2,32,128]{3,2,1,0:T(8,128)(2,1)S(1)} %pad_maximum_fusion.refs_2_, ...), custom_call_target="tpu_custom_call" | custom-call | flops 16777216 | bytes 1048576 | tf_op jit(solution)/shard_map/pallas_call | solution.py:174
  12.5 2.5 %collective-permute-start.6 = (bf16[32,16,128]{2,1,0:T(8,128)(2,1)S(1)}, bf16[32,16,128]{2,1,0:T(8,128)(2,1)S(1)}, u32[]{:S(2)}, u32[]{:S(2)}) collective-permute-start(bf16[32,16,128]{2,1,0:T(8,128)(2,1)S(1)} %get-tuple-element.26), channel_id=1, source_target_pairs={{0,3},{1,2},{2,1},{3,0},{4,7},{5,6},{6,5},{7,4},{8,11},{9,10},{10,... | collective-permute-start | bytes 393224 | tf_op jit(solution)/shard_map/ppermute | solution.py:232
  15.0 0.0 copy-start
  15.0 0.5 %shard_map.70 = (bf16[32,16,128]{2,1,0:T(8,128)(2,1)S(1)}, bf16[32,16,128]{2,1,0:T(8,128)(2,1)S(1)}) custom-call(bf16[128,128,128]{2,1,0:T(8,128)(2,1)S(1)} %get-tuple-element.20.refs_0_, s32[4,256]{1,0:T(4,128)S(4)} %get-tuple-element.21.refs_1_, f32[2,256,128]{2,1,0:T(8,128)S(1)} %get-tuple-element.23.refs_2_), custom_call_target="tpu_custom_call" | custom-call | flops 33554432 | bytes 2097152 | tf_op jit(solution)/shard_map/pallas_call | solution.py:174
  15.5 1.0 %collective-permute-start.4 = (bf16[32,16,128]{2,1,0:T(8,128)(2,1)S(1)}, bf16[32,16,128]{2,1,0:T(8,128)(2,1)S(1)}, u32[]{:S(2)}, u32[]{:S(2)}) collective-permute-start(bf16[32,16,128]{2,1,0:T(8,128)(2,1)S(1)} %get-tuple-element.24), channel_id=1, source_target_pairs={{0,1},{1,0},{2,3},{3,2},{4,5},{5,4},{6,7},{7,6},{8,9},{9,8},{10,11... | collective-permute-start | bytes 393224 | tf_op jit(solution)/shard_map/ppermute | solution.py:232
  16.6 0.9 %collective-permute-start.5 = (bf16[32,16,128]{2,1,0:T(8,128)(2,1)S(1)}, bf16[32,16,128]{2,1,0:T(8,128)(2,1)S(1)}, u32[]{:S(2)}, u32[]{:S(2)}) collective-permute-start(bf16[32,16,128]{2,1,0:T(8,128)(2,1)S(1)} %get-tuple-element.25), channel_id=1, source_target_pairs={{0,2},{1,3},{2,0},{3,1},{4,6},{5,7},{6,4},{7,5},{8,10},{9,11},{10,... | collective-permute-start | bytes 393224 | tf_op jit(solution)/shard_map/ppermute | solution.py:232
  17.5 0.0 copy-done.1
  17.5 0.5 %shard_map.69 = f32[32,16,128]{2,1,0:T(8,128)S(1)} custom-call(bf16[128,128,128]{2,1,0:T(8,128)(2,1)S(1)} %get-tuple-element.20.refs_0_, s32[4,256]{1,0:T(4,128)S(4)} %get-tuple-element.21.refs_1_, f32[2,256,128]{2,1,0:T(8,128)S(1)} %get-tuple-element.23.refs_2_), custom_call_target="tpu_custom_call" | custom-call | flops 16777216 | bytes 1048576 | tf_op jit(solution)/shard_map/pallas_call | solution.py:174
  18.0 1.5 %collective-permute-done.6 = bf16[32,16,128]{2,1,0:T(8,128)(2,1)S(1)} collective-permute-done((bf16[32,16,128]{2,1,0:T(8,128)(2,1)S(1)}, bf16[32,16,128]{2,1,0:T(8,128)(2,1)S(1)}, u32[]{:S(2)}, u32[]{:S(2)}) %collective-permute-start.6) | collective-permute-done | bytes 131104 | tf_op jit(solution)/shard_map/ppermute | solution.py:232
  19.5 1.6 %collective-permute-done.4 = bf16[32,16,128]{2,1,0:T(8,128)(2,1)S(1)} collective-permute-done((bf16[32,16,128]{2,1,0:T(8,128)(2,1)S(1)}, bf16[32,16,128]{2,1,0:T(8,128)(2,1)S(1)}, u32[]{:S(2)}, u32[]{:S(2)}) %collective-permute-start.4) | collective-permute-done | bytes 131104 | tf_op jit(solution)/shard_map/ppermute | solution.py:232
  21.2 0.4 collective-permute-done.5
  21.6 0.0 copy-done
  21.6 0.1 fusion.1.refs_2_
  21.7 0.1 collective-permute-start.8
  21.7 2.1 %collective-permute-start.7 = (bf16[32,16,128]{2,1,0:T(8,128)(2,1)S(1)}, bf16[32,16,128]{2,1,0:T(8,128)(2,1)S(1)}, u32[]{:S(2)}, u32[]{:S(2)}) collective-permute-start(bf16[32,16,128]{2,1,0:T(8,128)(2,1)S(1)} %fusion.1.refs_2_), channel_id=1, source_target_pairs={{0,16},{4,20},{16,24},{20,28},{24,8},{28,12},{8,0},{12,4},{1,17},{... | collective-permute-start | bytes 393224 | tf_op jit(solution)/shard_map/ppermute | solution.py:208
  23.8 0.0 collective-permute-done.8.refs_6_
  23.8 0.0 collective-permute-start.9
  23.8 3.8 %collective-permute-done.7.refs_3_ = bf16[32,16,128]{2,1,0:T(8,128)(2,1)S(1)} collective-permute-done((bf16[32,16,128]{2,1,0:T(8,128)(2,1)S(1)}, bf16[32,16,128]{2,1,0:T(8,128)(2,1)S(1)}, u32[]{:S(2)}, u32[]{:S(2)}) %collective-permute-start.7) | collective-permute-done | bytes 131104 | tf_op jit(solution)/shard_map/ppermute | solution.py:208
  27.7 3.4 %collective-permute-start.10 = (bf16[32,16,128]{2,1,0:T(8,128)(2,1)S(1)}, bf16[32,16,128]{2,1,0:T(8,128)(2,1)S(1)}, u32[]{:S(2)}, u32[]{:S(2)}) collective-permute-start(bf16[32,16,128]{2,1,0:T(8,128)(2,1)S(1)} %collective-permute-done.7.refs_3_), channel_id=1, source_target_pairs={{0,16},{4,20},{16,24},{20,28},{24,8},{28,12},{8,0},{12,4},{1,17},{... | collective-permute-start | bytes 393224 | tf_op jit(solution)/shard_map/ppermute | solution.py:212
  31.1 0.0 collective-permute-start.11
  31.1 0.0 collective-permute-done.9.refs_4_
  31.1 0.5 %collective-permute-start.12 = (bf16[32,16,128]{2,1,0:T(8,128)(2,1)S(1)}, bf16[32,16,128]{2,1,0:T(8,128)(2,1)S(1)}, u32[]{:S(2)}, u32[]{:S(2)}) collective-permute-start(bf16[32,16,128]{2,1,0:T(8,128)(2,1)S(1)} %collective-permute-done.9.refs_4_), channel_id=1, source_target_pairs={{0,4},{4,0},{8,12},{12,8},{16,20},{20,16},{24,28},{28,24},{1,5},{5... | collective-permute-start | bytes 393224 | tf_op jit(solution)/shard_map/ppermute | solution.py:229
  31.6 2.1 %collective-permute-done.10.refs_5_ = bf16[32,16,128]{2,1,0:T(8,128)(2,1)S(1)} collective-permute-done((bf16[32,16,128]{2,1,0:T(8,128)(2,1)S(1)}, bf16[32,16,128]{2,1,0:T(8,128)(2,1)S(1)}, u32[]{:S(2)}, u32[]{:S(2)}) %collective-permute-start.10) | collective-permute-done | bytes 131104 | tf_op jit(solution)/shard_map/ppermute | solution.py:212
  33.7 0.0 collective-permute-start.13
  33.7 0.0 collective-permute-done.11.refs_7_
  33.7 0.0 collective-permute-done.12.refs_8_
  33.7 1.3 %collective-permute-done.13.refs_9_ = bf16[32,16,128]{2,1,0:T(8,128)(2,1)S(1)} collective-permute-done((bf16[32,16,128]{2,1,0:T(8,128)(2,1)S(1)}, bf16[32,16,128]{2,1,0:T(8,128)(2,1)S(1)}, u32[]{:S(2)}, u32[]{:S(2)}) %collective-permute-start.13) | collective-permute-done | bytes 131104 | tf_op jit(solution)/shard_map/ppermute | solution.py:229
  35.0 0.6 %shard_map.71 = (bf16[32,16,128]{2,1,0:T(8,128)(2,1)S(1)}, bf16[256,16,128]{2,1,0:T(8,128)(2,1)S(1)}) custom-call(bf16[128,128,128]{2,1,0:T(8,128)(2,1)S(1)} %get-tuple-element.20.refs_0_, s32[4,256]{1,0:T(4,128)S(4)} %get-tuple-element.21.refs_1_, bf16[32,16,128]{2,1,0:T(8,128)(2,1)S(1)} %fusion.1.refs_2_, ...), custom_call_target="tpu_custom_call" | custom-call | flops 16777216 | bytes 1048576 | tf_op jit(solution)/shard_map/pallas_call | solution.py:174
  35.6 2.0 %collective-permute-start.16 = (bf16[32,16,128]{2,1,0:T(8,128)(2,1)S(1)}, bf16[32,16,128]{2,1,0:T(8,128)(2,1)S(1)}, u32[]{:S(2)}, u32[]{:S(2)}) collective-permute-start(bf16[32,16,128]{2,1,0:T(8,128)(2,1)S(1)} %get-tuple-element.32), channel_id=1, source_target_pairs={{0,3},{1,2},{2,1},{3,0},{4,7},{5,6},{6,5},{7,4},{8,11},{9,10},{10,... | collective-permute-start | bytes 393224 | tf_op jit(solution)/shard_map/ppermute | solution.py:232
  37.6 0.5 %shard_map.73 = (bf16[32,16,128]{2,1,0:T(8,128)(2,1)S(1)}, bf16[32,16,128]{2,1,0:T(8,128)(2,1)S(1)}) custom-call(bf16[128,128,128]{2,1,0:T(8,128)(2,1)S(1)} %get-tuple-element.20.refs_0_, s32[4,256]{1,0:T(4,128)S(4)} %get-tuple-element.21.refs_1_, bf16[256,16,128]{2,1,0:T(8,128)(2,1)S(1)} %get-tuple-element.29.refs_2_), custom_call_target="tpu_custom_call" | custom-call | flops 33554432 | bytes 2097152 | tf_op jit(solution)/shard_map/pallas_call | solution.py:174
  38.1 1.2 %collective-permute-start.14 = (bf16[32,16,128]{2,1,0:T(8,128)(2,1)S(1)}, bf16[32,16,128]{2,1,0:T(8,128)(2,1)S(1)}, u32[]{:S(2)}, u32[]{:S(2)}) collective-permute-start(bf16[32,16,128]{2,1,0:T(8,128)(2,1)S(1)} %get-tuple-element.30), channel_id=1, source_target_pairs={{0,1},{1,0},{2,3},{3,2},{4,5},{5,4},{6,7},{7,6},{8,9},{9,8},{10,11... | collective-permute-start | bytes 393224 | tf_op jit(solution)/shard_map/ppermute | solution.py:232
  39.3 1.4 %collective-permute-start.15 = (bf16[32,16,128]{2,1,0:T(8,128)(2,1)S(1)}, bf16[32,16,128]{2,1,0:T(8,128)(2,1)S(1)}, u32[]{:S(2)}, u32[]{:S(2)}) collective-permute-start(bf16[32,16,128]{2,1,0:T(8,128)(2,1)S(1)} %get-tuple-element.31), channel_id=1, source_target_pairs={{0,2},{1,3},{2,0},{3,1},{4,6},{5,7},{6,4},{7,5},{8,10},{9,11},{10,... | collective-permute-start | bytes 393224 | tf_op jit(solution)/shard_map/ppermute | solution.py:232
  40.6 0.5 %shard_map.72 = f32[32,16,128]{2,1,0:T(8,128)S(1)} custom-call(bf16[128,128,128]{2,1,0:T(8,128)(2,1)S(1)} %get-tuple-element.20.refs_0_, s32[4,256]{1,0:T(4,128)S(4)} %get-tuple-element.21.refs_1_, bf16[256,16,128]{2,1,0:T(8,128)(2,1)S(1)} %get-tuple-element.29.refs_2_), custom_call_target="tpu_custom_call" | custom-call | flops 16777216 | bytes 1048576 | tf_op jit(solution)/shard_map/pallas_call | solution.py:174
  41.1 1.6 %collective-permute-done.16 = bf16[32,16,128]{2,1,0:T(8,128)(2,1)S(1)} collective-permute-done((bf16[32,16,128]{2,1,0:T(8,128)(2,1)S(1)}, bf16[32,16,128]{2,1,0:T(8,128)(2,1)S(1)}, u32[]{:S(2)}, u32[]{:S(2)}) %collective-permute-start.16) | collective-permute-done | bytes 131104 | tf_op jit(solution)/shard_map/ppermute | solution.py:232
  42.8 1.8 %collective-permute-done.14 = bf16[32,16,128]{2,1,0:T(8,128)(2,1)S(1)} collective-permute-done((bf16[32,16,128]{2,1,0:T(8,128)(2,1)S(1)}, bf16[32,16,128]{2,1,0:T(8,128)(2,1)S(1)}, u32[]{:S(2)}, u32[]{:S(2)}) %collective-permute-start.14) | collective-permute-done | bytes 131104 | tf_op jit(solution)/shard_map/ppermute | solution.py:232
  44.6 0.4 collective-permute-done.15
  44.9 0.8 %select_add_fusion = f32[32,16,128]{2,1,0:T(8,128)} fusion(bf16[32,16,128]{2,1,0:T(8,128)(2,1)S(1)} %collective-permute-done.16, bf16[32,16,128]{2,1,0:T(8,128)(2,1)S(1)} %collective-permute-done.15, f32[32,16,128]{2,1,0:T(8,128)S(1)} %shard_map.72, bf16[32,16,128]{2,1,0:T(8,128)(2,1)S(1)} %collective-permute-done.14, s32[32,128]{1,0:T(8,128)S(1)} %copy-done, ...), kind=kLoop, calls=%fused_computation | loop fusion | flops 655360 | bytes 950272 | tf_op jit(solution)/shard_map/add | solution.py:256
  (4 shorter events, 0.0 us)
Async XLA Ops:
  0.8 1.4 %collective-permute-start = (bf16[2,32,128]{2,1,0:T(8,128)(2,1)S(1)}, bf16[2,32,128]{2,1,0:T(8,128)(2,1)S(1)}, u32[]{:S(2)}, u32[]{:S(2)}) collective-permute-start(bf16[2,32,128]{2,1,0:T(8,128)(2,1)S(1)} %fusion.2), channel_id=1, source_target_pairs={{0,4},{4,0},{8,12},{12,8},{16,20},{20,16},{24,28},{28,24},{1,5},{5... | collective-permute-start | bytes 49160 | tf_op jit(solution)/shard_map/ppermute | solution.py:229
  2.2 7.9 %collective-permute-start.3 = (bf16[2,2,32,128]{3,2,1,0:T(8,128)(2,1)S(1)}, bf16[2,2,32,128]{3,2,1,0:T(8,128)(2,1)S(1)}, u32[]{:S(2)}, u32[]{:S(2)}) collective-permute-start(bf16[2,2,32,128]{3,2,1,0:T(8,128)(2,1)S(1)} %pad_maximum_fusion.refs_2_), channel_id=1, source_target_pairs={{0,24},{4,28},{8,16},{12,20},{16,8},{20,12},{24,0},{28,4},{1,25},{... | collective-permute-start | bytes 98312 | tf_op jit(solution)/shard_map/ppermute | solution.py:229
  7.2 4.8 %collective-permute-start.2 = (bf16[2,2,32,128]{3,2,1,0:T(8,128)(2,1)S(1)}, bf16[2,2,32,128]{3,2,1,0:T(8,128)(2,1)S(1)}, u32[]{:S(2)}, u32[]{:S(2)}) collective-permute-start(bf16[2,2,32,128]{3,2,1,0:T(8,128)(2,1)S(1)} %pad_maximum_fusion.refs_2_), channel_id=1, source_target_pairs={{0,16},{4,20},{8,24},{12,28},{16,0},{20,4},{24,8},{28,12},{1,17},{... | collective-permute-start | bytes 98312 | tf_op jit(solution)/shard_map/ppermute | solution.py:229
  7.2 4.8 %collective-permute-start.1 = (bf16[2,2,32,128]{3,2,1,0:T(8,128)(2,1)S(1)}, bf16[2,2,32,128]{3,2,1,0:T(8,128)(2,1)S(1)}, u32[]{:S(2)}, u32[]{:S(2)}) collective-permute-start(bf16[2,2,32,128]{3,2,1,0:T(8,128)(2,1)S(1)} %pad_maximum_fusion.refs_2_), channel_id=1, source_target_pairs={{0,8},{4,12},{8,0},{12,4},{16,24},{20,28},{24,16},{28,20},{1,9},{5... | collective-permute-start | bytes 98312 | tf_op jit(solution)/shard_map/ppermute | solution.py:229
  12.0 5.5 %copy-start.1 = (s32[32,128]{1,0:T(8,128)S(1)}, s32[32,128]{1,0:T(8,128)}, u32[]{:S(2)}) copy-start(s32[32,128]{1,0:T(8,128)} %param.10) | copy-start | bytes 49156
  12.5 7.0 %collective-permute-start.6 = (bf16[32,16,128]{2,1,0:T(8,128)(2,1)S(1)}, bf16[32,16,128]{2,1,0:T(8,128)(2,1)S(1)}, u32[]{:S(2)}, u32[]{:S(2)}) collective-permute-start(bf16[32,16,128]{2,1,0:T(8,128)(2,1)S(1)} %get-tuple-element.26), channel_id=1, source_target_pairs={{0,3},{1,2},{2,1},{3,0},{4,7},{5,6},{6,5},{7,4},{8,11},{9,10},{10,... | collective-permute-start | bytes 393224 | tf_op jit(solution)/shard_map/ppermute | solution.py:232
  15.0 6.5 %copy-start = (s32[32,128]{1,0:T(8,128)S(1)}, s32[32,128]{1,0:T(8,128)}, u32[]{:S(2)}) copy-start(s32[32,128]{1,0:T(8,128)} %param.11) | copy-start | bytes 49156
  15.5 5.6 %collective-permute-start.4 = (bf16[32,16,128]{2,1,0:T(8,128)(2,1)S(1)}, bf16[32,16,128]{2,1,0:T(8,128)(2,1)S(1)}, u32[]{:S(2)}, u32[]{:S(2)}) collective-permute-start(bf16[32,16,128]{2,1,0:T(8,128)(2,1)S(1)} %get-tuple-element.24), channel_id=1, source_target_pairs={{0,1},{1,0},{2,3},{3,2},{4,5},{5,4},{6,7},{7,6},{8,9},{9,8},{10,11... | collective-permute-start | bytes 393224 | tf_op jit(solution)/shard_map/ppermute | solution.py:232
  16.6 5.0 %collective-permute-start.5 = (bf16[32,16,128]{2,1,0:T(8,128)(2,1)S(1)}, bf16[32,16,128]{2,1,0:T(8,128)(2,1)S(1)}, u32[]{:S(2)}, u32[]{:S(2)}) collective-permute-start(bf16[32,16,128]{2,1,0:T(8,128)(2,1)S(1)} %get-tuple-element.25), channel_id=1, source_target_pairs={{0,2},{1,3},{2,0},{3,1},{4,6},{5,7},{6,4},{7,5},{8,10},{9,11},{10,... | collective-permute-start | bytes 393224 | tf_op jit(solution)/shard_map/ppermute | solution.py:232
  21.7 2.2 %collective-permute-start.8 = (bf16[32,16,128]{2,1,0:T(8,128)(2,1)S(1)}, bf16[32,16,128]{2,1,0:T(8,128)(2,1)S(1)}, u32[]{:S(2)}, u32[]{:S(2)}) collective-permute-start(bf16[32,16,128]{2,1,0:T(8,128)(2,1)S(1)} %fusion.1.refs_2_), channel_id=1, source_target_pairs={{0,4},{4,0},{8,12},{12,8},{16,20},{20,16},{24,28},{28,24},{1,5},{5... | collective-permute-start | bytes 393224 | tf_op jit(solution)/shard_map/ppermute | solution.py:209
  21.7 5.9 %collective-permute-start.7 = (bf16[32,16,128]{2,1,0:T(8,128)(2,1)S(1)}, bf16[32,16,128]{2,1,0:T(8,128)(2,1)S(1)}, u32[]{:S(2)}, u32[]{:S(2)}) collective-permute-start(bf16[32,16,128]{2,1,0:T(8,128)(2,1)S(1)} %fusion.1.refs_2_), channel_id=1, source_target_pairs={{0,16},{4,20},{16,24},{20,28},{24,8},{28,12},{8,0},{12,4},{1,17},{... | collective-permute-start | bytes 393224 | tf_op jit(solution)/shard_map/ppermute | solution.py:208
  23.8 7.2 %collective-permute-start.9 = (bf16[32,16,128]{2,1,0:T(8,128)(2,1)S(1)}, bf16[32,16,128]{2,1,0:T(8,128)(2,1)S(1)}, u32[]{:S(2)}, u32[]{:S(2)}) collective-permute-start(bf16[32,16,128]{2,1,0:T(8,128)(2,1)S(1)} %fusion.1.refs_2_), channel_id=1, source_target_pairs={{16,0},{20,4},{24,16},{28,20},{8,24},{12,28},{0,8},{4,12},{17,1},{... | collective-permute-start | bytes 393224 | tf_op jit(solution)/shard_map/ppermute | solution.py:211
  27.7 6.0 %collective-permute-start.10 = (bf16[32,16,128]{2,1,0:T(8,128)(2,1)S(1)}, bf16[32,16,128]{2,1,0:T(8,128)(2,1)S(1)}, u32[]{:S(2)}, u32[]{:S(2)}) collective-permute-start(bf16[32,16,128]{2,1,0:T(8,128)(2,1)S(1)} %collective-permute-done.7.refs_3_), channel_id=1, source_target_pairs={{0,16},{4,20},{16,24},{20,28},{24,8},{28,12},{8,0},{12,4},{1,17},{... | collective-permute-start | bytes 393224 | tf_op jit(solution)/shard_map/ppermute | solution.py:212
  31.1 2.6 %collective-permute-start.11 = (bf16[32,16,128]{2,1,0:T(8,128)(2,1)S(1)}, bf16[32,16,128]{2,1,0:T(8,128)(2,1)S(1)}, u32[]{:S(2)}, u32[]{:S(2)}) collective-permute-start(bf16[32,16,128]{2,1,0:T(8,128)(2,1)S(1)} %collective-permute-done.7.refs_3_), channel_id=1, source_target_pairs={{0,4},{4,0},{8,12},{12,8},{16,20},{20,16},{24,28},{28,24},{1,5},{5... | collective-permute-start | bytes 393224 | tf_op jit(solution)/shard_map/ppermute | solution.py:229
  31.1 2.6 %collective-permute-start.12 = (bf16[32,16,128]{2,1,0:T(8,128)(2,1)S(1)}, bf16[32,16,128]{2,1,0:T(8,128)(2,1)S(1)}, u32[]{:S(2)}, u32[]{:S(2)}) collective-permute-start(bf16[32,16,128]{2,1,0:T(8,128)(2,1)S(1)} %collective-permute-done.9.refs_4_), channel_id=1, source_target_pairs={{0,4},{4,0},{8,12},{12,8},{16,20},{20,16},{24,28},{28,24},{1,5},{5... | collective-permute-start | bytes 393224 | tf_op jit(solution)/shard_map/ppermute | solution.py:229
  33.7 1.3 %collective-permute-start.13 = (bf16[32,16,128]{2,1,0:T(8,128)(2,1)S(1)}, bf16[32,16,128]{2,1,0:T(8,128)(2,1)S(1)}, u32[]{:S(2)}, u32[]{:S(2)}) collective-permute-start(bf16[32,16,128]{2,1,0:T(8,128)(2,1)S(1)} %collective-permute-done.10.refs_5_), channel_id=1, source_target_pairs={{0,4},{4,0},{8,12},{12,8},{16,20},{20,16},{24,28},{28,24},{1,5},{5... | collective-permute-start | bytes 393224 | tf_op jit(solution)/shard_map/ppermute | solution.py:229
  35.6 7.2 %collective-permute-start.16 = (bf16[32,16,128]{2,1,0:T(8,128)(2,1)S(1)}, bf16[32,16,128]{2,1,0:T(8,128)(2,1)S(1)}, u32[]{:S(2)}, u32[]{:S(2)}) collective-permute-start(bf16[32,16,128]{2,1,0:T(8,128)(2,1)S(1)} %get-tuple-element.32), channel_id=1, source_target_pairs={{0,3},{1,2},{2,1},{3,0},{4,7},{5,6},{6,5},{7,4},{8,11},{9,10},{10,... | collective-permute-start | bytes 393224 | tf_op jit(solution)/shard_map/ppermute | solution.py:232
  38.1 6.5 %collective-permute-start.14 = (bf16[32,16,128]{2,1,0:T(8,128)(2,1)S(1)}, bf16[32,16,128]{2,1,0:T(8,128)(2,1)S(1)}, u32[]{:S(2)}, u32[]{:S(2)}) collective-permute-start(bf16[32,16,128]{2,1,0:T(8,128)(2,1)S(1)} %get-tuple-element.30), channel_id=1, source_target_pairs={{0,1},{1,0},{2,3},{3,2},{4,5},{5,4},{6,7},{7,6},{8,9},{9,8},{10,11... | collective-permute-start | bytes 393224 | tf_op jit(solution)/shard_map/ppermute | solution.py:232
  39.3 5.7 %collective-permute-start.15 = (bf16[32,16,128]{2,1,0:T(8,128)(2,1)S(1)}, bf16[32,16,128]{2,1,0:T(8,128)(2,1)S(1)}, u32[]{:S(2)}, u32[]{:S(2)}) collective-permute-start(bf16[32,16,128]{2,1,0:T(8,128)(2,1)S(1)} %get-tuple-element.31), channel_id=1, source_target_pairs={{0,2},{1,3},{2,0},{3,1},{4,6},{5,7},{6,4},{7,5},{8,10},{9,11},{10,... | collective-permute-start | bytes 393224 | tf_op jit(solution)/shard_map/ppermute | solution.py:232

commit v9 on v8

--- a/solution.py
+++ b/solution.py
@@ -124,10 +124,12 @@
             return jnp.where(label == query, scale, 0.0).astype(jnp.bfloat16)
         return picks[place]
 
+    unroll = (24, 32, 16)[index]
+
     def step(i, carry):
-        base = begin + i * UNROLL
+        base = begin + i * unroll
         terms = []
-        for u in range(0, UNROLL, 2):
+        for u in range(0, unroll, 2):
             t = base + u
             pair = lax.dot_general(
                 jnp.concatenate([pick(t), pick(t + 1)], 0),
@@ -136,12 +138,12 @@
                 preferred_element_type=jnp.float32,
             )
             terms += [pair[:QC, :128], pair[QC:, 128:]]
-        for u in range(UNROLL):
+        for u in range(unroll):
             t = base + u
             total[jnp.where(t < end, table[1, t] - low * blk, (high - low) * blk)] += terms[u]
         return carry
 
-    lax.fori_loop(0, lax.div(end - begin + (UNROLL - 1), UNROLL), step, 0)
+    lax.fori_loop(0, lax.div(end - begin + (unroll - 1), unroll), step, 0)
     for k in range(high - low):
         outs[k][...] = total[pl.ds(k * blk, blk)].astype(outs[k].dtype)
 
@@ -196,17 +198,47 @@
     return slices
 
 
+def finish(ncol, *refs):
+    own, came, scale, labels, out, field, sem = refs[0], refs[1:ncol], *refs[ncol:]
+    blk = own.shape[0]
+    part = blk // 4
+    query = lax.broadcasted_iota(jnp.int32, (QC, 128), 0)
+    copies = []
+    for i in range(4):
+        for b in range(i * part, (i + 1) * part):
+            summed = own[b]
+            for x in came:
+                summed = summed + x[b].astype(jnp.float32)
+            prior = jnp.where(labels[pl.ds(b, 1), :] == query, 0.2, 0.0)
+            field[b] = 0.8 * scale[pl.ds(b, 1), :] * summed + prior
+        some = pl.ds(i * part, part)
+        copies.append(pltpu.make_async_copy(field.at[some], out.at[some], sem.at[i]))
+        copies[-1].start()
+    for c in copies:
+        c.wait()
+
+
+def finish_call(own, came, scale, labels):
+    return pl.pallas_call(
+        functools.partial(finish, 1 + len(came)),
+        out_shape=jax.ShapeDtypeStruct(own.shape, jnp.float32),
+        in_specs=[pl.BlockSpec(memory_space=VMEM)] * (3 + len(came)),
+        out_specs=pl.BlockSpec(memory_space=pl.ANY),
+        scratch_shapes=[VMEM(own.shape, jnp.float32), pltpu.SemaphoreType.DMA((4,))],
+        compiler_params=pltpu.CompilerParams(vmem_limit_bytes=16 << 20),
+        cost_estimate=pl.CostEstimate(flops=8 * own.size, bytes_accessed=12 * own.size, transcendentals=0),
+    )(own, *came, scale, labels)
+
+
 def gather_far(own, nrow):
     nz = nrow // 2
-    across = [(i, i ^ 1) for i in range(nrow)]
     if nz != 4:
-        far = [lax.ppermute(own, "row", [(i, i ^ (2 * m)) for i in range(nrow)]) for m in range(1, nz)]
-        return far, lax.ppermute(own, "row", across)
+        return [lax.ppermute(own, "row", [(i, i ^ (2 * m)) for i in range(nrow)]) for m in range(1, nz)], lax.ppermute(own, "row", [(i, i ^ 1) for i in range(nrow)])
     ring = [(0, 2), (2, 3), (3, 1), (1, 0)]
     ahead = [(2 * a + k, 2 * b + k) for a, b in ring for k in range(2)]
     back = [(b, a) for a, b in ahead]
     one = lax.ppermute(own, "row", ahead)
-    partner = lax.ppermute(own, "row", across)
+    partner = lax.ppermute(own, "row", [(i, i ^ 1) for i in range(nrow)])
     later, partner = lax.optimization_barrier((own, partner))
     other = lax.ppermute(later, "row", back)
     return [one, other, lax.ppermute(one, "row", ahead)], partner
@@ -250,9 +282,12 @@
             far, partner = gather_far(own, nrow)
             fields = [own] + far + [partner] + [from_row(x, 1) for x in far]
         outs = spread_calls(step == 0, nrow, ncol, blk, tiles, table, fields)
+        came = [from_col(outs[k], k) for k in range(1, ncol)]
+        if step == ITERS - 1:
+            return finish_call(outs[0], came, scale, labels)
         summed = outs[0]
-        for k in range(1, ncol):
-            summed = summed + from_col(outs[k], k).astype(jnp.float32)
+        for x in came:
+            summed = summed + x.astype(jnp.float32)
         field = 0.8 * scale[:, None, :] * summed + 0.2 * prior
     return field
 

time: 46.2 us -> 46.1 us (level)
  Pallas kernels: 5.34 us -> 7.06 us
  starting transfers between devices: 21.2 us -> 19.7 us
  other arithmetic: 1.73 us -> 0.94 us
  waiting for transfers between devices: 16.7 us -> 17.3 us
    ppermute x6, starting transfers between devices: 8.99 us -> 7.2 us  [from_col(): return lax.ppermute(x, 'col', [(i, i ^ k) for i in range(ncol)])]
    pallas_call x6, Pallas kernels: 3.06 us -> 4.01 us  [spread_calls(): pl.pallas_call(functools.partial(spread, seeded, first, index, (low, high...]
    add x1 -> x0, other arithmetic: 0.79 us -> none  [local(): field = 0.8 * scale[:, None, :] * summed + 0.2 * prior]
    pallas_call x0 -> x1, Pallas kernels: none -> 0.76 us  [finish_call(): pl.pallas_call(functools.partial(finish, 1 + len(came)), out_shape=jax.Sh...]
    ppermute x6, waiting for transfers between devices: 7.32 us -> 8.05 us  [from_col(): return lax.ppermute(x, 'col', [(i, i ^ k) for i in range(ncol)])]
  transfers between devices with their start and end apart: 17 -> 17, of which waited for: 11 -> 11; matrix products, arithmetic and copies ran while one was open for 0% -> 0% of each run, Pallas kernels for 9% -> 12%
where the time goes in v9:
time: 46.1 us; the launch traced here: 45.8 us
  starting transfers between devices  19.7 us (43%)
  waiting for transfers between devices  17.3 us (38%)
  Pallas kernels  7.06 us (15%)
  other arithmetic  0.94 us (2%)
  between operations  0.76 us (2%)
    ppermute x6, waiting for transfers between devices, from_col(): return lax.ppermute(x, 'col', [(i, i ^ k) for i in range(ncol)])  8.05 us
    ppermute x6, starting transfers between devices, from_col(): return lax.ppermute(x, 'col', [(i, i ^ k) for i in range(ncol)])  7.2 us
    ppermute x7, starting transfers between devices, from_row(): return lax.ppermute(x, 'row', [(i, i ^ d) for i in range(nrow)])  6.67 us
    pallas_call x6, Pallas kernels, spread_calls(): pl.pallas_call(functools.partial(spread, seeded, first, index, (low, high...  4.01 us
    ppermute x1, waiting for transfers between devices, gather_far(): one = lax.ppermute(own, 'row', ahead)  3.85 us
    ppermute x7, waiting for transfers between devices, from_row(): return lax.ppermute(x, 'row', [(i, i ^ d) for i in range(nrow)])  3.41 us
    ppermute x1, starting transfers between devices, gather_far(): return ([one, other, lax.ppermute(one, 'row', ahead)], partner)  3.38 us
    ppermute x1, starting transfers between devices, gather_far(): one = lax.ppermute(own, 'row', ahead)  2.37 us
  transfers between devices with their start and end apart: 17, of which 11 were waited for; matrix products, arithmetic and copies ran while one was open for 0% of the time, Pallas kernels for 12%

profile of v9, /device:TPU:0, one launch (start us, length us, event | category | flops | bytes accessed | tf_op | source)
XLA Modules:
  0.0 45.8 jit_solution(2814502384460682597)
XLA Ops:
  0.0 0.8 %fusion = bf16[2,32,128]{2,1,0:T(8,128)(2,1)S(1)} fusion(s32[32,128]{1,0:T(8,128)} %param.10, s32[32,128]{1,0:T(8,128)} %refs_5_.1, pred[2]{0:T(512)(128)(4,1)S(1)} %iota_compare_fusion.1), kind=kLoop, calls=%fused_computation.3 | loop fusion | flops 32768 | bytes 49154 | tf_op jit(solution)/shard_map/convert_element_type | solution.py:271
  0.8 0.5 %collective-permute-start = (bf16[2,32,128]{2,1,0:T(8,128)(2,1)S(1)}, bf16[2,32,128]{2,1,0:T(8,128)(2,1)S(1)}, u32[]{:S(2)}, u32[]{:S(2)}) collective-permute-start(bf16[2,32,128]{2,1,0:T(8,128)(2,1)S(1)} %fusion), channel_id=1, source_target_pairs={{0,4},{4,0},{8,12},{12,8},{16,20},{20,16},{24,28},{28,24},{1,5},{5... | collective-permute-start | bytes 49160 | tf_op jit(solution)/shard_map/ppermute | solution.py:261
  2.0 0.2 collective-permute-done
  2.2 5.0 %collective-permute-start.3 = (bf16[2,2,32,128]{3,2,1,0:T(8,128)(2,1)S(1)}, bf16[2,2,32,128]{3,2,1,0:T(8,128)(2,1)S(1)}, u32[]{:S(2)}, u32[]{:S(2)}) collective-permute-start(bf16[2,2,32,128]{3,2,1,0:T(8,128)(2,1)S(1)} %pad_maximum_fusion.refs_2_), channel_id=1, source_target_pairs={{0,24},{4,28},{8,16},{12,20},{16,8},{20,12},{24,0},{28,4},{1,25},{... | collective-permute-start | bytes 98312 | tf_op jit(solution)/shard_map/ppermute | solution.py:261
  7.2 0.0 collective-permute-start.2
  7.2 0.6 %collective-permute-start.1 = (bf16[2,2,32,128]{3,2,1,0:T(8,128)(2,1)S(1)}, bf16[2,2,32,128]{3,2,1,0:T(8,128)(2,1)S(1)}, u32[]{:S(2)}, u32[]{:S(2)}) collective-permute-start(bf16[2,2,32,128]{3,2,1,0:T(8,128)(2,1)S(1)} %pad_maximum_fusion.refs_2_), channel_id=1, source_target_pairs={{0,8},{4,12},{8,0},{12,4},{16,24},{20,28},{24,16},{28,20},{1,9},{5... | collective-permute-start | bytes 98312 | tf_op jit(solution)/shard_map/ppermute | solution.py:261
  7.8 2.3 %shard_map.67 = (bf16[128,128,128]{2,1,0:T(8,128)(2,1)S(1)}, s32[4,256]{1,0:T(4,128)S(4)}) custom-call(bf16[128,128,128]{2,1,0:T(8,128)(2,1)} %tiles_hbm.1, s32[1,128]{1,0:T(1,128)} %bitcast.8, s32[1,128]{1,0:T(1,128)} %bitcast.9, s32[1,128]{1,0:T(1,128)S(1)} %broadcast_in_dim.46.count), custom_call_target="tpu_custom_call" | custom-call | bytes 4194304 | tf_op jit(solution)/shard_map/pallas_call | solution.py:154
  10.1 0.0 collective-permute-done.3.refs_5_
  10.1 1.9 %collective-permute-done.2.refs_4_ = bf16[2,2,32,128]{3,2,1,0:T(8,128)(2,1)S(1)} collective-permute-done((bf16[2,2,32,128]{3,2,1,0:T(8,128)(2,1)S(1)}, bf16[2,2,32,128]{3,2,1,0:T(8,128)(2,1)S(1)}, u32[]{:S(2)}, u32[]{:S(2)}) %collective-permute-start.2) | collective-permute-done | bytes 32800 | tf_op jit(solution)/shard_map/ppermute | solution.py:261
  12.0 0.0 collective-permute-done.1.refs_3_
  12.0 0.0 copy-start.1
  12.0 0.4 shard_map.68
  12.4 2.9 %collective-permute-start.6 = (bf16[32,16,128]{2,1,0:T(8,128)(2,1)S(1)}, bf16[32,16,128]{2,1,0:T(8,128)(2,1)S(1)}, u32[]{:S(2)}, u32[]{:S(2)}) collective-permute-start(bf16[32,16,128]{2,1,0:T(8,128)(2,1)S(1)} %get-tuple-element.26), channel_id=1, source_target_pairs={{0,3},{1,2},{2,1},{3,0},{4,7},{5,6},{6,5},{7,4},{8,11},{9,10},{10,... | collective-permute-start | bytes 393224 | tf_op jit(solution)/shard_map/ppermute | solution.py:264
  15.3 0.0 copy-start
  15.3 1.0 %shard_map.70 = (bf16[32,16,128]{2,1,0:T(8,128)(2,1)S(1)}, bf16[32,16,128]{2,1,0:T(8,128)(2,1)S(1)}) custom-call(bf16[128,128,128]{2,1,0:T(8,128)(2,1)S(1)} %get-tuple-element.20.refs_0_, s32[4,256]{1,0:T(4,128)S(4)} %get-tuple-element.21.refs_1_, f32[2,256,128]{2,1,0:T(8,128)S(1)} %get-tuple-element.23.refs_2_), custom_call_target="tpu_custom_call" | custom-call | flops 33554432 | bytes 2097152 | tf_op jit(solution)/shard_map/pallas_call | solution.py:176
  16.3 0.2 collective-permute-start.4
  16.5 0.5 %collective-permute-start.5 = (bf16[32,16,128]{2,1,0:T(8,128)(2,1)S(1)}, bf16[32,16,128]{2,1,0:T(8,128)(2,1)S(1)}, u32[]{:S(2)}, u32[]{:S(2)}) collective-permute-start(bf16[32,16,128]{2,1,0:T(8,128)(2,1)S(1)} %get-tuple-element.25), channel_id=1, source_target_pairs={{0,2},{1,3},{2,0},{3,1},{4,6},{5,7},{6,4},{7,5},{8,10},{9,11},{10,... | collective-permute-start | bytes 393224 | tf_op jit(solution)/shard_map/ppermute | solution.py:264
  17.0 0.0 copy-done.1
  17.0 0.6 %shard_map.69 = f32[32,16,128]{2,1,0:T(8,128)S(1)} custom-call(bf16[128,128,128]{2,1,0:T(8,128)(2,1)S(1)} %get-tuple-element.20.refs_0_, s32[4,256]{1,0:T(4,128)S(4)} %get-tuple-element.21.refs_1_, f32[2,256,128]{2,1,0:T(8,128)S(1)} %get-tuple-element.23.refs_2_), custom_call_target="tpu_custom_call" | custom-call | flops 16777216 | bytes 1048576 | tf_op jit(solution)/shard_map/pallas_call | solution.py:176
  17.6 1.9 %collective-permute-done.6 = bf16[32,16,128]{2,1,0:T(8,128)(2,1)S(1)} collective-permute-done((bf16[32,16,128]{2,1,0:T(8,128)(2,1)S(1)}, bf16[32,16,128]{2,1,0:T(8,128)(2,1)S(1)}, u32[]{:S(2)}, u32[]{:S(2)}) %collective-permute-start.6) | collective-permute-done | bytes 131104 | tf_op jit(solution)/shard_map/ppermute | solution.py:264
  19.5 1.8 %collective-permute-done.4 = bf16[32,16,128]{2,1,0:T(8,128)(2,1)S(1)} collective-permute-done((bf16[32,16,128]{2,1,0:T(8,128)(2,1)S(1)}, bf16[32,16,128]{2,1,0:T(8,128)(2,1)S(1)}, u32[]{:S(2)}, u32[]{:S(2)}) %collective-permute-start.4) | collective-permute-done | bytes 131104 | tf_op jit(solution)/shard_map/ppermute | solution.py:264
  21.3 0.2 collective-permute-done.5
  21.5 0.0 copy-done
  21.5 0.1 multiply_convert_fusion.refs_2_
  21.6 0.1 collective-permute-start.8
  21.7 2.4 %collective-permute-start.7 = (bf16[32,16,128]{2,1,0:T(8,128)(2,1)S(1)}, bf16[32,16,128]{2,1,0:T(8,128)(2,1)S(1)}, u32[]{:S(2)}, u32[]{:S(2)}) collective-permute-start(bf16[32,16,128]{2,1,0:T(8,128)(2,1)S(1)} %multiply_convert_fusion.refs_2_), channel_id=1, source_target_pairs={{0,16},{4,20},{16,24},{20,28},{24,8},{28,12},{8,0},{12,4},{1,17},{... | collective-permute-start | bytes 393224 | tf_op jit(solution)/shard_map/ppermute | solution.py:240
  24.1 0.0 collective-permute-done.8.refs_6_
  24.1 0.0 collective-permute-start.9
  24.1 3.9 %collective-permute-done.7.refs_3_ = bf16[32,16,128]{2,1,0:T(8,128)(2,1)S(1)} collective-permute-done((bf16[32,16,128]{2,1,0:T(8,128)(2,1)S(1)}, bf16[32,16,128]{2,1,0:T(8,128)(2,1)S(1)}, u32[]{:S(2)}, u32[]{:S(2)}) %collective-permute-start.7) | collective-permute-done | bytes 131104 | tf_op jit(solution)/shard_map/ppermute | solution.py:240
  28.0 3.4 %collective-permute-start.10 = (bf16[32,16,128]{2,1,0:T(8,128)(2,1)S(1)}, bf16[32,16,128]{2,1,0:T(8,128)(2,1)S(1)}, u32[]{:S(2)}, u32[]{:S(2)}) collective-permute-start(bf16[32,16,128]{2,1,0:T(8,128)(2,1)S(1)} %collective-permute-done.7.refs_3_), channel_id=1, source_target_pairs={{0,16},{4,20},{16,24},{20,28},{24,8},{28,12},{8,0},{12,4},{1,17},{... | collective-permute-start | bytes 393224 | tf_op jit(solution)/shard_map/ppermute | solution.py:244
  31.3 0.0 collective-permute-start.11
  31.3 0.0 collective-permute-done.9.refs_4_
  31.3 0.5 %collective-permute-start.12 = (bf16[32,16,128]{2,1,0:T(8,128)(2,1)S(1)}, bf16[32,16,128]{2,1,0:T(8,128)(2,1)S(1)}, u32[]{:S(2)}, u32[]{:S(2)}) collective-permute-start(bf16[32,16,128]{2,1,0:T(8,128)(2,1)S(1)} %collective-permute-done.9.refs_4_), channel_id=1, source_target_pairs={{0,4},{4,0},{8,12},{12,8},{16,20},{20,16},{24,28},{28,24},{1,5},{5... | collective-permute-start | bytes 393224 | tf_op jit(solution)/shard_map/ppermute | solution.py:261
  31.9 2.0 %collective-permute-done.10.refs_5_ = bf16[32,16,128]{2,1,0:T(8,128)(2,1)S(1)} collective-permute-done((bf16[32,16,128]{2,1,0:T(8,128)(2,1)S(1)}, bf16[32,16,128]{2,1,0:T(8,128)(2,1)S(1)}, u32[]{:S(2)}, u32[]{:S(2)}) %collective-permute-start.10) | collective-permute-done | bytes 131104 | tf_op jit(solution)/shard_map/ppermute | solution.py:244
  33.9 0.0 collective-permute-start.13
  33.9 0.0 collective-permute-done.11.refs_7_
  33.9 0.0 collective-permute-done.12.refs_8_
  33.9 1.3 %collective-permute-done.13.refs_9_ = bf16[32,16,128]{2,1,0:T(8,128)(2,1)S(1)} collective-permute-done((bf16[32,16,128]{2,1,0:T(8,128)(2,1)S(1)}, bf16[32,16,128]{2,1,0:T(8,128)(2,1)S(1)}, u32[]{:S(2)}, u32[]{:S(2)}) %collective-permute-start.13) | collective-permute-done | bytes 131104 | tf_op jit(solution)/shard_map/ppermute | solution.py:261
  35.2 0.5 %shard_map.71 = (bf16[32,16,128]{2,1,0:T(8,128)(2,1)S(1)}, bf16[256,16,128]{2,1,0:T(8,128)(2,1)S(1)}) custom-call(bf16[128,128,128]{2,1,0:T(8,128)(2,1)S(1)} %get-tuple-element.20.refs_0_, s32[4,256]{1,0:T(4,128)S(4)} %get-tuple-element.21.refs_1_, bf16[32,16,128]{2,1,0:T(8,128)(2,1)S(1)} %multiply_convert_fusion.refs_2_, ...), custom_call_target="tpu_custom_call" | custom-call | flops 16777216 | bytes 1048576 | tf_op jit(solution)/shard_map/pallas_call | solution.py:176
  35.7 2.4 %collective-permute-start.16 = (bf16[32,16,128]{2,1,0:T(8,128)(2,1)S(1)}, bf16[32,16,128]{2,1,0:T(8,128)(2,1)S(1)}, u32[]{:S(2)}, u32[]{:S(2)}) collective-permute-start(bf16[32,16,128]{2,1,0:T(8,128)(2,1)S(1)} %get-tuple-element.32), channel_id=1, source_target_pairs={{0,3},{1,2},{2,1},{3,0},{4,7},{5,6},{6,5},{7,4},{8,11},{9,10},{10,... | collective-permute-start | bytes 393224 | tf_op jit(solution)/shard_map/ppermute | solution.py:264
  38.1 1.0 %shard_map.73 = (bf16[32,16,128]{2,1,0:T(8,128)(2,1)S(1)}, bf16[32,16,128]{2,1,0:T(8,128)(2,1)S(1)}) custom-call(bf16[128,128,128]{2,1,0:T(8,128)(2,1)S(1)} %get-tuple-element.20.refs_0_, s32[4,256]{1,0:T(4,128)S(4)} %get-tuple-element.21.refs_1_, bf16[256,16,128]{2,1,0:T(8,128)(2,1)S(1)} %get-tuple-element.29.refs_2_), custom_call_target="tpu_custom_call" | custom-call | flops 33554432 | bytes 2097152 | tf_op jit(solution)/shard_map/pallas_call | solution.py:176
  39.0 0.1 collective-permute-start.14
  39.2 1.1 %collective-permute-start.15 = (bf16[32,16,128]{2,1,0:T(8,128)(2,1)S(1)}, bf16[32,16,128]{2,1,0:T(8,128)(2,1)S(1)}, u32[]{:S(2)}, u32[]{:S(2)}) collective-permute-start(bf16[32,16,128]{2,1,0:T(8,128)(2,1)S(1)} %get-tuple-element.31), channel_id=1, source_target_pairs={{0,2},{1,3},{2,0},{3,1},{4,6},{5,7},{6,4},{7,5},{8,10},{9,11},{10,... | collective-permute-start | bytes 393224 | tf_op jit(solution)/shard_map/ppermute | solution.py:264
  40.2 0.6 %shard_map.72.refs_0_ = f32[32,16,128]{2,1,0:T(8,128)S(1)} custom-call(bf16[128,128,128]{2,1,0:T(8,128)(2,1)S(1)} %get-tuple-element.20.refs_0_, s32[4,256]{1,0:T(4,128)S(4)} %get-tuple-element.21.refs_1_, bf16[256,16,128]{2,1,0:T(8,128)(2,1)S(1)} %get-tuple-element.29.refs_2_), custom_call_target="tpu_custom_call" | custom-call | flops 16777216 | bytes 1048576 | tf_op jit(solution)/shard_map/pallas_call | solution.py:176
  40.9 1.8 %collective-permute-done.16.refs_3_ = bf16[32,16,128]{2,1,0:T(8,128)(2,1)S(1)} collective-permute-done((bf16[32,16,128]{2,1,0:T(8,128)(2,1)S(1)}, bf16[32,16,128]{2,1,0:T(8,128)(2,1)S(1)}, u32[]{:S(2)}, u32[]{:S(2)}) %collective-permute-start.16) | collective-permute-done | bytes 131104 | tf_op jit(solution)/shard_map/ppermute | solution.py:264
  42.7 2.1 %collective-permute-done.14.refs_1_ = bf16[32,16,128]{2,1,0:T(8,128)(2,1)S(1)} collective-permute-done((bf16[32,16,128]{2,1,0:T(8,128)(2,1)S(1)}, bf16[32,16,128]{2,1,0:T(8,128)(2,1)S(1)}, u32[]{:S(2)}, u32[]{:S(2)}) %collective-permute-start.14) | collective-permute-done | bytes 131104 | tf_op jit(solution)/shard_map/ppermute | solution.py:264
  44.8 0.2 collective-permute-done.15.refs_2_
  45.0 0.8 %shard_map.74 = f32[32,16,128]{2,1,0:T(8,128)} custom-call(f32[32,16,128]{2,1,0:T(8,128)S(1)} %shard_map.72.refs_0_, bf16[32,16,128]{2,1,0:T(8,128)(2,1)S(1)} %collective-permute-done.14.refs_1_, bf16[32,16,128]{2,1,0:T(8,128)(2,1)S(1)} %collective-permute-done.15.refs_2_, bf16[32,16,128]{2,1,0:T(8,128)(2,1)S(1)} %collective-permute-done.16.refs_3_, ...), custom_call_target="tpu_custom_call" | custom-call | flops 524288 | bytes 786432 | tf_op jit(solution)/shard_map/pallas_call | solution.py:222
  (4 shorter events, 0.0 us)
Async XLA Ops:
  0.8 1.4 %collective-permute-start = (bf16[2,32,128]{2,1,0:T(8,128)(2,1)S(1)}, bf16[2,32,128]{2,1,0:T(8,128)(2,1)S(1)}, u32[]{:S(2)}, u32[]{:S(2)}) collective-permute-start(bf16[2,32,128]{2,1,0:T(8,128)(2,1)S(1)} %fusion), channel_id=1, source_target_pairs={{0,4},{4,0},{8,12},{12,8},{16,20},{20,16},{24,28},{28,24},{1,5},{5... | collective-permute-start | bytes 49160 | tf_op jit(solution)/shard_map/ppermute | solution.py:261
  2.2 7.9 %collective-permute-start.3 = (bf16[2,2,32,128]{3,2,1,0:T(8,128)(2,1)S(1)}, bf16[2,2,32,128]{3,2,1,0:T(8,128)(2,1)S(1)}, u32[]{:S(2)}, u32[]{:S(2)}) collective-permute-start(bf16[2,2,32,128]{3,2,1,0:T(8,128)(2,1)S(1)} %pad_maximum_fusion.refs_2_), channel_id=1, source_target_pairs={{0,24},{4,28},{8,16},{12,20},{16,8},{20,12},{24,0},{28,4},{1,25},{... | collective-permute-start | bytes 98312 | tf_op jit(solution)/shard_map/ppermute | solution.py:261
  7.2 4.8 %collective-permute-start.2 = (bf16[2,2,32,128]{3,2,1,0:T(8,128)(2,1)S(1)}, bf16[2,2,32,128]{3,2,1,0:T(8,128)(2,1)S(1)}, u32[]{:S(2)}, u32[]{:S(2)}) collective-permute-start(bf16[2,2,32,128]{3,2,1,0:T(8,128)(2,1)S(1)} %pad_maximum_fusion.refs_2_), channel_id=1, source_target_pairs={{0,16},{4,20},{8,24},{12,28},{16,0},{20,4},{24,8},{28,12},{1,17},{... | collective-permute-start | bytes 98312 | tf_op jit(solution)/shard_map/ppermute | solution.py:261
  7.2 4.8 %collective-permute-start.1 = (bf16[2,2,32,128]{3,2,1,0:T(8,128)(2,1)S(1)}, bf16[2,2,32,128]{3,2,1,0:T(8,128)(2,1)S(1)}, u32[]{:S(2)}, u32[]{:S(2)}) collective-permute-start(bf16[2,2,32,128]{3,2,1,0:T(8,128)(2,1)S(1)} %pad_maximum_fusion.refs_2_), channel_id=1, source_target_pairs={{0,8},{4,12},{8,0},{12,4},{16,24},{20,28},{24,16},{28,20},{1,9},{5... | collective-permute-start | bytes 98312 | tf_op jit(solution)/shard_map/ppermute | solution.py:261
  12.0 5.0 %copy-start.1 = (s32[32,128]{1,0:T(8,128)S(1)}, s32[32,128]{1,0:T(8,128)}, u32[]{:S(2)}) copy-start(s32[32,128]{1,0:T(8,128)} %param.10) | copy-start | bytes 49156
  12.4 7.1 %collective-permute-start.6 = (bf16[32,16,128]{2,1,0:T(8,128)(2,1)S(1)}, bf16[32,16,128]{2,1,0:T(8,128)(2,1)S(1)}, u32[]{:S(2)}, u32[]{:S(2)}) collective-permute-start(bf16[32,16,128]{2,1,0:T(8,128)(2,1)S(1)} %get-tuple-element.26), channel_id=1, source_target_pairs={{0,3},{1,2},{2,1},{3,0},{4,7},{5,6},{6,5},{7,4},{8,11},{9,10},{10,... | collective-permute-start | bytes 393224 | tf_op jit(solution)/shard_map/ppermute | solution.py:264
  15.3 6.2 %copy-start = (s32[32,128]{1,0:T(8,128)S(1)}, s32[32,128]{1,0:T(8,128)}, u32[]{:S(2)}) copy-start(s32[32,128]{1,0:T(8,128)} %refs_5_.1) | copy-start | bytes 49156
  16.3 5.0 %collective-permute-start.4 = (bf16[32,16,128]{2,1,0:T(8,128)(2,1)S(1)}, bf16[32,16,128]{2,1,0:T(8,128)(2,1)S(1)}, u32[]{:S(2)}, u32[]{:S(2)}) collective-permute-start(bf16[32,16,128]{2,1,0:T(8,128)(2,1)S(1)} %get-tuple-element.24), channel_id=1, source_target_pairs={{0,1},{1,0},{2,3},{3,2},{4,5},{5,4},{6,7},{7,6},{8,9},{9,8},{10,11... | collective-permute-start | bytes 393224 | tf_op jit(solution)/shard_map/ppermute | solution.py:264
  16.5 5.0 %collective-permute-start.5 = (bf16[32,16,128]{2,1,0:T(8,128)(2,1)S(1)}, bf16[32,16,128]{2,1,0:T(8,128)(2,1)S(1)}, u32[]{:S(2)}, u32[]{:S(2)}) collective-permute-start(bf16[32,16,128]{2,1,0:T(8,128)(2,1)S(1)} %get-tuple-element.25), channel_id=1, source_target_pairs={{0,2},{1,3},{2,0},{3,1},{4,6},{5,7},{6,4},{7,5},{8,10},{9,11},{10,... | collective-permute-start | bytes 393224 | tf_op jit(solution)/shard_map/ppermute | solution.py:264
  21.6 2.5 %collective-permute-start.8 = (bf16[32,16,128]{2,1,0:T(8,128)(2,1)S(1)}, bf16[32,16,128]{2,1,0:T(8,128)(2,1)S(1)}, u32[]{:S(2)}, u32[]{:S(2)}) collective-permute-start(bf16[32,16,128]{2,1,0:T(8,128)(2,1)S(1)} %multiply_convert_fusion.refs_2_), channel_id=1, source_target_pairs={{0,4},{4,0},{8,12},{12,8},{16,20},{20,16},{24,28},{28,24},{1,5},{5... | collective-permute-start | bytes 393224 | tf_op jit(solution)/shard_map/ppermute | solution.py:241
  21.7 6.2 %collective-permute-start.7 = (bf16[32,16,128]{2,1,0:T(8,128)(2,1)S(1)}, bf16[32,16,128]{2,1,0:T(8,128)(2,1)S(1)}, u32[]{:S(2)}, u32[]{:S(2)}) collective-permute-start(bf16[32,16,128]{2,1,0:T(8,128)(2,1)S(1)} %multiply_convert_fusion.refs_2_), channel_id=1, source_target_pairs={{0,16},{4,20},{16,24},{20,28},{24,8},{28,12},{8,0},{12,4},{1,17},{... | collective-permute-start | bytes 393224 | tf_op jit(solution)/shard_map/ppermute | solution.py:240
  24.1 7.2 %collective-permute-start.9 = (bf16[32,16,128]{2,1,0:T(8,128)(2,1)S(1)}, bf16[32,16,128]{2,1,0:T(8,128)(2,1)S(1)}, u32[]{:S(2)}, u32[]{:S(2)}) collective-permute-start(bf16[32,16,128]{2,1,0:T(8,128)(2,1)S(1)} %multiply_convert_fusion.refs_2_), channel_id=1, source_target_pairs={{16,0},{20,4},{24,16},{28,20},{8,24},{12,28},{0,8},{4,12},{17,1},{... | collective-permute-start | bytes 393224 | tf_op jit(solution)/shard_map/ppermute | solution.py:243
  28.0 5.9 %collective-permute-start.10 = (bf16[32,16,128]{2,1,0:T(8,128)(2,1)S(1)}, bf16[32,16,128]{2,1,0:T(8,128)(2,1)S(1)}, u32[]{:S(2)}, u32[]{:S(2)}) collective-permute-start(bf16[32,16,128]{2,1,0:T(8,128)(2,1)S(1)} %collective-permute-done.7.refs_3_), channel_id=1, source_target_pairs={{0,16},{4,20},{16,24},{20,28},{24,8},{28,12},{8,0},{12,4},{1,17},{... | collective-permute-start | bytes 393224 | tf_op jit(solution)/shard_map/ppermute | solution.py:244
  31.3 2.5 %collective-permute-start.11 = (bf16[32,16,128]{2,1,0:T(8,128)(2,1)S(1)}, bf16[32,16,128]{2,1,0:T(8,128)(2,1)S(1)}, u32[]{:S(2)}, u32[]{:S(2)}) collective-permute-start(bf16[32,16,128]{2,1,0:T(8,128)(2,1)S(1)} %collective-permute-done.7.refs_3_), channel_id=1, source_target_pairs={{0,4},{4,0},{8,12},{12,8},{16,20},{20,16},{24,28},{28,24},{1,5},{5... | collective-permute-start | bytes 393224 | tf_op jit(solution)/shard_map/ppermute | solution.py:261
  31.3 2.5 %collective-permute-start.12 = (bf16[32,16,128]{2,1,0:T(8,128)(2,1)S(1)}, bf16[32,16,128]{2,1,0:T(8,128)(2,1)S(1)}, u32[]{:S(2)}, u32[]{:S(2)}) collective-permute-start(bf16[32,16,128]{2,1,0:T(8,128)(2,1)S(1)} %collective-permute-done.9.refs_4_), channel_id=1, source_target_pairs={{0,4},{4,0},{8,12},{12,8},{16,20},{20,16},{24,28},{28,24},{1,5},{5... | collective-permute-start | bytes 393224 | tf_op jit(solution)/shard_map/ppermute | solution.py:261
  33.9 1.3 %collective-permute-start.13 = (bf16[32,16,128]{2,1,0:T(8,128)(2,1)S(1)}, bf16[32,16,128]{2,1,0:T(8,128)(2,1)S(1)}, u32[]{:S(2)}, u32[]{:S(2)}) collective-permute-start(bf16[32,16,128]{2,1,0:T(8,128)(2,1)S(1)} %collective-permute-done.10.refs_5_), channel_id=1, source_target_pairs={{0,4},{4,0},{8,12},{12,8},{16,20},{20,16},{24,28},{28,24},{1,5},{5... | collective-permute-start | bytes 393224 | tf_op jit(solution)/shard_map/ppermute | solution.py:261
  35.7 7.0 %collective-permute-start.16 = (bf16[32,16,128]{2,1,0:T(8,128)(2,1)S(1)}, bf16[32,16,128]{2,1,0:T(8,128)(2,1)S(1)}, u32[]{:S(2)}, u32[]{:S(2)}) collective-permute-start(bf16[32,16,128]{2,1,0:T(8,128)(2,1)S(1)} %get-tuple-element.32), channel_id=1, source_target_pairs={{0,3},{1,2},{2,1},{3,0},{4,7},{5,6},{6,5},{7,4},{8,11},{9,10},{10,... | collective-permute-start | bytes 393224 | tf_op jit(solution)/shard_map/ppermute | solution.py:264
  39.0 5.8 %collective-permute-start.14 = (bf16[32,16,128]{2,1,0:T(8,128)(2,1)S(1)}, bf16[32,16,128]{2,1,0:T(8,128)(2,1)S(1)}, u32[]{:S(2)}, u32[]{:S(2)}) collective-permute-start(bf16[32,16,128]{2,1,0:T(8,128)(2,1)S(1)} %get-tuple-element.30), channel_id=1, source_target_pairs={{0,1},{1,0},{2,3},{3,2},{4,5},{5,4},{6,7},{7,6},{8,9},{9,8},{10,11... | collective-permute-start | bytes 393224 | tf_op jit(solution)/shard_map/ppermute | solution.py:264
  39.2 5.8 %collective-permute-start.15 = (bf16[32,16,128]{2,1,0:T(8,128)(2,1)S(1)}, bf16[32,16,128]{2,1,0:T(8,128)(2,1)S(1)}, u32[]{:S(2)}, u32[]{:S(2)}) collective-permute-start(bf16[32,16,128]{2,1,0:T(8,128)(2,1)S(1)} %get-tuple-element.31), channel_id=1, source_target_pairs={{0,2},{1,3},{2,0},{3,1},{4,6},{5,7},{6,4},{7,5},{8,10},{9,11},{10,... | collective-permute-start | bytes 393224 | tf_op jit(solution)/shard_map/ppermute | solution.py:264
